TPU v7x, 32 devices: a whole 2x2x4 slice. The times are simulated.
32 devices in a mesh: ctx: 8 (over z, core), fsdp: 4 (over y, x).
Axes of the slice: x: 2, y: 2, z: 4, core: 2. Of those that a mesh axis runs over, the one named last changes fastest.
Arguments:
- tokens: float32 [4, 2048, 640], P('fsdp', 'ctx'), may hold values from -6 to 6
- cotangent: float32 [4, 2048, 640], P('fsdp', 'ctx'), may hold values from -6 to 6
- positions: int32 [4, 2048], P('fsdp', 'ctx'), may hold values from 0 to 1023, as said below
- block_order: int32 [16], replicated, may hold values from 0 to 15, as said below
- query_weight: bfloat16 [640, 1024], P('fsdp'), may hold values from -0.25 to 0.25
- key_weight: bfloat16 [640, 256], P('fsdp'), may hold values from -0.25 to 0.25
- value_weight: bfloat16 [640, 256], P('fsdp'), may hold values from -0.25 to 0.25
- output_weight: bfloat16 [1024, 640], P('fsdp'), may hold values from -0.1875 to 0.1875
- gate_weight: bfloat16 [640, 2048], P(None, 'fsdp'), may hold values from -0.25 to 0.25
- up_weight: bfloat16 [640, 2048], P(None, 'fsdp'), may hold values from -0.25 to 0.25
- down_weight: bfloat16 [2048, 640], P('fsdp'), may hold values from -0.125 to 0.125
- input_gain: bfloat16 [640], P('fsdp'), may hold values from -0.5 to 0.5
- query_gain: bfloat16 [256], P('fsdp'), may hold values from -0.5 to 0.5
- key_gain: bfloat16 [256], P('fsdp'), may hold values from -0.5 to 0.5
- mixer_gain: bfloat16 [640], P('fsdp'), may hold values from -0.5 to 0.5
- prefeed_gain: bfloat16 [640], P('fsdp'), may hold values from -0.5 to 0.5
- postfeed_gain: bfloat16 [640], P('fsdp'), may hold values from -0.5 to 0.5
Outputs:
- output: float32 [4, 2048, 640], P('fsdp', 'ctx')
- tokens_grad: float32 [4, 2048, 640], P('fsdp', 'ctx')
- query_grad: float32 [640, 1024], P('fsdp')
- key_grad: float32 [640, 256], P('fsdp')
- value_grad: float32 [640, 256], P('fsdp')
- outproj_grad: float32 [1024, 640], P('fsdp')
- gate_grad: float32 [640, 2048], P(None, 'fsdp')
- up_grad: float32 [640, 2048], P(None, 'fsdp')
- down_grad: float32 [2048, 640], P('fsdp')
- ingain_grad: float32 [640], P('fsdp')
- qgain_grad: float32 [256], P('fsdp')
- kgain_grad: float32 [256], P('fsdp')
- mixgain_grad: float32 [640], P('fsdp')
- pregain_grad: float32 [640], P('fsdp')
- postgain_grad: float32 [640], P('fsdp')
Inputs may be any that keep to these rules, and one draw needn't show every extreme that they name: `block_order`: a permutation of 0 to 15 in which entries 2c and 2c + 1 sum to 15 for every c. `positions`: each token's index within its document: 0 at a document's first token, else one more than that of the token before it in sequence order; each sequence holds at most 4 documents, the first of them exactly 1024 tokens long.
All inputs are finite; a program needn't handle non-finite values.
Results may differ from a plain program's by a relative error of at most 0.015.
Values may be sent and summed in bfloat16 or wider, within the bound.
No kernel may reach another device: no remote copies, remote signals or barrier semaphores. Data moves between devices by JAX's collectives and lax.ppermute only.
A program may use at most 128 MiB of HBM per device.

v0:
```python
import jax
import jax.numpy as jnp
from jax import lax
from jax.experimental import pallas as pl
from jax.experimental.pallas import tpu as pltpu
from jax.sharding import PartitionSpec as P


norm_eps = 1e-06
rope_base = 1000000.0
tanh_coef = 0.7978845608028654
cubic_coef = 0.044715
bf16 = jnp.bfloat16
f32 = jnp.float32


def norm_factor(inputs):
    return lax.rsqrt(jnp.mean(inputs * inputs, axis=-1, keepdims=True) + norm_eps)


def norm_apply(inputs, gain):
    return inputs * norm_factor(inputs) * (1.0 + gain)


def norm_back(inputs, gain, upstream):
    factor = norm_factor(inputs)
    normal = inputs * factor
    weighted = upstream * (1.0 + gain)
    grad_inputs = factor * (weighted - normal * jnp.mean(normal * weighted, axis=-1, keepdims=True))
    grad_gain = jnp.sum((upstream * normal).reshape(-1, inputs.shape[-1]), axis=0)
    return (grad_inputs, grad_gain)


def rope_tables(places, width):
    half_width = width // 2
    frequency = rope_base ** (-2.0 * jnp.arange(half_width, dtype=f32) / width)
    angles = places.astype(f32)[:, None] * frequency[None, :]
    return (jnp.cos(angles), jnp.sin(angles))


def rope_apply(inputs, cosines, sine_terms):
    half_width = inputs.shape[-1] // 2
    first_half = inputs[..., :half_width]
    second_half = inputs[..., half_width:]
    return jnp.concatenate(
        [
            first_half * cosines - second_half * sine_terms,
            second_half * cosines + first_half * sine_terms,
        ],
        axis=-1,
    )


def rope_back(upstream, cosines, sine_terms):
    half_width = upstream.shape[-1] // 2
    first_half = upstream[..., :half_width]
    second_half = upstream[..., half_width:]
    return jnp.concatenate(
        [
            first_half * cosines + second_half * sine_terms,
            second_half * cosines - first_half * sine_terms,
        ],
        axis=-1,
    )


def gelu_parts(inputs):
    tanh_part = jnp.tanh(tanh_coef * (inputs + cubic_coef * inputs * inputs * inputs))
    activated = 0.5 * inputs * (1.0 + tanh_part)
    gelu_slope = 0.5 * (1.0 + tanh_part) + 0.5 * inputs * (
        1.0 - tanh_part * tanh_part
    ) * tanh_coef * (1.0 + 3.0 * cubic_coef * inputs * inputs)
    return (activated, gelu_slope)


def dot(a, b, dims):
    return lax.dot_general(a, b, (dims, ((), ())), preferred_element_type=f32)


def put_rows(ref, order, low, high):
    rows = low.shape[0]
    at = pl.multiple_of(order * rows, rows)
    other = pl.multiple_of((1 - order) * rows, rows)
    ref[pl.ds(at, rows), :] = low
    ref[pl.ds(other, rows), :] = high


def get_rows(ref, order):
    rows = ref.shape[0] // 2
    at = pl.multiple_of(order * rows, rows)
    other = pl.multiple_of((1 - order) * rows, rows)
    return jnp.concatenate([ref[pl.ds(at, rows), :], ref[pl.ds(other, rows), :]], axis=0)


def rope_norm(raw, gain, cosines, sine_terms):
    return rope_apply(norm_apply(raw, gain), cosines, sine_terms)


def pre_kernel(ins, outs, scratch):
    place_ref, tok_ref, gains_ref, qk_gain_ref, cos_ref, sin_ref, qw_ref, kw_ref, vw_ref, mine, theirs = ins
    normed_ref, q_ref, kv_ref, qraw_ref, kraw_ref, full_ref = outs
    order, fsdp_place, parity = place_ref[0], place_ref[1], place_ref[2]
    count = len(mine)
    size = count + 1
    shard, half = mine[0].shape
    query_width, head_dim = qw_ref.shape[1], kw_ref.shape[1]
    gain_in, gain_q, gain_k = gains_ref[0:1, :], qk_gain_ref[0:1, :], qk_gain_ref[1:2, :]
    at = pl.multiple_of(fsdp_place * shard, 16)
    full_ref[pl.ds(at, shard), :query_width] = qw_ref[...]
    full_ref[pl.ds(at, shard), query_width : query_width + head_dim] = kw_ref[...]
    full_ref[pl.ds(at, shard), query_width + head_dim :] = vw_ref[...]
    left = pl.multiple_of(parity * half, 128)
    right = pl.multiple_of((1 - parity) * half, 128)
    for k in range(count):
        at = pl.multiple_of(lax.rem(fsdp_place + k + 1, size) * shard, 16)
        full_ref[pl.ds(at, shard), pl.ds(left, half)] = mine[k][...]
        full_ref[pl.ds(at, shard), pl.ds(right, half)] = theirs[k][...]
    residual = get_rows(tok_ref, order)
    normed = norm_apply(residual, gain_in).astype(bf16)
    normed_ref[...] = normed
    cosines, sine_terms = cos_ref[...], sin_ref[...]
    for at in range(0, query_width, head_dim):
        raw = dot(normed, full_ref[:, at : at + head_dim], ((1,), (0,)))
        qraw_ref[:, at : at + head_dim] = raw
        q_ref[:, at : at + head_dim] = rope_norm(
            raw, gain_q, cosines, sine_terms
        ).astype(bf16)
    raw = dot(normed, full_ref[:, query_width : query_width + head_dim], ((1,), (0,)))
    kraw_ref[...] = raw
    kv_ref[:, :head_dim] = rope_norm(raw, gain_k, cosines, sine_terms).astype(bf16)
    kv_ref[:, head_dim:] = dot(
        normed, full_ref[:, query_width + head_dim :], ((1,), (0,))
    ).astype(bf16)


def mask_bias(ids, last, first):
    return jnp.where((ids <= last) & (ids >= first), 0.0, -1e30)


def attend_kernel(ins, outs, scratch):
    (place_ref, tok_ref, q_ref, mine, theirs, last_ref, first_ref, ids_ref,
     outw_ref, outp, outt, gains_ref) = ins
    att_ref, lse_ref, kv_ref, outfull_ref, projected_ref, hidden_ref, feed_ref = outs
    order, fsdp_place, parity = place_ref[0], place_ref[1], place_ref[2]
    chips = len(mine)
    rows = mine[0].shape[0] // 2
    head_dim = mine[0].shape[1] // 2
    heads = q_ref.shape[1] // head_dim
    scale = head_dim ** (-0.5)
    size = len(outp) + 1
    shard = outw_ref.shape[0]
    half = shard // 2
    at = pl.multiple_of(fsdp_place * shard, 16)
    outfull_ref[pl.ds(at, shard), :] = outw_ref[...]
    for k in range(1, size):
        at = lax.rem(fsdp_place + k, size) * shard
        left = pl.multiple_of(at + parity * half, 16)
        right = pl.multiple_of(at + (1 - parity) * half, 16)
        outfull_ref[pl.ds(left, half), :] = outp[k - 1][...]
        outfull_ref[pl.ds(right, half), :] = outt[k - 1][...]
    for part in range(2):
        own = slice(part * rows, (part + 1) * rows)
        for k in range(chips):
            kv_ref[part, k * rows : (k + 1) * rows, :] = mine[k][own, :]
            kv_ref[part, (chips + k) * rows : (chips + k + 1) * rows, :] = theirs[k][own, :]
        queries = jnp.concatenate(
            [q_ref[own, h * head_dim : (h + 1) * head_dim] for h in range(heads)], axis=0
        )
        scores = dot(queries, kv_ref[part, :, :head_dim], ((1,), (1,))) * scale
        bias = mask_bias(ids_ref[part], last_ref[own, :], first_ref[own, :])
        pieces = []
        for h in range(heads):
            one = scores[h * rows : (h + 1) * rows] + bias
            top = jnp.max(one, axis=1, keepdims=True)
            weights = jnp.exp(one - top)
            lse = top + jnp.log(jnp.sum(weights, axis=1, keepdims=True))
            lse_ref[part, h * rows : (h + 1) * rows, :] = lse
            pieces.append((weights * jnp.exp(top - lse)).astype(bf16))
        probs = jnp.concatenate(pieces, axis=0)
        attended = dot(probs, kv_ref[part, :, head_dim:], ((1,), (0,))).astype(bf16)
        for h in range(heads):
            att_ref[own, h * head_dim : (h + 1) * head_dim] = attended[h * rows : (h + 1) * rows]
    projected = dot(att_ref[...], outfull_ref[...], ((1,), (0,)))
    projected_ref[...] = projected
    hidden = get_rows(tok_ref, order) + norm_apply(projected, gains_ref[1:2, :])
    hidden_ref[...] = hidden
    feed_ref[...] = norm_apply(hidden, gains_ref[2:3, :]).astype(bf16)


def norm_back_rows(inputs, gain, upstream):
    grad, grad_gain = norm_back(inputs, gain, upstream)
    return grad, grad_gain[None, :]


def feed_kernel(ins, outs, scratch):
    (place_ref, cot_ref, feed_ref, hidden_ref, projected_ref, outfull_ref, gains_ref,
     gate_ref, up_ref, down_ref, pair_refs, down_refs) = ins
    out_ref, gfeed_ref, ghidden_ref, gproj_ref, gatt_ref, mix_ref, pre_ref, post_ref = outs
    act_ref, slope_ref = scratch
    order = place_ref[0]
    rows = feed_ref.shape[0] // 2
    half = pair_refs[0].shape[1] // 2
    pieces = [(lambda: gate_ref[...], lambda: up_ref[...], lambda: down_ref[...], gate_ref.shape[1])]
    for pr, dr in zip(pair_refs, down_refs):
        pieces.append(
            (
                lambda pr=pr: pr[:, :half],
                lambda pr=pr: pr[:, half:],
                lambda dr=dr: dr[...],
                half,
            )
        )
    feed_in = feed_ref[...]
    total = jnp.zeros(hidden_ref.shape, f32)
    at = 0
    for gate, up, down, units in pieces:
        gate_vals = dot(feed_in, gate(), ((1,), (0,)))
        up_vals = dot(feed_in, up(), ((1,), (0,)))
        activated, slope = gelu_parts(gate_vals)
        act_ref[:, at : at + units] = activated
        slope_ref[:, at : at + units] = up_vals * slope
        total = total + dot((activated * up_vals).astype(bf16), down(), ((1,), (0,)))
        at += units
    hidden = hidden_ref[...]
    output = hidden + norm_apply(total, gains_ref[3:4, :])
    put_rows(out_ref, order, output[:rows], output[rows:])
    upstream = get_rows(cot_ref, order)
    grad_feed, post_ref[...] = norm_back_rows(total, gains_ref[3:4, :], upstream)
    grad_feed = grad_feed.astype(bf16)
    gfeed_ref[...] = grad_feed
    back = jnp.zeros(hidden_ref.shape, f32)
    at = 0
    for gate, up, down, units in pieces:
        grad_mixed = dot(grad_feed, down(), ((1,), (1,)))
        grad_gate = (grad_mixed * slope_ref[:, at : at + units]).astype(bf16)
        grad_up = (grad_mixed * act_ref[:, at : at + units]).astype(bf16)
        back = back + dot(grad_gate, gate(), ((1,), (1,))) + dot(grad_up, up(), ((1,), (1,)))
        at += units
    part, pre_ref[...] = norm_back_rows(hidden, gains_ref[2:3, :], back)
    grad_hidden = upstream + part
    ghidden_ref[...] = grad_hidden
    grad_proj, mix_ref[...] = norm_back_rows(projected_ref[...], gains_ref[1:2, :], grad_hidden)
    grad_proj = grad_proj.astype(bf16)
    gproj_ref[...] = grad_proj
    gatt_ref[...] = dot(grad_proj, outfull_ref[...], ((1,), (1,))).astype(bf16)


def attend_back_kernel(ins, outs, scratch):
    (q_ref, kv_ref, gatt_ref, att_ref, lse_ref, last_ref, first_ref, ids_ref,
     qraw_ref, qk_gain_ref, cos_ref, sin_ref) = ins
    gq_ref, mine_ref, theirs_ref, qgain_ref = outs
    chips, rows, head_dim = mine_ref.shape[0], mine_ref.shape[1] // 2, mine_ref.shape[2] // 2
    heads = q_ref.shape[1] // head_dim
    scale = head_dim ** (-0.5)
    gain_total = jnp.zeros(qgain_ref.shape, f32)
    for part in range(2):
        own = slice(part * rows, (part + 1) * rows)

        def stacked(ref):
            return jnp.concatenate(
                [ref[own, h * head_dim : (h + 1) * head_dim] for h in range(heads)], axis=0
            )

        queries, upstream, attended = stacked(q_ref), stacked(gatt_ref), stacked(att_ref)
        keys, values = kv_ref[part, :, :head_dim], kv_ref[part, :, head_dim:]
        delta = jnp.sum(upstream.astype(f32) * attended.astype(f32), axis=1, keepdims=True)
        scores = dot(queries, keys, ((1,), (1,))) * scale
        grad_probs = dot(upstream, values, ((1,), (1,)))
        bias = mask_bias(ids_ref[part], last_ref[own, :], first_ref[own, :])
        prob_list, score_list = [], []
        for h in range(heads):
            one = slice(h * rows, (h + 1) * rows)
            probs = jnp.exp(scores[one] + bias - lse_ref[part, one, :])
            prob_list.append(probs.astype(bf16))
            score_list.append((probs * (grad_probs[one] - delta[one]) * scale).astype(bf16))
        probs = jnp.concatenate(prob_list, axis=0)
        grad_scores = jnp.concatenate(score_list, axis=0)
        grad_keys = dot(grad_scores, queries, ((0,), (0,)))
        grad_values = dot(probs, upstream, ((0,), (0,)))
        for k in range(chips):
            for ref, base, kind in ((mine_ref, 0, f32), (theirs_ref, chips, bf16)):
                piece = slice((base + k) * rows, (base + k + 1) * rows)
                ref[k, own, :head_dim] = grad_keys[piece].astype(kind)
                ref[k, own, head_dim:] = grad_values[piece].astype(kind)
        grad_queries = dot(grad_scores, keys, ((1,), (0,)))
        cosines, sine_terms = cos_ref[own, :], sin_ref[own, :]
        for h in range(heads):
            cols = slice(h * head_dim, (h + 1) * head_dim)
            rotated = rope_back(grad_queries[h * rows : (h + 1) * rows], cosines, sine_terms)
            grad_raw, grad_gain = norm_back_rows(
                qraw_ref[own, cols], qk_gain_ref[0:1, :], rotated
            )
            gq_ref[own, cols] = grad_raw.astype(bf16)
            gain_total = gain_total + grad_gain
    qgain_ref[...] = gain_total


def weight_kernel(ins, outs, scratch):
    place_ref, feed_refs, grad_refs, gate_ref, up_ref, down_ref, att_ref, gproj_ref = ins
    mine_ref, theirs_ref = outs
    (grad_ref,) = scratch
    parity = place_ref[2]
    count = len(feed_refs) - 1
    units = down_ref.shape[0]
    half = units // 2
    feed_in = jnp.concatenate([ref[...] for ref in feed_refs], axis=0)
    grad_feed = jnp.concatenate([ref[...] for ref in grad_refs], axis=0)
    gate_vals = dot(feed_in, gate_ref[...], ((1,), (0,)))
    up_vals = dot(feed_in, up_ref[...], ((1,), (0,)))
    activated, slope = gelu_parts(gate_vals)
    mixed = (activated * up_vals).astype(bf16)
    grad_mixed = dot(grad_feed, down_ref[...], ((1,), (1,)))
    grad_gate = (grad_mixed * up_vals * slope).astype(bf16)
    grad_up = (grad_mixed * activated).astype(bf16)
    grad_ref[0:units, :] = dot(grad_gate, feed_in, ((0,), (0,)))
    grad_ref[units : 2 * units, :] = dot(grad_up, feed_in, ((0,), (0,)))
    grad_ref[2 * units : 3 * units, :] = dot(mixed, grad_feed, ((0,), (0,)))
    grad_ref[3 * units :, :] = dot(att_ref[...], gproj_ref[...], ((0,), (0,)))
    shard = att_ref.shape[1] // (count + 1)
    groups = [(k * units, k * half, half) for k in range(3)]
    groups += [
        (3 * units + k * shard, 3 * half + k * (shard // 2), shard // 2) for k in range(count + 1)
    ]
    for start, to, size in groups:
        mine = pl.multiple_of(start + parity * size, 16)
        theirs = pl.multiple_of(start + (1 - parity) * size, 16)
        mine_ref[to : to + size, :] = grad_ref[pl.ds(mine, size), :]
        theirs_ref[to : to + size, :] = grad_ref[pl.ds(theirs, size), :].astype(bf16)


def put_gains(ref, at, value):
    top = value.astype(bf16)
    count = value.shape[0]
    ref[at : at + count, :] = top
    ref[at + count : at + 2 * count, :] = (value - top.astype(f32)).astype(bf16)


def post_kernel(ins, outs, scratch):
    (place_ref, tok_ref, own_ref, parts, kraw_ref, gains_ref, qk_gain_ref, cos_ref, sin_ref,
     normed_ref, gq_ref, full_ref, ghidden_ref, qgain_ref, mix_ref, pre_ref, post_ref) = ins
    tgrad_ref, mine_ref, theirs_ref, terms_ref = outs
    back_ref, grad_ref, sums_ref = scratch
    order, parity = place_ref[0], place_ref[2]
    head_dim = kraw_ref.shape[1]
    query_width = gq_ref.shape[1]
    rows = normed_ref.shape[0] // 2
    half = mine_ref.shape[1]
    total = own_ref[...]
    for k in range(len(parts)):
        total = total + parts[k][...].astype(f32)
    rotated = rope_back(total[:, :head_dim], cos_ref[...], sin_ref[...])
    grad_key, key_gain = norm_back_rows(
        kraw_ref[...], qk_gain_ref[1:2, :], rotated
    )
    back_ref[:, :query_width] = gq_ref[...]
    back_ref[:, query_width : query_width + head_dim] = grad_key.astype(bf16)
    back_ref[:, query_width + head_dim :] = total[:, head_dim:].astype(bf16)
    grad_ref[...] = dot(normed_ref[...], back_ref[...], ((0,), (0,)))
    left = pl.multiple_of(parity * half, 128)
    right = pl.multiple_of((1 - parity) * half, 128)
    mine_ref[...] = grad_ref[:, pl.ds(left, half)]
    theirs_ref[...] = grad_ref[:, pl.ds(right, half)].astype(bf16)
    grad_normed = dot(back_ref[...], full_ref[...], ((1,), (1,)))
    part, in_gain = norm_back_rows(
        get_rows(tok_ref, order), gains_ref[0:1, :], grad_normed
    )
    grads = ghidden_ref[...] + part
    put_rows(tgrad_ref, order, grads[:rows], grads[rows:])
    sums_ref[...] = jnp.zeros(sums_ref.shape, f32)
    for row, value in enumerate(
        (in_gain, mix_ref[...], pre_ref[...], post_ref[...], qgain_ref[...], key_gain)
    ):
        sums_ref[row : row + 1, : value.shape[1]] = value
    put_gains(terms_ref, 0, sums_ref[...])


def late_pack_kernel(ins, outs, scratch):
    place_ref, mine_ref, other_ref, terms_ref = ins
    fsdp_place = place_ref[1]
    size = len(outs)
    shard = mine_ref.shape[0] // size
    for k in range(size):
        at = pl.multiple_of(lax.rem(fsdp_place + size - k, size) * shard, 16)
        chunk = mine_ref[pl.ds(at, shard), :] + other_ref[pl.ds(at, shard), :].astype(f32)
        outs[k][:shard, :] = chunk.astype(bf16)
        outs[k][shard:, :] = terms_ref[...]


def late_sum_kernel(ins, outs, scratch):
    (out_ref,) = outs
    total = ins[0][...].astype(f32)
    for ref in ins[1:]:
        total = total + ref[...].astype(f32)
    rows = total.shape[0] - 16
    out_ref[:rows, :] = total[:rows].astype(bf16)
    put_gains(out_ref, rows, total[rows : rows + 8] + total[rows + 8 :])


def late_last_kernel(ins, outs, scratch):
    place_ref, mine_ref, other_ref = ins
    q_ref, k_ref, v_ref, gains_ref = outs
    (full_ref,) = scratch
    parity = place_ref[2]
    rows, half = q_ref.shape[0], mine_ref.shape[1]
    left = pl.multiple_of(parity * half, 128)
    right = pl.multiple_of((1 - parity) * half, 128)
    full_ref[:, pl.ds(left, half)] = mine_ref[:rows, :].astype(f32)
    full_ref[:, pl.ds(right, half)] = other_ref[:rows, :].astype(f32)
    width, head_dim = q_ref.shape[1], k_ref.shape[1]
    q_ref[...] = full_ref[:, :width]
    k_ref[...] = full_ref[:, width : width + head_dim]
    v_ref[...] = full_ref[:, width + head_dim :]
    both = mine_ref[rows:, :].astype(f32) + other_ref[rows:, :].astype(f32)
    gains_ref[...] = both[:8] + both[8:]


def early_pack_kernel(ins, outs, scratch):
    place_ref, mine_ref, other_ref = ins
    feed_ref, chunks = outs
    fsdp_place = place_ref[1]
    size = len(chunks)
    base, shard = feed_ref.shape[0], chunks[0].shape[0]
    feed_ref[...] = (mine_ref[:base, :] + other_ref[:base, :].astype(f32)).astype(bf16)
    for k in range(size):
        at = pl.multiple_of(base + lax.rem(fsdp_place + size - k, size) * shard, 16)
        chunk = mine_ref[pl.ds(at, shard), :] + other_ref[pl.ds(at, shard), :].astype(f32)
        chunks[k][...] = chunk.astype(bf16)


def early_last_kernel(ins, outs, scratch):
    place_ref, mine_ref, other_ref = ins
    gate_ref, up_ref, down_ref, out_ref = outs
    parity = place_ref[2]
    half = down_ref.shape[0] // 2
    out_half = out_ref.shape[0] // 2
    for ref, side in ((mine_ref, parity), (other_ref, 1 - parity)):
        cols = pl.multiple_of(side * half, 128)
        gate_ref[:, pl.ds(cols, half)] = ref[:half, :].astype(f32).T
        up_ref[:, pl.ds(cols, half)] = ref[half : 2 * half, :].astype(f32).T
        at = pl.multiple_of(side * half, 16)
        down_ref[pl.ds(at, half), :] = ref[2 * half : 3 * half, :].astype(f32)
        at = pl.multiple_of(side * out_half, 16)
        out_ref[pl.ds(at, out_half), :] = ref[3 * half :, :].astype(f32)


def run_kernel(kernel, args, outs, scratch=()):
    vmem = pl.BlockSpec(memory_space=pltpu.VMEM)
    smem = pl.BlockSpec(memory_space=pltpu.SMEM)
    flat, in_tree = jax.tree.flatten(args)
    shapes = jax.tree.map(
        lambda o: jax.ShapeDtypeStruct(*o), outs, is_leaf=lambda o: not isinstance(o[0][0], tuple)
    )
    flat_out, out_tree = jax.tree.flatten(shapes)

    def wrapped(*refs):
        ins = jax.tree.unflatten(in_tree, refs[: len(flat)])
        targets = jax.tree.unflatten(out_tree, refs[len(flat) : len(flat) + len(flat_out)])
        kernel(ins, targets, refs[len(flat) + len(flat_out) :])

    call = pl.pallas_call(
        wrapped,
        in_specs=[smem if a.ndim == 1 else vmem for a in flat],
        out_specs=[vmem for _ in flat_out],
        out_shape=flat_out,
        scratch_shapes=[pltpu.VMEM(s, d) for s, d in scratch],
        compiler_params=pltpu.CompilerParams(vmem_limit_bytes=56 * 2**20),
    )
    return jax.tree.unflatten(out_tree, call(*flat))


def make_body(fsdp_size, ctx_size):
    chips = ctx_size // 2

    def from_peer(x, axis, offset):
        size = fsdp_size if axis == "fsdp" else ctx_size
        return lax.ppermute(x, axis, [((i + offset) % size, i) for i in range(size)])

    def with_partner(x, bit=1):
        return lax.ppermute(x, "ctx", [(i, i ^ bit) for i in range(ctx_size)])

    def others_fsdp(x):
        return [from_peer(x, "fsdp", k) for k in range(1, fsdp_size)]

    def with_partners(parts):
        return [with_partner(p) for p in parts]

    def after(x, *others):
        return lax.optimization_barrier((x,) + others)[0]

    def pick(x, at, axis=0):
        return lax.dynamic_index_in_dim(x, at, axis, keepdims=False)

    def sum_chips(half, ctx_place):
        _, width = half.shape
        steps = []
        bit = 2
        while bit < ctx_size:
            side = (ctx_place // bit) % 2
            half = half.reshape(2, -1, width)
            sent = with_partner(pick(half, 1 - side), bit)
            half = (pick(half, side).astype(f32) + sent.astype(f32)).astype(bf16)
            steps.append((bit, side))
            bit *= 2
        for bit, side in reversed(steps):
            other = with_partner(half, bit)
            first = jnp.where(side == 0, half, other)
            second = jnp.where(side == 0, other, half)
            half = jnp.concatenate([first, second], axis=0)
        return half

    def body(
        tokens,
        cotangent,
        positions,
        block_order,
        query_weight,
        key_weight,
        value_weight,
        output_weight,
        gate_weight,
        up_weight,
        down_weight,
        input_gain,
        query_gain,
        key_gain,
        mixer_gain,
        prefeed_gain,
        postfeed_gain,
    ):
        row_count = tokens.shape[1]
        width = tokens.shape[2]
        block_rows = row_count // 2
        head_dim = key_weight.shape[1]
        query_width = query_weight.shape[1]
        head_count = query_width // head_dim
        proj_width = query_width + 2 * head_dim
        proj_half = proj_width // 2
        shard_rows = query_weight.shape[0]
        out_rows = output_weight.shape[0]
        hidden_rows = down_weight.shape[0]
        half_rows = hidden_rows // 2
        ctx_place = lax.axis_index("ctx")
        fsdp_place = lax.axis_index("fsdp")
        parity = ctx_place % 2

        proj_send = jnp.where(
            parity == 0,
            query_weight[:, :proj_half],
            jnp.concatenate([query_weight[:, proj_half:], key_weight, value_weight], axis=1),
        )
        proj_mine = others_fsdp(proj_send)

        wide = (input_gain, mixer_gain, prefeed_gain, postfeed_gain)
        narrow = (query_gain, key_gain)
        gain_cols, head_cols = input_gain.shape[0], query_gain.shape[0]
        gains_own = jnp.stack(
            [g.astype(f32) for g in wide]
            + [jnp.pad(g.astype(f32), (0, gain_cols - head_cols)) for g in narrow]
        )
        gain_parts = [gains_own] + others_fsdp(gains_own)
        gain_full = jnp.zeros((fsdp_size,) + gains_own.shape, f32)
        for k, part in enumerate(gain_parts):
            gain_full = lax.dynamic_update_index_in_dim(
                gain_full, part, (fsdp_place + k) % fsdp_size, 0
            )
        gain_full = gain_full.transpose(1, 0, 2)
        gains = gain_full[:4].reshape(4, width)
        qk_gains = gain_full[4:, :, :head_cols].reshape(2, head_dim)

        own_blocks = lax.dynamic_slice_in_dim(block_order, 2 * ctx_place, 2)
        flipped = (own_blocks[0] > own_blocks[1]).astype(jnp.int32)
        place = jnp.stack([flipped, fsdp_place, parity]).astype(jnp.int32)
        places = jnp.where(flipped == 0, positions[0], jnp.roll(positions[0], block_rows))
        offsets = jnp.arange(block_rows, dtype=jnp.int32)
        low_blocks = jnp.minimum(block_order[0::2], block_order[1::2])
        high_blocks = jnp.maximum(block_order[0::2], block_order[1::2])
        sorted_blocks = jnp.stack([low_blocks, high_blocks])
        query_blocks = lax.dynamic_slice_in_dim(sorted_blocks, ctx_place, 1, axis=1)
        query_index = (query_blocks * block_rows + offsets[None, :]).reshape(-1)
        query_last = query_index[:, None]
        query_first = (query_index - places)[:, None]
        sources = jnp.concatenate(
            [
                (ctx_place + 2 * jnp.arange(chips)) % ctx_size,
                ((ctx_place ^ 1) + 2 * jnp.arange(chips)) % ctx_size,
            ]
        )
        key_blocks = jnp.take(sorted_blocks, sources, axis=1)
        key_ids = (key_blocks[:, :, None] * block_rows + offsets).reshape(2, 1, -1)
        cosines, sine_terms = rope_tables(places, head_dim)
        tok, cot = tokens[0], cotangent[0]
        rows_width = (row_count, width)
        proj_ready = list(
            lax.optimization_barrier((*proj_mine, gains, qk_gains, place, cosines, sine_terms))
        )[: fsdp_size - 1]
        proj_theirs = with_partners(proj_ready)

        gate_half = lax.dynamic_slice_in_dim(gate_weight, parity * half_rows, half_rows, axis=1)
        up_half = lax.dynamic_slice_in_dim(up_weight, parity * half_rows, half_rows, axis=1)
        down_half = lax.dynamic_slice_in_dim(down_weight, parity * half_rows, half_rows, axis=0)
        out_half = lax.dynamic_slice_in_dim(
            output_weight, parity * (out_rows // 2), out_rows // 2, axis=0
        )
        pair_half = jnp.concatenate([gate_half, up_half], axis=1)
        pair_half = after(pair_half, *proj_mine)
        out_mine = others_fsdp(out_half)
        pair_mine = others_fsdp(pair_half)

        normed, query_rows, own_pair, query_raw, key_raw, proj_full = run_kernel(
            pre_kernel,
            (place, tok, gains, qk_gains, cosines, sine_terms,
             query_weight, key_weight, value_weight, proj_ready, proj_theirs),
            (
                (rows_width, bf16),
                ((row_count, query_width), bf16),
                ((row_count, 2 * head_dim), bf16),
                ((row_count, query_width), f32),
                ((row_count, head_dim), f32),
                ((fsdp_size * shard_rows, proj_width), bf16),
            ),
        )
        kv_mine = [own_pair] + [from_peer(own_pair, "ctx", 2 * k) for k in range(1, chips)]
        kv_ready = after(own_pair, query_last, query_first, key_ids)
        kv_theirs = [with_partner(kv_ready)] + with_partners(kv_mine[1:])
        down_mine = others_fsdp(after(down_half, own_pair))
        out_theirs = with_partners(out_mine)
        pair_ready = list(lax.optimization_barrier((*pair_mine, *kv_mine[1:])))[: fsdp_size - 1]
        pair_theirs = with_partners(pair_ready)
        down_theirs = with_partners(down_mine)
        attended, log_total, key_pairs, output_full, projected, hidden, feed_in = run_kernel(
            attend_kernel,
            (place, tok, query_rows, kv_mine, kv_theirs, query_last, query_first, key_ids,
             output_weight, out_mine, out_theirs, gains),
            (
                ((row_count, query_width), bf16),
                ((2, head_count * block_rows, 1), f32),
                ((2, ctx_size * block_rows, 2 * head_dim), bf16),
                ((fsdp_size * out_rows, width), bf16),
                (rows_width, f32),
                (rows_width, f32),
                (rows_width, bf16),
            ),
        )
        feed_all = [feed_in] + others_fsdp(feed_in)
        output, grad_feed, grad_hidden, grad_proj, grad_attended, gmix, gpre, gpost = run_kernel(
            feed_kernel,
            (place, cot, feed_in, hidden, projected, output_full, gains,
             gate_weight, up_weight, down_weight,
             pair_ready + pair_theirs, down_mine + down_theirs),
            (
                (rows_width, f32),
                (rows_width, bf16),
                (rows_width, f32),
                (rows_width, bf16),
                ((row_count, query_width), bf16),
                ((1, width), f32),
                ((1, width), f32),
                ((1, width), f32),
            ),
            (((row_count, fsdp_size * hidden_rows), f32),) * 2,
        )
        grad_all = [grad_feed] + others_fsdp(grad_feed)
        query_back, pairs_mine, pairs_theirs, gqgain = run_kernel(
            attend_back_kernel,
            (query_rows, key_pairs, grad_attended, attended, log_total,
             query_last, query_first, key_ids, query_raw, qk_gains, cosines, sine_terms),
            (
                ((row_count, query_width), bf16),
                ((chips, row_count, 2 * head_dim), f32),
                ((chips, row_count, 2 * head_dim), bf16),
                ((1, head_dim), f32),
            ),
        )

        pairs_other = with_partner(pairs_theirs)
        chip_part = pairs_mine + pairs_other.astype(f32)
        chip_send = [chip_part[chips - k].astype(bf16) for k in range(1, chips)]
        chip_own = chip_part[0]
        back_parts = [from_peer(chip_send[k - 1], "ctx", 2 * k) for k in range(1, chips)]

        early_rows = 3 * half_rows + fsdp_size * out_rows // 2
        early_mine, early_theirs = run_kernel(
            weight_kernel,
            (place, feed_all, grad_all, gate_weight, up_weight, down_weight, attended, grad_proj),
            (
                ((early_rows, width), f32),
                ((early_rows, width), bf16),
            ),
            (((2 * early_rows, width), f32),),
        )
        early_feed, out_chunks = run_kernel(
            early_pack_kernel,
            (place, early_mine, with_partner(early_theirs)),
            (
                ((3 * half_rows, width), bf16),
                [((out_rows // 2, width), bf16)] * fsdp_size,
            ),
        )
        out_sum = out_chunks[0].astype(f32)
        for k in range(1, fsdp_size):
            out_sum = out_sum + from_peer(out_chunks[k], "fsdp", k).astype(f32)
        early = sum_chips(jnp.concatenate([early_feed, out_sum.astype(bf16)], axis=0), ctx_place)
        gate_grad, up_grad, down_grad, out_grad = run_kernel(
            early_last_kernel,
            (place, early, with_partner(early)),
            (
                ((width, hidden_rows), f32),
                ((width, hidden_rows), f32),
                ((hidden_rows, width), f32),
                ((out_rows, width), f32),
            ),
        )

        tokens_grad, late_mine, late_theirs, late_terms = run_kernel(
            post_kernel,
            (place, tok, chip_own, back_parts, key_raw, gains, qk_gains,
             cosines, sine_terms, normed, query_back, proj_full, grad_hidden,
             gqgain, gmix, gpre, gpost),
            (
                (rows_width, f32),
                ((width, proj_half), f32),
                ((width, proj_half), bf16),
                ((16, proj_half), bf16),
            ),
            (
                ((row_count, proj_width), bf16),
                ((width, proj_width), f32),
                ((8, proj_half), f32),
            ),
        )
        late_shape = ((shard_rows + 16, proj_half), bf16)
        late_chunks = run_kernel(
            late_pack_kernel,
            (place, late_mine, with_partner(late_theirs), late_terms),
            [late_shape] * fsdp_size,
        )
        late_parts = [late_chunks[0]] + [
            from_peer(late_chunks[k], "fsdp", k) for k in range(1, fsdp_size)
        ]
        (late,) = run_kernel(late_sum_kernel, late_parts, [late_shape])
        bit = 2
        while bit < ctx_size:
            other = with_partner(late, bit)
            (late,) = run_kernel(late_sum_kernel, [late, other], [late_shape])
            bit *= 2
        query_grad, key_grad, value_grad, gain_sums = run_kernel(
            late_last_kernel,
            (place, late, with_partner(late)),
            (
                ((shard_rows, query_width), f32),
                ((shard_rows, head_dim), f32),
                ((shard_rows, head_dim), f32),
                ((8, proj_half), f32),
            ),
            (((shard_rows, proj_width), f32),),
        )
        wide_sums = lax.dynamic_slice(gain_sums, (0, fsdp_place * gain_cols), (4, gain_cols))
        head_sums = lax.dynamic_slice(gain_sums, (4, fsdp_place * head_cols), (2, head_cols))
        return (
            output[None],
            tokens_grad[None],
            query_grad,
            key_grad,
            value_grad,
            out_grad,
            gate_grad,
            up_grad,
            down_grad,
            wide_sums[0],
            head_sums[0],
            head_sums[1],
            wide_sums[1],
            wide_sums[2],
            wide_sums[3],
        )

    return body


def solution(mesh):
    in_specs = (
        P("fsdp", "ctx", None),
        P("fsdp", "ctx", None),
        P("fsdp", "ctx"),
        P(),
        P("fsdp", None),
        P("fsdp", None),
        P("fsdp", None),
        P("fsdp", None),
        P(None, "fsdp"),
        P(None, "fsdp"),
        P("fsdp", None),
        P("fsdp"),
        P("fsdp"),
        P("fsdp"),
        P("fsdp"),
        P("fsdp"),
        P("fsdp"),
    )
    out_specs = (
        P("fsdp", "ctx", None),
        P("fsdp", "ctx", None),
        P("fsdp", None),
        P("fsdp", None),
        P("fsdp", None),
        P("fsdp", None),
        P(None, "fsdp"),
        P(None, "fsdp"),
        P("fsdp", None),
        P("fsdp"),
        P("fsdp"),
        P("fsdp"),
        P("fsdp"),
        P("fsdp"),
        P("fsdp"),
    )
    inner = make_body(mesh.shape["fsdp"], mesh.shape["ctx"])

    return jax.shard_map(inner, mesh=mesh, in_specs=in_specs, out_specs=out_specs, check_vma=False)
```

profile of v0, /device:TPU:0, one launch (start us, length us, event | category | flops | bytes accessed | tf_op | source)
XLA Modules:
  0.0 310.6 jit_solution(11790051483998387144)
XLA Ops:
  4.7 4.0 %collective-permute-start = (f32[6,160]{1,0:T(8,128)S(1)}, f32[6,160]{1,0:T(8,128)S(1)}, u32[]{:S(2)}, u32[]{:S(2)}) collective-permute-start(f32[6,160]{1,0:T(8,128)S(1)} %get-tuple-element.142), channel_id=1, source_target_pairs={{1,0},{2,1},{3,2},{0,3},{5,4},{6,5},{7,6},{4,7},{9,8},{10,9},{11,1... | collective-permute-start | bytes 11528 | tf_op jit(solution)/shard_map/ppermute | solution.py:476
  11.3 2.0 collective-permute-start.4
  23.8 3.0 collective-permute-start.16
  32.8 4.3 %shard_map.280 = (bf16[256,640]{1,0:T(8,128)(2,1)}, bf16[256,1024]{1,0:T(8,128)(2,1)}, bf16[256,512]{1,0:T(8,128)(2,1)}, f32[256,1024]{1,0:T(8,128)}, f32[256,256]{1,0:T(8,128)}, /*index=5*/bf16[640,1536]{1,0:T(8,128)(2,1)}) custom-call(s32[3]{0:T(128)} %pad_add_fusion.2.refs_0_, f32[256,640]{1,0:T(8,128)} %bitcast.66, ...), custom_call_target="tpu_custom_call" | custom-call | tf_op jit(solution)/shard_map/pallas_call | solution.py:468
  37.1 2.6 collective-permute-start.10
  40.4 1.6 collective-permute-start.11
  42.1 2.4 collective-permute-start.22
  44.5 1.5 collective-permute-start.23
  46.0 12.0 %collective-permute-done.10.refs_5_ = bf16[256,512]{1,0:T(8,128)(2,1)S(1)} collective-permute-done((bf16[256,512]{1,0:T(8,128)(2,1)}, bf16[256,512]{1,0:T(8,128)(2,1)S(1)}, u32[]{:S(2)}, u32[]{:S(2)}) %collective-permute-start.10) | collective-permute-done | bytes 262176 | tf_op jit(solution)/shard_map/ppermute | solution.py:476
  58.1 2.4 collective-permute-start.28
  61.2 4.5 %collective-permute-done.9.refs_4_ = bf16[256,512]{1,0:T(8,128)(2,1)} collective-permute-done((bf16[256,512]{1,0:T(8,128)(2,1)S(1)}, bf16[256,512]{1,0:T(8,128)(2,1)}, u32[]{:S(2)}, u32[]{:S(2)}) %collective-permute-start.9) | collective-permute-done | bytes 262176 | tf_op jit(solution)/shard_map/ppermute | solution.py:476
  65.7 1.5 collective-permute-done.12.refs_7_
  68.7 12.0 %collective-permute-done.28.refs_16_ = bf16[256,640]{1,0:T(8,128)(2,1)S(1)} collective-permute-done((bf16[256,640]{1,0:T(8,128)(2,1)S(1)}, bf16[256,640]{1,0:T(8,128)(2,1)S(1)}, u32[]{:S(2)}, u32[]{:S(2)}) %collective-permute-start.28) | collective-permute-done | bytes 327712 | tf_op jit(solution)/shard_map/ppermute | solution.py:476
  80.7 2.7 collective-permute-start.30
  84.5 6.3 %collective-permute-done.30.refs_18_ = bf16[256,640]{1,0:T(8,128)(2,1)S(1)} collective-permute-done((bf16[256,640]{1,0:T(8,128)(2,1)S(1)}, bf16[256,640]{1,0:T(8,128)(2,1)S(1)}, u32[]{:S(2)}, u32[]{:S(2)}) %collective-permute-start.30) | collective-permute-done | bytes 327712 | tf_op jit(solution)/shard_map/ppermute | solution.py:476
  92.1 7.4 %shard_map.281 = (bf16[256,1024]{1,0:T(8,128)(2,1)}, f32[2,512,1]{2,1,0:T(8,128)}, bf16[2,1024,512]{2,1,0:T(8,128)(2,1)}, bf16[1024,640]{1,0:T(8,128)(2,1)}, f32...) custom-call(s32[3]{0:T(128)} %pad_add_fusion.2.refs_0_, f32[256,640]{1,0:T(8,128)} %bitcast.67, ...), custom_call_target="tpu_custom_call" | custom-call | tf_op jit(solution)/shard_map/pallas_call | solution.py:468
  99.6 1.5 collective-permute-start.45
  101.1 1.5 collective-permute-start.46
  104.1 13.5 %shard_map.282 = (f32[256,640]{1,0:T(8,128)}, bf16[256,640]{1,0:T(8,128)(2,1)}, f32[256,640]{1,0:T(8,128)}, bf16[256,640]{1,0:T(8,128)(2,1)}, bf16[256,1024]{1,0...) custom-call(s32[3]{0:T(128)} %pad_add_fusion.2.refs_0_, f32[256,640]{1,0:T(8,128)} %bitcast.73, ...), custom_call_target="tpu_custom_call" | custom-call | tf_op jit(solution)/shard_map/pallas_call | solution.py:468
  117.6 2.7 collective-permute-start.48
  121.0 7.7 %collective-permute-done.48.refs_6_ = bf16[256,640]{1,0:T(8,128)(2,1)S(1)} collective-permute-done((bf16[256,640]{1,0:T(8,128)(2,1)}, bf16[256,640]{1,0:T(8,128)(2,1)S(1)}, u32[]{:S(2)}, u32[]{:S(2)}) %collective-permute-start.48) | collective-permute-done | bytes 327712 | tf_op jit(solution)/shard_map/ppermute | solution.py:476
  128.7 7.7 %collective-permute-done.49.refs_7_ = bf16[256,640]{1,0:T(8,128)(2,1)S(1)} collective-permute-done((bf16[256,640]{1,0:T(8,128)(2,1)}, bf16[256,640]{1,0:T(8,128)(2,1)S(1)}, u32[]{:S(2)}, u32[]{:S(2)}) %collective-permute-start.49) | collective-permute-done | bytes 327712 | tf_op jit(solution)/shard_map/ppermute | solution.py:476
  137.3 11.0 %shard_map.290 = (f32[1280,640]{1,0:T(8,128)}, bf16[1280,640]{1,0:T(8,128)(2,1)}) custom-call(s32[3]{0:T(128)} %pad_add_fusion.2.refs_0_, bf16[256,640]{1,0:T(8,128)(2,1)} %get-tuple-element.78.refs_2_.refs_1_, bf16[256,640]{1,0:T(8,128)(2,1)} %copy-done.22, bf16[256,640]{1,0:T(8,128)(2,1)} %copy-done.24, bf16[256,640]{1,0:T(8,128)(2,1)} %copy-done.26, ...), custom_call_target="tpu_custom_call" | custom-call | tf_op jit(solution)/shard_map/pallas_call | solution.py:468
  148.4 7.9 %shard_map.283 = (bf16[256,1024]{1,0:T(8,128)(2,1)}, f32[4,256,512]{2,1,0:T(8,128)}, bf16[4,256,512]{2,1,0:T(8,128)(2,1)}, f32[1,256]{1,0:T(1,128)}) custom-call(bf16[256,1024]{1,0:T(8,128)(2,1)} %get-tuple-element.75.refs_2_.refs_0_, bf16[2,1024,512]{2,1,0:T(8,128)(2,1)} %get-tuple-element.88.refs_1_, bf16[256,1024]{1,0:T(8,128)(2,1)} %get-tuple-element.89.refs_2_, ...), custom_call_target="tpu_custom_call" | custom-call | tf_op jit(solution)/shard_map/pallas_call | solution.py:468
  158.0 3.7 %shard_map.291 = (bf16[768,640]{1,0:T(8,128)(2,1)}, bf16[128,640]{1,0:T(8,128)(2,1)}, bf16[128,640]{1,0:T(8,128)(2,1)}, bf16[128,640]{1,0:T(8,128)(2,1)}, bf16[128,640]{1,0:T(8,128)(2,1)}) custom-call(s32[3]{0:T(128)} %pad_add_fusion.2.refs_0_, f32[1280,640]{1,0:T(8,128)} %get-tuple-element.117.refs_1_, bf16[1280,640]{1,0:T(8,128)(2,1)} %copy-done.7), custom_call_target="tpu_custom_call" | custom-call | tf_op jit(solution)/shard_map/pallas_call | solution.py:468
  164.2 4.7 %collective-permute-done.52 = bf16[128,640]{1,0:T(8,128)(2,1)S(1)} collective-permute-done((bf16[128,640]{1,0:T(8,128)(2,1)}, bf16[128,640]{1,0:T(8,128)(2,1)S(1)}, u32[]{:S(2)}, u32[]{:S(2)}) %collective-permute-start.52) | collective-permute-done | bytes 163872 | tf_op jit(solution)/shard_map/ppermute | solution.py:476
  169.0 2.6 collective-permute-done.53
  176.4 2.3 fusion.10
  178.7 10.4 %collective-permute-done.55 = bf16[448,640]{1,0:T(8,128)(2,1)} collective-permute-done((bf16[448,640]{1,0:T(8,128)(2,1)}, bf16[448,640]{1,0:T(8,128)(2,1)}, u32[]{:S(2)}, u32[]{:S(2)}) %collective-permute-start.55) | collective-permute-done | bytes 573472 | tf_op jit(solution)/shard_map/ppermute | solution.py:479
  192.3 1.9 collective-permute-start.35
  197.1 7.3 %collective-permute-done.35.refs_3_ = bf16[256,512]{1,0:T(8,128)(2,1)S(1)} collective-permute-done((bf16[256,512]{1,0:T(8,128)(2,1)}, bf16[256,512]{1,0:T(8,128)(2,1)S(1)}, u32[]{:S(2)}, u32[]{:S(2)}) %collective-permute-start.35) | collective-permute-done | bytes 262176 | tf_op jit(solution)/shard_map/ppermute | solution.py:476
  204.4 22.5 %collective-permute-done.36.refs_4_ = bf16[256,512]{1,0:T(8,128)(2,1)S(1)} collective-permute-done((bf16[256,512]{1,0:T(8,128)(2,1)}, bf16[256,512]{1,0:T(8,128)(2,1)S(1)}, u32[]{:S(2)}, u32[]{:S(2)}) %collective-permute-start.36) | collective-permute-done | bytes 262176 | tf_op jit(solution)/shard_map/ppermute | solution.py:476
  227.7 5.9 %shard_map.284 = (f32[256,640]{1,0:T(8,128)}, f32[640,768]{1,0:T(8,128)}, bf16[640,768]{1,0:T(8,128)(2,1)}, bf16[16,768]{1,0:T(8,128)(2,1)}) custom-call(s32[3]{0:T(128)} %pad_add_fusion.2.refs_0_, f32[256,640]{1,0:T(8,128)} %bitcast.68, f32[256,512]{1,0:T(8,128)} %slice_bitcast_fusion.refs_2_, bf16[256,512]{1,0:T(8,128)(2,1)} %copy-done.42, ...), custom_call_target="tpu_custom_call" | custom-call | tf_op jit(solution)/shard_map/pallas_call | solution.py:468
  235.1 13.9 %collective-permute-done.57 = bf16[224,640]{1,0:T(8,128)(2,1)S(1)} collective-permute-done((bf16[224,640]{1,0:T(8,128)(2,1)S(1)}, bf16[224,640]{1,0:T(8,128)(2,1)S(1)}, u32[]{:S(2)}, u32[]{:S(2)}) %collective-permute-start.57) | collective-permute-done | bytes 286752 | tf_op jit(solution)/shard_map/ppermute | solution.py:479
  250.1 2.9 shard_map.285
  253.0 3.1 collective-permute-start.39
  257.4 6.1 %collective-permute-done.39.refs_1_ = bf16[176,768]{1,0:T(8,128)(2,1)S(1)} collective-permute-done((bf16[176,768]{1,0:T(8,128)(2,1)}, bf16[176,768]{1,0:T(8,128)(2,1)S(1)}, u32[]{:S(2)}, u32[]{:S(2)}) %collective-permute-start.39) | collective-permute-done | bytes 270368 | tf_op jit(solution)/shard_map/ppermute | solution.py:476
  263.5 6.8 %collective-permute-done.40.refs_2_ = bf16[176,768]{1,0:T(8,128)(2,1)S(1)} collective-permute-done((bf16[176,768]{1,0:T(8,128)(2,1)}, bf16[176,768]{1,0:T(8,128)(2,1)S(1)}, u32[]{:S(2)}, u32[]{:S(2)}) %collective-permute-start.40) | collective-permute-done | bytes 270368 | tf_op jit(solution)/shard_map/ppermute | solution.py:476
  271.1 2.0 shard_map.286.refs_0_
  273.1 1.7 collective-permute-start.42
  275.2 5.4 %collective-permute-done.42.refs_1_ = bf16[176,768]{1,0:T(8,128)(2,1)S(1)} collective-permute-done((bf16[176,768]{1,0:T(8,128)(2,1)}, bf16[176,768]{1,0:T(8,128)(2,1)S(1)}, u32[]{:S(2)}, u32[]{:S(2)}) %collective-permute-start.42) | collective-permute-done | bytes 270368 | tf_op jit(solution)/shard_map/ppermute | solution.py:479
  281.3 1.8 shard_map.287.refs_0_
  283.1 12.5 %collective-permute-done.43.refs_1_ = bf16[176,768]{1,0:T(8,128)(2,1)S(1)} collective-permute-done((bf16[176,768]{1,0:T(8,128)(2,1)}, bf16[176,768]{1,0:T(8,128)(2,1)S(1)}, u32[]{:S(2)}, u32[]{:S(2)}) %collective-permute-start.43) | collective-permute-done | bytes 270368 | tf_op jit(solution)/shard_map/ppermute | solution.py:479
  296.3 1.8 shard_map.288.refs_1_
  298.1 1.8 collective-permute-done.44.refs_2_
  300.6 2.1 shard_map.289
  303.4 1.5 fusion.11
  306.5 4.1 %shard_map.292 = (f32[640,512]{1,0:T(8,128)}, f32[640,512]{1,0:T(8,128)}, f32[512,640]{1,0:T(8,128)}, f32[256,640]{1,0:T(8,128)}) custom-call(s32[3]{0:T(128)} %pad_add_fusion.2.refs_0_, bf16[896,640]{1,0:T(8,128)(2,1)} %copy-done, bf16[896,640]{1,0:T(8,128)(2,1)} %copy-done.8), custom_call_target="tpu_custom_call" | custom-call | tf_op jit(solution)/shard_map/pallas_call | solution.py:468
  (268 shorter events, 55.4 us)
Async XLA Ops:
  4.7 18.3 %collective-permute-start = (f32[6,160]{1,0:T(8,128)S(1)}, f32[6,160]{1,0:T(8,128)S(1)}, u32[]{:S(2)}, u32[]{:S(2)}) collective-permute-start(f32[6,160]{1,0:T(8,128)S(1)} %get-tuple-element.142), channel_id=1, source_target_pairs={{1,0},{2,1},{3,2},{0,3},{5,4},{6,5},{7,6},{4,7},{9,8},{10,9},{11,1... | collective-permute-start | bytes 11528 | tf_op jit(solution)/shard_map/ppermute | solution.py:476
  8.7 15.1 %collective-permute-start.1 = (f32[6,160]{1,0:T(8,128)S(1)}, f32[6,160]{1,0:T(8,128)S(1)}, u32[]{:S(2)}, u32[]{:S(2)}) collective-permute-start(f32[6,160]{1,0:T(8,128)S(1)} %get-tuple-element.142), channel_id=1, source_target_pairs={{2,0},{3,1},{0,2},{1,3},{6,4},{7,5},{4,6},{5,7},{10,8},{11,9},{8,1... | collective-permute-start | bytes 11528 | tf_op jit(solution)/shard_map/ppermute | solution.py:476
  11.2 18.6 %collective-permute-start.3 = (bf16[160,768]{1,0:T(8,128)(2,1)S(1)}, bf16[160,768]{1,0:T(8,128)(2,1)S(1)}, u32[]{:S(2)}, u32[]{:S(2)}) collective-permute-start(bf16[160,768]{1,0:T(8,128)(2,1)S(1)} %maximum_select_fusion), channel_id=1, source_target_pairs={{1,0},{2,1},{3,2},{0,3},{5,4},{6,5},{7,6},{4,7},{9,8},{10,9},{11,1... | collective-permute-start | bytes 737288 | tf_op jit(solution)/shard_map/ppermute | solution.py:476
  11.3 18.4 %collective-permute-start.4 = (bf16[160,768]{1,0:T(8,128)(2,1)S(1)}, bf16[160,768]{1,0:T(8,128)(2,1)S(1)}, u32[]{:S(2)}, u32[]{:S(2)}) collective-permute-start(bf16[160,768]{1,0:T(8,128)(2,1)S(1)} %maximum_select_fusion), channel_id=1, source_target_pairs={{2,0},{3,1},{0,2},{1,3},{6,4},{7,5},{4,6},{5,7},{10,8},{11,9},{8,1... | collective-permute-start | bytes 737288 | tf_op jit(solution)/shard_map/ppermute | solution.py:476
  13.3 16.5 %collective-permute-start.5 = (bf16[160,768]{1,0:T(8,128)(2,1)S(1)}, bf16[160,768]{1,0:T(8,128)(2,1)S(1)}, u32[]{:S(2)}, u32[]{:S(2)}) collective-permute-start(bf16[160,768]{1,0:T(8,128)(2,1)S(1)} %maximum_select_fusion), channel_id=1, source_target_pairs={{3,0},{0,1},{1,2},{2,3},{7,4},{4,5},{5,6},{6,7},{11,8},{8,9},{9,10... | collective-permute-start | bytes 737288 | tf_op jit(solution)/shard_map/ppermute | solution.py:476
  23.8 15.9 %collective-permute-start.16 = (bf16[128,640]{1,0:T(8,128)(2,1)S(1)}, bf16[128,640]{1,0:T(8,128)(2,1)S(1)}, u32[]{:S(2)}, u32[]{:S(2)}) collective-permute-start(bf16[128,640]{1,0:T(8,128)(2,1)S(1)} %constant_dynamic-slice_fusion.4), channel_id=1, source_target_pairs={{1,0},{2,1},{3,2},{0,3},{5,4},{6,5},{7,6},{4,7},{9,8},{10,9},{11,1... | collective-permute-start | bytes 491528 | tf_op jit(solution)/shard_map/ppermute | solution.py:476
  27.7 12.1 %collective-permute-start.17 = (bf16[128,640]{1,0:T(8,128)(2,1)S(1)}, bf16[128,640]{1,0:T(8,128)(2,1)}, u32[]{:S(2)}, u32[]{:S(2)}) collective-permute-start(bf16[128,640]{1,0:T(8,128)(2,1)S(1)} %constant_dynamic-slice_fusion.4), channel_id=1, source_target_pairs={{2,0},{3,1},{0,2},{1,3},{6,4},{7,5},{4,6},{5,7},{10,8},{11,9},{8,1... | collective-permute-start | bytes 491528 | tf_op jit(solution)/shard_map/ppermute | solution.py:476
  31.4 9.0 %collective-permute-start.18 = (bf16[128,640]{1,0:T(8,128)(2,1)S(1)}, bf16[128,640]{1,0:T(8,128)(2,1)}, u32[]{:S(2)}, u32[]{:S(2)}) collective-permute-start(bf16[128,640]{1,0:T(8,128)(2,1)S(1)} %constant_dynamic-slice_fusion.4), channel_id=1, source_target_pairs={{3,0},{0,1},{1,2},{2,3},{7,4},{4,5},{5,6},{6,7},{11,8},{8,9},{9,10... | collective-permute-start | bytes 491528 | tf_op jit(solution)/shard_map/ppermute | solution.py:476
  37.1 21.0 %collective-permute-start.10 = (bf16[256,512]{1,0:T(8,128)(2,1)}, bf16[256,512]{1,0:T(8,128)(2,1)S(1)}, u32[]{:S(2)}, u32[]{:S(2)}) collective-permute-start(bf16[256,512]{1,0:T(8,128)(2,1)} %get-tuple-element.77.refs_3_), channel_id=1, source_target_pairs={{16,0},{20,4},{24,8},{28,12},{0,16},{4,20},{8,24},{12,28},{17,1},{... | collective-permute-start | bytes 786440 | tf_op jit(solution)/shard_map/ppermute | solution.py:476
  40.4 17.7 %collective-permute-start.11 = (bf16[256,512]{1,0:T(8,128)(2,1)S(1)}, bf16[256,512]{1,0:T(8,128)(2,1)}, u32[]{:S(2)}, u32[]{:S(2)}) collective-permute-start(bf16[256,512]{1,0:T(8,128)(2,1)S(1)} %copy-done.36), channel_id=1, source_target_pairs={{24,0},{28,4},{0,8},{4,12},{8,16},{12,20},{16,24},{20,28},{25,1},{... | collective-permute-start | bytes 786440 | tf_op jit(solution)/shard_map/ppermute | solution.py:476
  42.1 41.3 %collective-permute-start.22 = (bf16[640,512]{1,0:T(8,128)(2,1)S(1)}, bf16[640,512]{1,0:T(8,128)(2,1)S(1)}, u32[]{:S(2)}, u32[]{:S(2)}) collective-permute-start(bf16[640,512]{1,0:T(8,128)(2,1)S(1)} %pad_maximum_fusion.2), channel_id=1, source_target_pairs={{1,0},{2,1},{3,2},{0,3},{5,4},{6,5},{7,6},{4,7},{9,8},{10,9},{11,1... | collective-permute-start | bytes 1966088 | tf_op jit(solution)/shard_map/ppermute | solution.py:476
  44.5 39.0 %collective-permute-start.23 = (bf16[640,512]{1,0:T(8,128)(2,1)S(1)}, bf16[640,512]{1,0:T(8,128)(2,1)S(1)}, u32[]{:S(2)}, u32[]{:S(2)}) collective-permute-start(bf16[640,512]{1,0:T(8,128)(2,1)S(1)} %pad_maximum_fusion.2), channel_id=1, source_target_pairs={{2,0},{3,1},{0,2},{1,3},{6,4},{7,5},{4,6},{5,7},{10,8},{11,9},{8,1... | collective-permute-start | bytes 1966088 | tf_op jit(solution)/shard_map/ppermute | solution.py:476
  46.0 37.9 %collective-permute-start.24 = (bf16[640,512]{1,0:T(8,128)(2,1)S(1)}, bf16[640,512]{1,0:T(8,128)(2,1)S(1)}, u32[]{:S(2)}, u32[]{:S(2)}) collective-permute-start(bf16[640,512]{1,0:T(8,128)(2,1)S(1)} %pad_maximum_fusion.2), channel_id=1, source_target_pairs={{3,0},{0,1},{1,2},{2,3},{7,4},{4,5},{5,6},{6,7},{11,8},{8,9},{9,10... | collective-permute-start | bytes 1966088 | tf_op jit(solution)/shard_map/ppermute | solution.py:476
  58.0 7.7 %collective-permute-start.9 = (bf16[256,512]{1,0:T(8,128)(2,1)S(1)}, bf16[256,512]{1,0:T(8,128)(2,1)}, u32[]{:S(2)}, u32[]{:S(2)}) collective-permute-start(bf16[256,512]{1,0:T(8,128)(2,1)S(1)} %copy-done.36), channel_id=1, source_target_pairs={{8,0},{12,4},{16,8},{20,12},{24,16},{28,20},{0,24},{4,28},{9,1},{1... | collective-permute-start | bytes 786440 | tf_op jit(solution)/shard_map/ppermute | solution.py:476
  58.1 22.6 %collective-permute-start.28 = (bf16[256,640]{1,0:T(8,128)(2,1)S(1)}, bf16[256,640]{1,0:T(8,128)(2,1)S(1)}, u32[]{:S(2)}, u32[]{:S(2)}) collective-permute-start(bf16[256,640]{1,0:T(8,128)(2,1)S(1)} %constant_dynamic-slice_fusion.1), channel_id=1, source_target_pairs={{1,0},{2,1},{3,2},{0,3},{5,4},{6,5},{7,6},{4,7},{9,8},{10,9},{11,1... | collective-permute-start | bytes 983048 | tf_op jit(solution)/shard_map/ppermute | solution.py:476
  67.2 16.8 %collective-permute-start.29 = (bf16[256,640]{1,0:T(8,128)(2,1)S(1)}, bf16[256,640]{1,0:T(8,128)(2,1)S(1)}, u32[]{:S(2)}, u32[]{:S(2)}) collective-permute-start(bf16[256,640]{1,0:T(8,128)(2,1)S(1)} %constant_dynamic-slice_fusion.1), channel_id=1, source_target_pairs={{2,0},{3,1},{0,2},{1,3},{6,4},{7,5},{4,6},{5,7},{10,8},{11,9},{8,1... | collective-permute-start | bytes 983048 | tf_op jit(solution)/shard_map/ppermute | solution.py:476
  80.7 10.1 %collective-permute-start.30 = (bf16[256,640]{1,0:T(8,128)(2,1)S(1)}, bf16[256,640]{1,0:T(8,128)(2,1)S(1)}, u32[]{:S(2)}, u32[]{:S(2)}) collective-permute-start(bf16[256,640]{1,0:T(8,128)(2,1)S(1)} %constant_dynamic-slice_fusion.1), channel_id=1, source_target_pairs={{3,0},{0,1},{1,2},{2,3},{7,4},{4,5},{5,6},{6,7},{11,8},{8,9},{9,10... | collective-permute-start | bytes 983048 | tf_op jit(solution)/shard_map/ppermute | solution.py:476
  83.5 7.8 %collective-permute-start.14 = (bf16[256,512]{1,0:T(8,128)(2,1)S(1)}, bf16[256,512]{1,0:T(8,128)(2,1)S(1)}, u32[]{:S(2)}, u32[]{:S(2)}) collective-permute-start(bf16[256,512]{1,0:T(8,128)(2,1)S(1)} %collective-permute-done.10.refs_5_), channel_id=1, source_target_pairs={{0,4},{4,0},{8,12},{12,8},{16,20},{20,16},{24,28},{28,24},{1,5},{5... | collective-permute-start | bytes 786440 | tf_op jit(solution)/shard_map/ppermute | solution.py:479
  84.1 7.8 %collective-permute-start.31 = (bf16[256,640]{1,0:T(8,128)(2,1)S(1)}, bf16[256,640]{1,0:T(8,128)(2,1)S(1)}, u32[]{:S(2)}, u32[]{:S(2)}) collective-permute-start(bf16[256,640]{1,0:T(8,128)(2,1)S(1)} %collective-permute-done.28.refs_16_), channel_id=1, source_target_pairs={{0,4},{4,0},{8,12},{12,8},{16,20},{20,16},{24,28},{28,24},{1,5},{5... | collective-permute-start | bytes 983048 | tf_op jit(solution)/shard_map/ppermute | solution.py:479
  90.8 11.9 %collective-permute-start.25 = (bf16[640,512]{1,0:T(8,128)(2,1)S(1)}, bf16[640,512]{1,0:T(8,128)(2,1)S(1)}, u32[]{:S(2)}, u32[]{:S(2)}) collective-permute-start(bf16[640,512]{1,0:T(8,128)(2,1)S(1)} %collective-permute-done.22.refs_10_), channel_id=1, source_target_pairs={{0,4},{4,0},{8,12},{12,8},{16,20},{20,16},{24,28},{28,24},{1,5},{5... | collective-permute-start | bytes 1966088 | tf_op jit(solution)/shard_map/ppermute | solution.py:479
  90.8 12.1 %collective-permute-start.26 = (bf16[640,512]{1,0:T(8,128)(2,1)S(1)}, bf16[640,512]{1,0:T(8,128)(2,1)S(1)}, u32[]{:S(2)}, u32[]{:S(2)}) collective-permute-start(bf16[640,512]{1,0:T(8,128)(2,1)S(1)} %collective-permute-done.23.refs_11_), channel_id=1, source_target_pairs={{0,4},{4,0},{8,12},{12,8},{16,20},{20,16},{24,28},{28,24},{1,5},{5... | collective-permute-start | bytes 1966088 | tf_op jit(solution)/shard_map/ppermute | solution.py:479
  91.3 11.6 %collective-permute-start.27 = (bf16[640,512]{1,0:T(8,128)(2,1)S(1)}, bf16[640,512]{1,0:T(8,128)(2,1)S(1)}, u32[]{:S(2)}, u32[]{:S(2)}) collective-permute-start(bf16[640,512]{1,0:T(8,128)(2,1)S(1)} %collective-permute-done.24.refs_12_), channel_id=1, source_target_pairs={{0,4},{4,0},{8,12},{12,8},{16,20},{20,16},{24,28},{28,24},{1,5},{5... | collective-permute-start | bytes 1966088 | tf_op jit(solution)/shard_map/ppermute | solution.py:479
  91.4 8.2 %collective-permute-start.32 = (bf16[256,640]{1,0:T(8,128)(2,1)S(1)}, bf16[256,640]{1,0:T(8,128)(2,1)S(1)}, u32[]{:S(2)}, u32[]{:S(2)}) collective-permute-start(bf16[256,640]{1,0:T(8,128)(2,1)S(1)} %collective-permute-done.29.refs_17_), channel_id=1, source_target_pairs={{0,4},{4,0},{8,12},{12,8},{16,20},{20,16},{24,28},{28,24},{1,5},{5... | collective-permute-start | bytes 983048 | tf_op jit(solution)/shard_map/ppermute | solution.py:479
  91.8 9.3 %collective-permute-start.33 = (bf16[256,640]{1,0:T(8,128)(2,1)S(1)}, bf16[256,640]{1,0:T(8,128)(2,1)S(1)}, u32[]{:S(2)}, u32[]{:S(2)}) collective-permute-start(bf16[256,640]{1,0:T(8,128)(2,1)S(1)} %collective-permute-done.30.refs_18_), channel_id=1, source_target_pairs={{0,4},{4,0},{8,12},{12,8},{16,20},{20,16},{24,28},{28,24},{1,5},{5... | collective-permute-start | bytes 983048 | tf_op jit(solution)/shard_map/ppermute | solution.py:479
  99.6 21.2 %collective-permute-start.45 = (bf16[256,640]{1,0:T(8,128)(2,1)}, bf16[256,640]{1,0:T(8,128)(2,1)S(1)}, u32[]{:S(2)}, u32[]{:S(2)}) collective-permute-start(bf16[256,640]{1,0:T(8,128)(2,1)} %get-tuple-element.78.refs_2_.refs_1_), channel_id=1, source_target_pairs={{1,0},{2,1},{3,2},{0,3},{5,4},{6,5},{7,6},{4,7},{9,8},{10,9},{11,1... | collective-permute-start | bytes 983048 | tf_op jit(solution)/shard_map/ppermute | solution.py:476
  101.1 19.8 %collective-permute-start.46 = (bf16[256,640]{1,0:T(8,128)(2,1)}, bf16[256,640]{1,0:T(8,128)(2,1)S(1)}, u32[]{:S(2)}, u32[]{:S(2)}) collective-permute-start(bf16[256,640]{1,0:T(8,128)(2,1)} %get-tuple-element.78.refs_2_.refs_1_), channel_id=1, source_target_pairs={{2,0},{3,1},{0,2},{1,3},{6,4},{7,5},{4,6},{5,7},{10,8},{11,9},{8,1... | collective-permute-start | bytes 983048 | tf_op jit(solution)/shard_map/ppermute | solution.py:476
  102.6 18.3 %collective-permute-start.47 = (bf16[256,640]{1,0:T(8,128)(2,1)}, bf16[256,640]{1,0:T(8,128)(2,1)S(1)}, u32[]{:S(2)}, u32[]{:S(2)}) collective-permute-start(bf16[256,640]{1,0:T(8,128)(2,1)} %get-tuple-element.78.refs_2_.refs_1_), channel_id=1, source_target_pairs={{3,0},{0,1},{1,2},{2,3},{7,4},{4,5},{5,6},{6,7},{11,8},{8,9},{9,10... | collective-permute-start | bytes 983048 | tf_op jit(solution)/shard_map/ppermute | solution.py:476
  117.6 11.1 %collective-permute-start.48 = (bf16[256,640]{1,0:T(8,128)(2,1)}, bf16[256,640]{1,0:T(8,128)(2,1)S(1)}, u32[]{:S(2)}, u32[]{:S(2)}) collective-permute-start(bf16[256,640]{1,0:T(8,128)(2,1)} %get-tuple-element.115.refs_5_), channel_id=1, source_target_pairs={{1,0},{2,1},{3,2},{0,3},{5,4},{6,5},{7,6},{4,7},{9,8},{10,9},{11,1... | collective-permute-start | bytes 983048 | tf_op jit(solution)/shard_map/ppermute | solution.py:476
  120.3 16.2 %collective-permute-start.49 = (bf16[256,640]{1,0:T(8,128)(2,1)}, bf16[256,640]{1,0:T(8,128)(2,1)S(1)}, u32[]{:S(2)}, u32[]{:S(2)}) collective-permute-start(bf16[256,640]{1,0:T(8,128)(2,1)} %get-tuple-element.115.refs_5_), channel_id=1, source_target_pairs={{2,0},{3,1},{0,2},{1,3},{6,4},{7,5},{4,6},{5,7},{10,8},{11,9},{8,1... | collective-permute-start | bytes 983048 | tf_op jit(solution)/shard_map/ppermute | solution.py:476
  120.8 15.6 %collective-permute-start.50 = (bf16[256,640]{1,0:T(8,128)(2,1)}, bf16[256,640]{1,0:T(8,128)(2,1)S(1)}, u32[]{:S(2)}, u32[]{:S(2)}) collective-permute-start(bf16[256,640]{1,0:T(8,128)(2,1)} %get-tuple-element.115.refs_5_), channel_id=1, source_target_pairs={{3,0},{0,1},{1,2},{2,3},{7,4},{4,5},{5,6},{6,7},{11,8},{8,9},{9,10... | collective-permute-start | bytes 983048 | tf_op jit(solution)/shard_map/ppermute | solution.py:476
  148.4 8.4 %collective-permute-start.51 = (bf16[1280,640]{1,0:T(8,128)(2,1)}, bf16[1280,640]{1,0:T(8,128)(2,1)S(1)}, u32[]{:S(2)}, u32[]{:S(2)}) collective-permute-start(bf16[1280,640]{1,0:T(8,128)(2,1)} %get-tuple-element.118), channel_id=1, source_target_pairs={{0,4},{4,0},{8,12},{12,8},{16,20},{20,16},{24,28},{28,24},{1,5},{5... | collective-permute-start | bytes 4915208 | tf_op jit(solution)/shard_map/ppermute | solution.py:479
  156.3 19.1 %collective-permute-start.34 = (bf16[4,256,512]{2,1,0:T(8,128)(2,1)}, bf16[4,256,512]{2,1,0:T(8,128)(2,1)S(1)}, u32[]{:S(2)}, u32[]{:S(2)}) collective-permute-start(bf16[4,256,512]{2,1,0:T(8,128)(2,1)} %get-tuple-element.94), channel_id=1, source_target_pairs={{0,4},{4,0},{8,12},{12,8},{16,20},{20,16},{24,28},{28,24},{1,5},{5... | collective-permute-start | bytes 3145736 | tf_op jit(solution)/shard_map/ppermute | solution.py:479
  162.0 9.6 %collective-permute-start.53 = (bf16[128,640]{1,0:T(8,128)(2,1)}, bf16[128,640]{1,0:T(8,128)(2,1)S(1)}, u32[]{:S(2)}, u32[]{:S(2)}) collective-permute-start(bf16[128,640]{1,0:T(8,128)(2,1)} %get-tuple-element.122), channel_id=1, source_target_pairs={{2,0},{3,1},{0,2},{1,3},{6,4},{7,5},{4,6},{5,7},{10,8},{11,9},{8,1... | collective-permute-start | bytes 491528 | tf_op jit(solution)/shard_map/ppermute | solution.py:476
  163.3 8.2 %collective-permute-start.54 = (bf16[128,640]{1,0:T(8,128)(2,1)}, bf16[128,640]{1,0:T(8,128)(2,1)S(1)}, u32[]{:S(2)}, u32[]{:S(2)}) collective-permute-start(bf16[128,640]{1,0:T(8,128)(2,1)} %get-tuple-element.123), channel_id=1, source_target_pairs={{3,0},{0,1},{1,2},{2,3},{7,4},{4,5},{5,6},{6,7},{11,8},{8,9},{9,10... | collective-permute-start | bytes 491528 | tf_op jit(solution)/shard_map/ppermute | solution.py:476
  174.8 14.3 %collective-permute-start.55 = (bf16[448,640]{1,0:T(8,128)(2,1)}, bf16[448,640]{1,0:T(8,128)(2,1)}, u32[]{:S(2)}, u32[]{:S(2)}) collective-permute-start(bf16[448,640]{1,0:T(8,128)(2,1)} %dynamic-slice_bitcast_fusion), channel_id=1, source_target_pairs={{0,8},{4,12},{8,0},{12,4},{16,24},{20,28},{24,16},{28,20},{1,9},{5... | collective-permute-start | bytes 1720328 | tf_op jit(solution)/shard_map/ppermute | solution.py:479
  190.3 43.3 %collective-permute-start.56 = (bf16[224,640]{1,0:T(8,128)(2,1)S(1)}, bf16[224,640]{1,0:T(8,128)(2,1)S(1)}, u32[]{:S(2)}, u32[]{:S(2)}) collective-permute-start(bf16[224,640]{1,0:T(8,128)(2,1)S(1)} %dynamic-slice_bitcast_fusion.1), channel_id=1, source_target_pairs={{0,16},{4,20},{8,24},{12,28},{16,0},{20,4},{24,8},{28,12},{1,17},{... | collective-permute-start | bytes 860168 | tf_op jit(solution)/shard_map/ppermute | solution.py:479
  192.3 12.0 %collective-permute-start.35 = (bf16[256,512]{1,0:T(8,128)(2,1)}, bf16[256,512]{1,0:T(8,128)(2,1)S(1)}, u32[]{:S(2)}, u32[]{:S(2)}) collective-permute-start(bf16[256,512]{1,0:T(8,128)(2,1)} %get-tuple-element.135), channel_id=1, source_target_pairs={{8,0},{12,4},{16,8},{20,12},{24,16},{28,20},{0,24},{4,28},{9,1},{1... | collective-permute-start | bytes 786440 | tf_op jit(solution)/shard_map/ppermute | solution.py:476
  194.3 32.6 %collective-permute-start.36 = (bf16[256,512]{1,0:T(8,128)(2,1)}, bf16[256,512]{1,0:T(8,128)(2,1)S(1)}, u32[]{:S(2)}, u32[]{:S(2)}) collective-permute-start(bf16[256,512]{1,0:T(8,128)(2,1)} %get-tuple-element.134), channel_id=1, source_target_pairs={{16,0},{20,4},{24,8},{28,12},{0,16},{4,20},{8,24},{12,28},{17,1},{... | collective-permute-start | bytes 786440 | tf_op jit(solution)/shard_map/ppermute | solution.py:476
  195.6 31.3 %collective-permute-start.37 = (bf16[256,512]{1,0:T(8,128)(2,1)}, bf16[256,512]{1,0:T(8,128)(2,1)S(1)}, u32[]{:S(2)}, u32[]{:S(2)}) collective-permute-start(bf16[256,512]{1,0:T(8,128)(2,1)} %get-tuple-element.133), channel_id=1, source_target_pairs={{24,0},{28,4},{0,8},{4,12},{8,16},{12,20},{16,24},{20,28},{25,1},{... | collective-permute-start | bytes 786440 | tf_op jit(solution)/shard_map/ppermute | solution.py:476
  233.5 15.6 %collective-permute-start.38 = (bf16[640,768]{1,0:T(8,128)(2,1)}, bf16[640,768]{1,0:T(8,128)(2,1)S(1)}, u32[]{:S(2)}, u32[]{:S(2)}) collective-permute-start(bf16[640,768]{1,0:T(8,128)(2,1)} %get-tuple-element.106), channel_id=1, source_target_pairs={{0,4},{4,0},{8,12},{12,8},{16,20},{20,16},{24,28},{28,24},{1,5},{5... | collective-permute-start | bytes 2949128 | tf_op jit(solution)/shard_map/ppermute | solution.py:479
  233.7 15.2 %collective-permute-start.57 = (bf16[224,640]{1,0:T(8,128)(2,1)S(1)}, bf16[224,640]{1,0:T(8,128)(2,1)S(1)}, u32[]{:S(2)}, u32[]{:S(2)}) collective-permute-start(bf16[224,640]{1,0:T(8,128)(2,1)S(1)} %fusion.1), channel_id=1, source_target_pairs={{0,16},{4,20},{8,24},{12,28},{16,0},{20,4},{24,8},{28,12},{1,17},{... | collective-permute-start | bytes 860168 | tf_op jit(solution)/shard_map/ppermute | solution.py:479
  249.1 25.8 %collective-permute-start.58 = (bf16[448,640]{1,0:T(8,128)(2,1)S(1)}, bf16[448,640]{1,0:T(8,128)(2,1)S(1)}, u32[]{:S(2)}, u32[]{:S(2)}) collective-permute-start(bf16[448,640]{1,0:T(8,128)(2,1)S(1)} %pad_maximum_fusion.3), channel_id=1, source_target_pairs={{0,8},{4,12},{8,0},{12,4},{16,24},{20,28},{24,16},{28,20},{1,9},{5... | collective-permute-start | bytes 1720328 | tf_op jit(solution)/shard_map/ppermute | solution.py:479
  253.0 10.5 %collective-permute-start.39 = (bf16[176,768]{1,0:T(8,128)(2,1)}, bf16[176,768]{1,0:T(8,128)(2,1)S(1)}, u32[]{:S(2)}, u32[]{:S(2)}) collective-permute-start(bf16[176,768]{1,0:T(8,128)(2,1)} %get-tuple-element.109), channel_id=1, source_target_pairs={{1,0},{2,1},{3,2},{0,3},{5,4},{6,5},{7,6},{4,7},{9,8},{10,9},{11,1... | collective-permute-start | bytes 811016 | tf_op jit(solution)/shard_map/ppermute | solution.py:476
  256.1 14.2 %collective-permute-start.40 = (bf16[176,768]{1,0:T(8,128)(2,1)}, bf16[176,768]{1,0:T(8,128)(2,1)S(1)}, u32[]{:S(2)}, u32[]{:S(2)}) collective-permute-start(bf16[176,768]{1,0:T(8,128)(2,1)} %get-tuple-element.110), channel_id=1, source_target_pairs={{2,0},{3,1},{0,2},{1,3},{6,4},{7,5},{4,6},{5,7},{10,8},{11,9},{8,1... | collective-permute-start | bytes 811016 | tf_op jit(solution)/shard_map/ppermute | solution.py:476
  257.4 12.9 %collective-permute-start.41 = (bf16[176,768]{1,0:T(8,128)(2,1)}, bf16[176,768]{1,0:T(8,128)(2,1)S(1)}, u32[]{:S(2)}, u32[]{:S(2)}) collective-permute-start(bf16[176,768]{1,0:T(8,128)(2,1)} %get-tuple-element.111), channel_id=1, source_target_pairs={{3,0},{0,1},{1,2},{2,3},{7,4},{4,5},{5,6},{6,7},{11,8},{8,9},{9,10... | collective-permute-start | bytes 811016 | tf_op jit(solution)/shard_map/ppermute | solution.py:476
  273.1 7.5 %collective-permute-start.42 = (bf16[176,768]{1,0:T(8,128)(2,1)}, bf16[176,768]{1,0:T(8,128)(2,1)S(1)}, u32[]{:S(2)}, u32[]{:S(2)}) collective-permute-start(bf16[176,768]{1,0:T(8,128)(2,1)} %shard_map.286.refs_0_), channel_id=1, source_target_pairs={{0,8},{4,12},{8,0},{12,4},{16,24},{20,28},{24,16},{28,20},{1,9},{5... | collective-permute-start | bytes 811016 | tf_op jit(solution)/shard_map/ppermute | solution.py:479
  275.2 30.3 %collective-permute-start.59 = (bf16[896,640]{1,0:T(8,128)(2,1)S(1)}, bf16[896,640]{1,0:T(8,128)(2,1)S(1)}, u32[]{:S(2)}, u32[]{:S(2)}) collective-permute-start(bf16[896,640]{1,0:T(8,128)(2,1)S(1)} %pad_maximum_fusion.1.refs_1_), channel_id=1, source_target_pairs={{0,4},{4,0},{8,12},{12,8},{16,20},{20,16},{24,28},{28,24},{1,5},{5... | collective-permute-start | bytes 3440648 | tf_op jit(solution)/shard_map/ppermute | solution.py:479
  283.1 12.5 %collective-permute-start.43 = (bf16[176,768]{1,0:T(8,128)(2,1)}, bf16[176,768]{1,0:T(8,128)(2,1)S(1)}, u32[]{:S(2)}, u32[]{:S(2)}) collective-permute-start(bf16[176,768]{1,0:T(8,128)(2,1)} %shard_map.287.refs_0_), channel_id=1, source_target_pairs={{0,16},{4,20},{8,24},{12,28},{16,0},{20,4},{24,8},{28,12},{1,17},{... | collective-permute-start | bytes 811016 | tf_op jit(solution)/shard_map/ppermute | solution.py:479
  (66 other events, 461.0 us)
where the time goes:
time: 311 us
  waiting for transfers between devices  147 us (47%)
  Pallas kernels  68.5 us (22%)
  starting transfers between devices  53.3 us (17%)
  local copies, waits for them, and re-layouts  28.1 us (9%)
  other arithmetic  11.2 us (4%)
    ppermute x33, waiting for transfers between devices, from_peer(): lax.ppermute(x, axis, [((i + offset) % size, i) for i in range(size)])  101 us
    pallas_call x13, Pallas kernels, run_kernel(): return jax.tree.unflatten(out_tree, call(*flat))  68.5 us
    ppermute x27, waiting for transfers between devices, with_partner(): return lax.ppermute(x, 'ctx', [(i, i ^ bit) for i in range(ctx_size)])  45.6 us
    ppermute x33, starting transfers between devices, from_peer(): lax.ppermute(x, axis, [((i + offset) % size, i) for i in range(size)])  44.3 us
    unnamed x108, local copies, waits for them, and re-layouts  10.8 us
    ppermute x27, starting transfers between devices, with_partner(): return lax.ppermute(x, 'ctx', [(i, i ^ bit) for i in range(ctx_size)])  8.97 us
  transfers between devices with their start and end apart: 60, of which 21 were waited for; matrix products, arithmetic and copies ran while one was open for 7% of the time, Pallas kernels for 17%

commit v1 on v0

--- a/solution.py
+++ b/solution.py
@@ -29,13 +29,6 @@
     grad_inputs = factor * (weighted - normal * jnp.mean(normal * weighted, axis=-1, keepdims=True))
     grad_gain = jnp.sum((upstream * normal).reshape(-1, inputs.shape[-1]), axis=0)
     return (grad_inputs, grad_gain)
-
-
-def rope_tables(places, width):
-    half_width = width // 2
-    frequency = rope_base ** (-2.0 * jnp.arange(half_width, dtype=f32) / width)
-    angles = places.astype(f32)[:, None] * frequency[None, :]
-    return (jnp.cos(angles), jnp.sin(angles))
 
 
 def rope_apply(inputs, cosines, sine_terms):
@@ -77,6 +70,12 @@
     return lax.dot_general(a, b, (dims, ((), ())), preferred_element_type=f32)
 
 
+def scalars(place_ref):
+    ctx_place, fsdp_place, parity = place_ref[0], place_ref[1], place_ref[2]
+    first, second = place_ref[3 + 2 * ctx_place], place_ref[4 + 2 * ctx_place]
+    return (first > second).astype(jnp.int32), ctx_place, fsdp_place, parity
+
+
 def put_rows(ref, order, low, high):
     rows = low.shape[0]
     at = pl.multiple_of(order * rows, rows)
@@ -96,10 +95,71 @@
     return rope_apply(norm_apply(raw, gain), cosines, sine_terms)
 
 
+def first_kernel(ins, outs, scratch):
+    parity_ref, qw_ref, kw_ref, vw_ref = ins
+    (send_ref,) = outs
+    parity = parity_ref[0]
+    half = send_ref.shape[1]
+    rest = qw_ref.shape[1] - half
+    head_dim = kw_ref.shape[1]
+
+    @pl.when(parity == 0)
+    def _():
+        send_ref[...] = qw_ref[:, :half]
+
+    @pl.when(parity == 1)
+    def _():
+        send_ref[:, :rest] = qw_ref[:, half:]
+        send_ref[:, rest : rest + head_dim] = kw_ref[...]
+        send_ref[:, rest + head_dim :] = vw_ref[...]
+
+
+def halves_kernel(ins, outs, scratch):
+    place_ref, outw_ref, gate_ref, up_ref, down_ref = ins
+    out_ref, pair_ref, dn_ref = outs
+    parity = place_ref[2]
+    half, out_half = dn_ref.shape[0], out_ref.shape[0]
+    cols = pl.multiple_of(parity * half, 128)
+    pair_ref[:, :half] = gate_ref[:, pl.ds(cols, half)]
+    pair_ref[:, half:] = up_ref[:, pl.ds(cols, half)]
+    dn_ref[...] = down_ref[pl.ds(pl.multiple_of(parity * half, 16), half), :]
+    out_ref[...] = outw_ref[pl.ds(pl.multiple_of(parity * out_half, 16), out_half), :]
+
+
+def table_kernel(ins, outs, scratch):
+    place_ref, pos_ref, freq_ref = ins
+    cos_ref, sin_ref, last_ref, first_ref, ids_ref = outs
+    order, ctx_place, _, _ = scalars(place_ref)
+    rows = pos_ref.shape[0] // 2
+    size = ids_ref.shape[2] // rows
+    places = get_rows(pos_ref, order)
+    angles = places.astype(f32) * freq_ref[...]
+    cos_ref[...] = jnp.cos(angles)
+    sin_ref[...] = jnp.sin(angles)
+
+    def blocks(at):
+        one, two = place_ref[3 + 2 * at], place_ref[4 + 2 * at]
+        return jnp.minimum(one, two), jnp.maximum(one, two)
+
+    own = blocks(ctx_place)
+    column = lax.broadcasted_iota(jnp.int32, (rows, 1), 0)
+    line = lax.broadcasted_iota(jnp.int32, (1, rows), 1)
+    for part in range(2):
+        index = column + own[part] * rows
+        at = slice(part * rows, (part + 1) * rows)
+        last_ref[at, :] = index
+        first_ref[at, :] = index - places[at]
+    for slot in range(size):
+        base = ctx_place if slot < size // 2 else ctx_place + 1 - 2 * place_ref[2]
+        source = blocks(lax.rem(base + 2 * (slot % (size // 2)), size))
+        for part in range(2):
+            ids_ref[part, :, slot * rows : (slot + 1) * rows] = line + source[part] * rows
+
+
 def pre_kernel(ins, outs, scratch):
     place_ref, tok_ref, gains_ref, qk_gain_ref, cos_ref, sin_ref, qw_ref, kw_ref, vw_ref, mine, theirs = ins
     normed_ref, q_ref, kv_ref, qraw_ref, kraw_ref, full_ref = outs
-    order, fsdp_place, parity = place_ref[0], place_ref[1], place_ref[2]
+    order, _, fsdp_place, parity = scalars(place_ref)
     count = len(mine)
     size = count + 1
     shard, half = mine[0].shape
@@ -141,7 +201,7 @@
     (place_ref, tok_ref, q_ref, mine, theirs, last_ref, first_ref, ids_ref,
      outw_ref, outp, outt, gains_ref) = ins
     att_ref, lse_ref, kv_ref, outfull_ref, projected_ref, hidden_ref, feed_ref = outs
-    order, fsdp_place, parity = place_ref[0], place_ref[1], place_ref[2]
+    order, _, fsdp_place, parity = scalars(place_ref)
     chips = len(mine)
     rows = mine[0].shape[0] // 2
     head_dim = mine[0].shape[1] // 2
@@ -192,12 +252,22 @@
     return grad, grad_gain[None, :]
 
 
+def split_halves(ref, parity, size, mine_ref, theirs_ref):
+    half = size // 2
+    for k in range(ref.shape[0] // size):
+        mine = pl.multiple_of(k * size + parity * half, 16)
+        theirs = pl.multiple_of(k * size + (1 - parity) * half, 16)
+        mine_ref[k * half : (k + 1) * half, :] = ref[pl.ds(mine, half), :]
+        theirs_ref[k * half : (k + 1) * half, :] = ref[pl.ds(theirs, half), :].astype(bf16)
+
+
 def feed_kernel(ins, outs, scratch):
     (place_ref, cot_ref, feed_ref, hidden_ref, projected_ref, outfull_ref, gains_ref,
-     gate_ref, up_ref, down_ref, pair_refs, down_refs) = ins
-    out_ref, gfeed_ref, ghidden_ref, gproj_ref, gatt_ref, mix_ref, pre_ref, post_ref = outs
-    act_ref, slope_ref = scratch
-    order = place_ref[0]
+     att_ref, gate_ref, up_ref, down_ref, pair_refs, down_refs) = ins
+    (out_ref, gfeed_ref, ghidden_ref, gatt_ref, mix_ref, pre_ref, post_ref,
+     omine_ref, otheirs_ref) = outs
+    act_ref, slope_ref, ograd_ref = scratch
+    order, _, _, parity = scalars(place_ref)
     rows = feed_ref.shape[0] // 2
     half = pair_refs[0].shape[1] // 2
     pieces = [(lambda: gate_ref[...], lambda: up_ref[...], lambda: down_ref[...], gate_ref.shape[1])]
@@ -241,8 +311,11 @@
     ghidden_ref[...] = grad_hidden
     grad_proj, mix_ref[...] = norm_back_rows(projected_ref[...], gains_ref[1:2, :], grad_hidden)
     grad_proj = grad_proj.astype(bf16)
-    gproj_ref[...] = grad_proj
     gatt_ref[...] = dot(grad_proj, outfull_ref[...], ((1,), (1,))).astype(bf16)
+    ograd_ref[...] = dot(att_ref[...], grad_proj, ((0,), (0,)))
+    units = gate_ref.shape[1]
+    shard = ograd_ref.shape[0] // (act_ref.shape[1] // units)
+    split_halves(ograd_ref, parity, shard, omine_ref, otheirs_ref)
 
 
 def attend_back_kernel(ins, outs, scratch):
@@ -296,13 +369,11 @@
 
 
 def weight_kernel(ins, outs, scratch):
-    place_ref, feed_refs, grad_refs, gate_ref, up_ref, down_ref, att_ref, gproj_ref = ins
+    place_ref, feed_refs, grad_refs, gate_ref, up_ref, down_ref = ins
     mine_ref, theirs_ref = outs
     (grad_ref,) = scratch
     parity = place_ref[2]
-    count = len(feed_refs) - 1
     units = down_ref.shape[0]
-    half = units // 2
     feed_in = jnp.concatenate([ref[...] for ref in feed_refs], axis=0)
     grad_feed = jnp.concatenate([ref[...] for ref in grad_refs], axis=0)
     gate_vals = dot(feed_in, gate_ref[...], ((1,), (0,)))
@@ -315,17 +386,7 @@
     grad_ref[0:units, :] = dot(grad_gate, feed_in, ((0,), (0,)))
     grad_ref[units : 2 * units, :] = dot(grad_up, feed_in, ((0,), (0,)))
     grad_ref[2 * units : 3 * units, :] = dot(mixed, grad_feed, ((0,), (0,)))
-    grad_ref[3 * units :, :] = dot(att_ref[...], gproj_ref[...], ((0,), (0,)))
-    shard = att_ref.shape[1] // (count + 1)
-    groups = [(k * units, k * half, half) for k in range(3)]
-    groups += [
-        (3 * units + k * shard, 3 * half + k * (shard // 2), shard // 2) for k in range(count + 1)
-    ]
-    for start, to, size in groups:
-        mine = pl.multiple_of(start + parity * size, 16)
-        theirs = pl.multiple_of(start + (1 - parity) * size, 16)
-        mine_ref[to : to + size, :] = grad_ref[pl.ds(mine, size), :]
-        theirs_ref[to : to + size, :] = grad_ref[pl.ds(theirs, size), :].astype(bf16)
+    split_halves(grad_ref, parity, units, mine_ref, theirs_ref)
 
 
 def put_gains(ref, at, value):
@@ -340,7 +401,7 @@
      normed_ref, gq_ref, full_ref, ghidden_ref, qgain_ref, mix_ref, pre_ref, post_ref) = ins
     tgrad_ref, mine_ref, theirs_ref, terms_ref = outs
     back_ref, grad_ref, sums_ref = scratch
-    order, parity = place_ref[0], place_ref[2]
+    order, _, _, parity = scalars(place_ref)
     head_dim = kraw_ref.shape[1]
     query_width = gq_ref.shape[1]
     rows = normed_ref.shape[0] // 2
@@ -398,9 +459,10 @@
 
 def late_last_kernel(ins, outs, scratch):
     place_ref, mine_ref, other_ref = ins
-    q_ref, k_ref, v_ref, gains_ref = outs
+    q_ref, k_ref, v_ref, wide_ref, narrow_ref = outs
     (full_ref,) = scratch
     parity = place_ref[2]
+    fsdp_place = place_ref[1]
     rows, half = q_ref.shape[0], mine_ref.shape[1]
     left = pl.multiple_of(parity * half, 128)
     right = pl.multiple_of((1 - parity) * half, 128)
@@ -411,20 +473,37 @@
     k_ref[...] = full_ref[:, width : width + head_dim]
     v_ref[...] = full_ref[:, width + head_dim :]
     both = mine_ref[rows:, :].astype(f32) + other_ref[rows:, :].astype(f32)
-    gains_ref[...] = both[:8] + both[8:]
+    sums = both[:8] + both[8:]
+    for ref in (wide_ref, narrow_ref):
+        cols = ref.shape[1]
+        ref[...] = pltpu.roll(sums, lax.rem(half - fsdp_place * cols, half), 1)[:, :cols]
+
+
+def out_pack_kernel(ins, outs, scratch):
+    place_ref, mine_ref, other_ref = ins
+    fsdp_place = place_ref[1]
+    size = len(outs)
+    shard = outs[0].shape[0]
+    for k in range(size):
+        at = pl.multiple_of(lax.rem(fsdp_place + size - k, size) * shard, 16)
+        chunk = mine_ref[pl.ds(at, shard), :] + other_ref[pl.ds(at, shard), :].astype(f32)
+        outs[k][...] = chunk.astype(bf16)
 
 
 def early_pack_kernel(ins, outs, scratch):
-    place_ref, mine_ref, other_ref = ins
-    feed_ref, chunks = outs
-    fsdp_place = place_ref[1]
-    size = len(chunks)
-    base, shard = feed_ref.shape[0], chunks[0].shape[0]
-    feed_ref[...] = (mine_ref[:base, :] + other_ref[:base, :].astype(f32)).astype(bf16)
-    for k in range(size):
-        at = pl.multiple_of(base + lax.rem(fsdp_place + size - k, size) * shard, 16)
-        chunk = mine_ref[pl.ds(at, shard), :] + other_ref[pl.ds(at, shard), :].astype(f32)
-        chunks[k][...] = chunk.astype(bf16)
+    place_ref, mine_ref, other_ref, parts = ins
+    keep_ref, send_ref = outs
+    (all_ref,) = scratch
+    base = mine_ref.shape[0]
+    all_ref[:base, :] = (mine_ref[...] + other_ref[...].astype(f32)).astype(bf16)
+    total = parts[0][...].astype(f32)
+    for ref in parts[1:]:
+        total = total + ref[...].astype(f32)
+    all_ref[base:, :] = total.astype(bf16)
+    rows = keep_ref.shape[0]
+    side = lax.rem(lax.div(place_ref[0], 2), 2)
+    keep_ref[...] = all_ref[pl.ds(pl.multiple_of(side * rows, 16), rows), :]
+    send_ref[...] = all_ref[pl.ds(pl.multiple_of((1 - side) * rows, 16), rows), :]
 
 
 def early_last_kernel(ins, outs, scratch):
@@ -490,23 +569,26 @@
     def pick(x, at, axis=0):
         return lax.dynamic_index_in_dim(x, at, axis, keepdims=False)
 
-    def sum_chips(half, ctx_place):
-        _, width = half.shape
+    def sum_chips(keep, send, ctx_place):
+        width = keep.shape[1]
         steps = []
         bit = 2
         while bit < ctx_size:
             side = (ctx_place // bit) % 2
-            half = half.reshape(2, -1, width)
-            sent = with_partner(pick(half, 1 - side), bit)
-            half = (pick(half, side).astype(f32) + sent.astype(f32)).astype(bf16)
+            sent = with_partner(send, bit)
+            total = (keep.astype(f32) + sent.astype(f32)).astype(bf16)
+            if 2 * bit < ctx_size:
+                parts = total.reshape(2, -1, width)
+                ahead = (ctx_place // (2 * bit)) % 2
+                keep, send = pick(parts, ahead), pick(parts, 1 - ahead)
             steps.append((bit, side))
             bit *= 2
         for bit, side in reversed(steps):
-            other = with_partner(half, bit)
-            first = jnp.where(side == 0, half, other)
-            second = jnp.where(side == 0, other, half)
-            half = jnp.concatenate([first, second], axis=0)
-        return half
+            other = with_partner(total, bit)
+            first = jnp.where(side == 0, total, other)
+            second = jnp.where(side == 0, other, total)
+            total = jnp.concatenate([first, second], axis=0)
+        return total
 
     def body(
         tokens,
@@ -543,19 +625,21 @@
         fsdp_place = lax.axis_index("fsdp")
         parity = ctx_place % 2
 
-        proj_send = jnp.where(
-            parity == 0,
-            query_weight[:, :proj_half],
-            jnp.concatenate([query_weight[:, proj_half:], key_weight, value_weight], axis=1),
+        place = jnp.concatenate(
+            [jnp.stack([ctx_place, fsdp_place, parity]).astype(jnp.int32), block_order]
+        )
+        tok, cot = tokens[0], cotangent[0]
+        rows_width = (row_count, width)
+        (proj_send,) = run_kernel(
+            first_kernel,
+            (parity.astype(jnp.int32).reshape(1), query_weight, key_weight, value_weight),
+            (((shard_rows, proj_half), bf16),),
         )
         proj_mine = others_fsdp(proj_send)
-
-        wide = (input_gain, mixer_gain, prefeed_gain, postfeed_gain)
-        narrow = (query_gain, key_gain)
         gain_cols, head_cols = input_gain.shape[0], query_gain.shape[0]
         gains_own = jnp.stack(
-            [g.astype(f32) for g in wide]
-            + [jnp.pad(g.astype(f32), (0, gain_cols - head_cols)) for g in narrow]
+            [g.astype(f32) for g in (input_gain, mixer_gain, prefeed_gain, postfeed_gain)]
+            + [jnp.pad(g.astype(f32), (0, gain_cols - head_cols)) for g in (query_gain, key_gain)]
         )
         gain_parts = [gains_own] + others_fsdp(gains_own)
         gain_full = jnp.zeros((fsdp_size,) + gains_own.shape, f32)
@@ -567,41 +651,32 @@
         gains = gain_full[:4].reshape(4, width)
         qk_gains = gain_full[4:, :, :head_cols].reshape(2, head_dim)
 
-        own_blocks = lax.dynamic_slice_in_dim(block_order, 2 * ctx_place, 2)
-        flipped = (own_blocks[0] > own_blocks[1]).astype(jnp.int32)
-        place = jnp.stack([flipped, fsdp_place, parity]).astype(jnp.int32)
-        places = jnp.where(flipped == 0, positions[0], jnp.roll(positions[0], block_rows))
-        offsets = jnp.arange(block_rows, dtype=jnp.int32)
-        low_blocks = jnp.minimum(block_order[0::2], block_order[1::2])
-        high_blocks = jnp.maximum(block_order[0::2], block_order[1::2])
-        sorted_blocks = jnp.stack([low_blocks, high_blocks])
-        query_blocks = lax.dynamic_slice_in_dim(sorted_blocks, ctx_place, 1, axis=1)
-        query_index = (query_blocks * block_rows + offsets[None, :]).reshape(-1)
-        query_last = query_index[:, None]
-        query_first = (query_index - places)[:, None]
-        sources = jnp.concatenate(
-            [
-                (ctx_place + 2 * jnp.arange(chips)) % ctx_size,
-                ((ctx_place ^ 1) + 2 * jnp.arange(chips)) % ctx_size,
-            ]
-        )
-        key_blocks = jnp.take(sorted_blocks, sources, axis=1)
-        key_ids = (key_blocks[:, :, None] * block_rows + offsets).reshape(2, 1, -1)
-        cosines, sine_terms = rope_tables(places, head_dim)
-        tok, cot = tokens[0], cotangent[0]
-        rows_width = (row_count, width)
+        frequency = rope_base ** (-2.0 * jnp.arange(head_dim // 2, dtype=f32) / head_dim)
+        cosines, sine_terms, query_last, query_first, key_ids = run_kernel(
+            table_kernel,
+            (place, positions[0][:, None], frequency[None]),
+            (
+                ((row_count, head_dim // 2), f32),
+                ((row_count, head_dim // 2), f32),
+                ((row_count, 1), jnp.int32),
+                ((row_count, 1), jnp.int32),
+                ((2, 1, ctx_size * block_rows), jnp.int32),
+            ),
+        )
         proj_ready = list(
-            lax.optimization_barrier((*proj_mine, gains, qk_gains, place, cosines, sine_terms))
+            lax.optimization_barrier((*proj_mine, gains, qk_gains, cosines, sine_terms))
         )[: fsdp_size - 1]
         proj_theirs = with_partners(proj_ready)
 
-        gate_half = lax.dynamic_slice_in_dim(gate_weight, parity * half_rows, half_rows, axis=1)
-        up_half = lax.dynamic_slice_in_dim(up_weight, parity * half_rows, half_rows, axis=1)
-        down_half = lax.dynamic_slice_in_dim(down_weight, parity * half_rows, half_rows, axis=0)
-        out_half = lax.dynamic_slice_in_dim(
-            output_weight, parity * (out_rows // 2), out_rows // 2, axis=0
-        )
-        pair_half = jnp.concatenate([gate_half, up_half], axis=1)
+        out_half, pair_half, down_half = run_kernel(
+            halves_kernel,
+            (place, output_weight, gate_weight, up_weight, down_weight),
+            (
+                ((out_rows // 2, width), bf16),
+                ((width, 2 * half_rows), bf16),
+                ((half_rows, width), bf16),
+            ),
+        )
         pair_half = after(pair_half, *proj_mine)
         out_mine = others_fsdp(out_half)
         pair_mine = others_fsdp(pair_half)
@@ -620,8 +695,7 @@
             ),
         )
         kv_mine = [own_pair] + [from_peer(own_pair, "ctx", 2 * k) for k in range(1, chips)]
-        kv_ready = after(own_pair, query_last, query_first, key_ids)
-        kv_theirs = [with_partner(kv_ready)] + with_partners(kv_mine[1:])
+        kv_theirs = [with_partner(own_pair)] + with_partners(kv_mine[1:])
         down_mine = others_fsdp(after(down_half, own_pair))
         out_theirs = with_partners(out_mine)
         pair_ready = list(lax.optimization_barrier((*pair_mine, *kv_mine[1:])))[: fsdp_size - 1]
@@ -642,23 +716,27 @@
             ),
         )
         feed_all = [feed_in] + others_fsdp(feed_in)
-        output, grad_feed, grad_hidden, grad_proj, grad_attended, gmix, gpre, gpost = run_kernel(
+        (output, grad_feed, grad_hidden, grad_attended, gmix, gpre, gpost,
+         out_own, out_other) = run_kernel(
             feed_kernel,
             (place, cot, feed_in, hidden, projected, output_full, gains,
-             gate_weight, up_weight, down_weight,
+             attended, gate_weight, up_weight, down_weight,
              pair_ready + pair_theirs, down_mine + down_theirs),
             (
                 (rows_width, f32),
                 (rows_width, bf16),
                 (rows_width, f32),
-                (rows_width, bf16),
                 ((row_count, query_width), bf16),
                 ((1, width), f32),
                 ((1, width), f32),
                 ((1, width), f32),
-            ),
-            (((row_count, fsdp_size * hidden_rows), f32),) * 2,
-        )
+                ((fsdp_size * out_rows // 2, width), f32),
+                ((fsdp_size * out_rows // 2, width), bf16),
+            ),
+            (((row_count, fsdp_size * hidden_rows), f32),) * 2
+            + (((fsdp_size * out_rows, width), f32),),
+        )
+        out_other = with_partner(out_other)
         grad_all = [grad_feed] + others_fsdp(grad_feed)
         query_back, pairs_mine, pairs_theirs, gqgain = run_kernel(
             attend_back_kernel,
@@ -678,28 +756,34 @@
         chip_own = chip_part[0]
         back_parts = [from_peer(chip_send[k - 1], "ctx", 2 * k) for k in range(1, chips)]
 
-        early_rows = 3 * half_rows + fsdp_size * out_rows // 2
+        out_chunks = run_kernel(
+            out_pack_kernel,
+            (place, out_own, out_other),
+            [((out_rows // 2, width), bf16)] * fsdp_size,
+        )
+        out_parts = [out_chunks[0]] + [
+            from_peer(out_chunks[k], "fsdp", k) for k in range(1, fsdp_size)
+        ]
+
+        feed_rows = 3 * half_rows
         early_mine, early_theirs = run_kernel(
             weight_kernel,
-            (place, feed_all, grad_all, gate_weight, up_weight, down_weight, attended, grad_proj),
-            (
-                ((early_rows, width), f32),
-                ((early_rows, width), bf16),
-            ),
-            (((2 * early_rows, width), f32),),
-        )
-        early_feed, out_chunks = run_kernel(
+            (place, [after(feed_in, out_chunks[0])] + feed_all[1:], grad_all,
+             gate_weight, up_weight, down_weight),
+            (
+                ((feed_rows, width), f32),
+                ((feed_rows, width), bf16),
+            ),
+            (((2 * feed_rows, width), f32),),
+        )
+        early_rows = feed_rows + out_rows // 2
+        keep, send = run_kernel(
             early_pack_kernel,
-            (place, early_mine, with_partner(early_theirs)),
-            (
-                ((3 * half_rows, width), bf16),
-                [((out_rows // 2, width), bf16)] * fsdp_size,
-            ),
-        )
-        out_sum = out_chunks[0].astype(f32)
-        for k in range(1, fsdp_size):
-            out_sum = out_sum + from_peer(out_chunks[k], "fsdp", k).astype(f32)
-        early = sum_chips(jnp.concatenate([early_feed, out_sum.astype(bf16)], axis=0), ctx_place)
+            (place, early_mine, with_partner(early_theirs), out_parts),
+            (((early_rows // 2, width), bf16),) * 2,
+            (((early_rows, width), bf16),),
+        )
+        early = sum_chips(keep, send, ctx_place)
         gate_grad, up_grad, down_grad, out_grad = run_kernel(
             early_last_kernel,
             (place, early, with_partner(early)),
@@ -743,19 +827,18 @@
             other = with_partner(late, bit)
             (late,) = run_kernel(late_sum_kernel, [late, other], [late_shape])
             bit *= 2
-        query_grad, key_grad, value_grad, gain_sums = run_kernel(
+        query_grad, key_grad, value_grad, wide_sums, narrow_sums = run_kernel(
             late_last_kernel,
             (place, late, with_partner(late)),
             (
                 ((shard_rows, query_width), f32),
                 ((shard_rows, head_dim), f32),
                 ((shard_rows, head_dim), f32),
-                ((8, proj_half), f32),
+                ((8, gain_cols), f32),
+                ((8, head_cols), f32),
             ),
             (((shard_rows, proj_width), f32),),
         )
-        wide_sums = lax.dynamic_slice(gain_sums, (0, fsdp_place * gain_cols), (4, gain_cols))
-        head_sums = lax.dynamic_slice(gain_sums, (4, fsdp_place * head_cols), (2, head_cols))
         return (
             output[None],
             tokens_grad[None],
@@ -767,8 +850,8 @@
             up_grad,
             down_grad,
             wide_sums[0],
-            head_sums[0],
-            head_sums[1],
+            narrow_sums[4],
+            narrow_sums[5],
             wide_sums[1],
             wide_sums[2],
             wide_sums[3],

time: 311 us -> 314 us (level)
  starting transfers between devices: 53.3 us -> 66.6 us
  Pallas kernels: 68.5 us -> 77.2 us
  local copies, waits for them, and re-layouts: 28.1 us -> 20.9 us
  other arithmetic: 11.2 us -> 4.85 us
  waiting for transfers between devices: 147 us -> 142 us
    ppermute x27 -> x28, starting transfers between devices: 8.97 us -> 20.8 us  [with_partner(): return lax.ppermute(x, 'ctx', [(i, i ^ bit) for i in range(ctx_size)])]
    pallas_call x13 -> x17, Pallas kernels: 68.5 us -> 77.2 us  [run_kernel(): return jax.tree.unflatten(out_tree, call(*flat))]
    ppermute x27 -> x28, waiting for transfers between devices: 45.6 us -> 42 us  [with_partner(): return lax.ppermute(x, 'ctx', [(i, i ^ bit) for i in range(ctx_size)])]
    unnamed x108 -> x122, local copies, waits for them, and re-layouts: 10.8 us -> 9.96 us
  transfers between devices with their start and end apart: 60 -> 61, of which waited for: 21 -> 23; matrix products, arithmetic and copies ran while one was open for 7% -> 5% of each run, Pallas kernels for 17% -> 15%
where the time goes in v1:
time: 314 us; the launch traced here: 313 us
  waiting for transfers between devices  142 us (45%)
  Pallas kernels  77.2 us (25%)
  starting transfers between devices  66.6 us (21%)
  local copies, waits for them, and re-layouts  20.9 us (7%)
  other arithmetic  4.85 us (2%)
    ppermute x33, waiting for transfers between devices, from_peer(): lax.ppermute(x, axis, [((i + offset) % size, i) for i in range(size)])  100 us
    pallas_call x17, Pallas kernels, run_kernel(): return jax.tree.unflatten(out_tree, call(*flat))  77.2 us
    ppermute x33, starting transfers between devices, from_peer(): lax.ppermute(x, axis, [((i + offset) % size, i) for i in range(size)])  45.8 us
    ppermute x28, waiting for transfers between devices, with_partner(): return lax.ppermute(x, 'ctx', [(i, i ^ bit) for i in range(ctx_size)])  42 us
    ppermute x28, starting transfers between devices, with_partner(): return lax.ppermute(x, 'ctx', [(i, i ^ bit) for i in range(ctx_size)])  20.8 us
    unnamed x122, local copies, waits for them, and re-layouts  9.96 us
  transfers between devices with their start and end apart: 61, of which 23 were waited for; matrix products, arithmetic and copies ran while one was open for 5% of the time, Pallas kernels for 15%

profile of v1, /device:TPU:0, one launch (start us, length us, event | category | flops | bytes accessed | tf_op | source)
XLA Modules:
  0.0 313.2 jit_solution(15292220974674754298)
XLA Ops:
  2.4 3.0 collective-permute-start.5
  12.4 2.0 collective-permute-start
  15.8 2.7 shard_map.283
  22.4 2.2 shard_map.280
  29.3 4.1 %collective-permute-done.17.refs_16_ = bf16[128,640]{1,0:T(8,128)(2,1)S(1)} collective-permute-done((bf16[128,640]{1,0:T(8,128)(2,1)}, bf16[128,640]{1,0:T(8,128)(2,1)S(1)}, u32[]{:S(2)}, u32[]{:S(2)}) %collective-permute-start.17) | collective-permute-done | bytes 163872 | tf_op jit(solution)/shard_map/ppermute | solution.py:555
  34.5 3.9 %collective-permute-start.24 = (bf16[640,512]{1,0:T(8,128)(2,1)}, bf16[640,512]{1,0:T(8,128)(2,1)S(1)}, u32[]{:S(2)}, u32[]{:S(2)}) collective-permute-start(bf16[640,512]{1,0:T(8,128)(2,1)} %get-tuple-element.100), channel_id=1, source_target_pairs={{3,0},{0,1},{1,2},{2,3},{7,4},{4,5},{5,6},{6,7},{11,8},{8,9},{9,10... | collective-permute-start | bytes 1966088 | tf_op jit(solution)/shard_map/ppermute | solution.py:555
  40.1 4.3 %shard_map.282 = (bf16[256,640]{1,0:T(8,128)(2,1)}, bf16[256,1024]{1,0:T(8,128)(2,1)}, bf16[256,512]{1,0:T(8,128)(2,1)}, f32[256,1024]{1,0:T(8,128)}, f32[256,256]{1,0:T(8,128)}, /*index=5*/bf16[640,1536]{1,0:T(8,128)(2,1)}) custom-call(s32[19]{0:T(128)} %pad_add_fusion.refs_0_, f32[256,640]{1,0:T(8,128)} %bitcast.35, ...), custom_call_target="tpu_custom_call" | custom-call | tf_op jit(solution)/shard_map/pallas_call | solution.py:547
  46.7 2.6 collective-permute-start.10
  49.3 6.6 %collective-permute-done.11.refs_6_ = bf16[256,512]{1,0:T(8,128)(2,1)S(1)} collective-permute-done((bf16[256,512]{1,0:T(8,128)(2,1)}, bf16[256,512]{1,0:T(8,128)(2,1)S(1)}, u32[]{:S(2)}, u32[]{:S(2)}) %collective-permute-start.11) | collective-permute-done | bytes 262176 | tf_op jit(solution)/shard_map/ppermute | solution.py:555
  57.2 9.4 %collective-permute-done.10.refs_5_ = bf16[256,512]{1,0:T(8,128)(2,1)S(1)} collective-permute-done((bf16[256,512]{1,0:T(8,128)(2,1)}, bf16[256,512]{1,0:T(8,128)(2,1)S(1)}, u32[]{:S(2)}, u32[]{:S(2)}) %collective-permute-start.10) | collective-permute-done | bytes 262176 | tf_op jit(solution)/shard_map/ppermute | solution.py:555
  66.7 3.7 %collective-permute-done.9.refs_4_ = bf16[256,512]{1,0:T(8,128)(2,1)S(1)} collective-permute-done((bf16[256,512]{1,0:T(8,128)(2,1)}, bf16[256,512]{1,0:T(8,128)(2,1)S(1)}, u32[]{:S(2)}, u32[]{:S(2)}) %collective-permute-start.9) | collective-permute-done | bytes 262176 | tf_op jit(solution)/shard_map/ppermute | solution.py:555
  72.5 5.6 %collective-permute-done.30.refs_19_ = bf16[256,640]{1,0:T(8,128)(2,1)S(1)} collective-permute-done((bf16[256,640]{1,0:T(8,128)(2,1)S(1)}, bf16[256,640]{1,0:T(8,128)(2,1)S(1)}, u32[]{:S(2)}, u32[]{:S(2)}) %collective-permute-start.30) | collective-permute-done | bytes 327712 | tf_op jit(solution)/shard_map/ppermute | solution.py:555
  78.1 5.2 %collective-permute-done.29.refs_18_ = bf16[256,640]{1,0:T(8,128)(2,1)S(1)} collective-permute-done((bf16[256,640]{1,0:T(8,128)(2,1)S(1)}, bf16[256,640]{1,0:T(8,128)(2,1)S(1)}, u32[]{:S(2)}, u32[]{:S(2)}) %collective-permute-start.29) | collective-permute-done | bytes 327712 | tf_op jit(solution)/shard_map/ppermute | solution.py:555
  84.3 3.3 %collective-permute-done.13.refs_8_ = bf16[256,512]{1,0:T(8,128)(2,1)S(1)} collective-permute-done((bf16[256,512]{1,0:T(8,128)(2,1)S(1)}, bf16[256,512]{1,0:T(8,128)(2,1)S(1)}, u32[]{:S(2)}, u32[]{:S(2)}) %collective-permute-start.13) | collective-permute-done | bytes 262176 | tf_op jit(solution)/shard_map/ppermute | solution.py:558
  88.3 7.4 %shard_map.284 = (bf16[256,1024]{1,0:T(8,128)(2,1)}, f32[2,512,1]{2,1,0:T(8,128)}, bf16[2,1024,512]{2,1,0:T(8,128)(2,1)}, bf16[1024,640]{1,0:T(8,128)(2,1)}, f32...) custom-call(s32[19]{0:T(128)} %pad_add_fusion.refs_0_, f32[256,640]{1,0:T(8,128)} %bitcast.36, ...), custom_call_target="tpu_custom_call" | custom-call | tf_op jit(solution)/shard_map/pallas_call | solution.py:547
  97.2 14.6 %shard_map.285 = (f32[256,640]{1,0:T(8,128)}, bf16[256,640]{1,0:T(8,128)(2,1)}, f32[256,640]{1,0:T(8,128)}, bf16[256,1024]{1,0:T(8,128)(2,1)}, f32[1,640]{1,0:T(...) custom-call(s32[19]{0:T(128)} %pad_add_fusion.refs_0_, ...), custom_call_target="tpu_custom_call" | custom-call | tf_op jit(solution)/shard_map/pallas_call | solution.py:547
  112.0 2.0 collective-permute-start.48
  117.2 6.4 %collective-permute-done.48.refs_4_ = bf16[256,640]{1,0:T(8,128)(2,1)S(1)} collective-permute-done((bf16[256,640]{1,0:T(8,128)(2,1)S(1)}, bf16[256,640]{1,0:T(8,128)(2,1)S(1)}, u32[]{:S(2)}, u32[]{:S(2)}) %collective-permute-start.48) | collective-permute-done | bytes 327712 | tf_op jit(solution)/shard_map/ppermute | solution.py:555
  124.2 1.8 collective-permute-start.49
  126.0 2.4 shard_map.293
  128.4 2.2 collective-permute-done.47.refs_3_
  130.6 7.0 %collective-permute-done.51.refs_8_ = bf16[256,640]{1,0:T(8,128)(2,1)S(1)} collective-permute-done((bf16[256,640]{1,0:T(8,128)(2,1)}, bf16[256,640]{1,0:T(8,128)(2,1)S(1)}, u32[]{:S(2)}, u32[]{:S(2)}) %collective-permute-start.51) | collective-permute-done | bytes 327712 | tf_op jit(solution)/shard_map/ppermute | solution.py:555
  137.6 6.3 %collective-permute-done.50.refs_7_ = bf16[256,640]{1,0:T(8,128)(2,1)S(1)} collective-permute-done((bf16[256,640]{1,0:T(8,128)(2,1)}, bf16[256,640]{1,0:T(8,128)(2,1)S(1)}, u32[]{:S(2)}, u32[]{:S(2)}) %collective-permute-start.50) | collective-permute-done | bytes 327712 | tf_op jit(solution)/shard_map/ppermute | solution.py:555
  145.4 9.9 %shard_map.294 = (f32[768,640]{1,0:T(8,128)}, bf16[768,640]{1,0:T(8,128)(2,1)}) custom-call(s32[19]{0:T(128)} %pad_add_fusion.refs_0_, bf16[256,640]{1,0:T(8,128)(2,1)} %get-tuple-element.136.refs_2_.refs_1_, bf16[256,640]{1,0:T(8,128)(2,1)} %copy-done.22, bf16[256,640]{1,0:T(8,128)(2,1)} %copy-done.21, bf16[256,640]{1,0:T(8,128)(2,1)} %copy-done.20, ...), custom_call_target="tpu_custom_call" | custom-call | tf_op jit(solution)/shard_map/pallas_call | solution.py:547
  155.4 8.0 %shard_map.286 = (bf16[256,1024]{1,0:T(8,128)(2,1)}, f32[4,256,512]{2,1,0:T(8,128)}, bf16[4,256,512]{2,1,0:T(8,128)(2,1)}, f32[1,256]{1,0:T(1,128)}) custom-call(bf16[256,1024]{1,0:T(8,128)(2,1)} %get-tuple-element.88.refs_2_.refs_0_, bf16[2,1024,512]{2,1,0:T(8,128)(2,1)} %get-tuple-element.107.refs_1_, bf16[256,1024]{1,0:T(8,128)(2,1)} %get-tuple-element.108.refs_2_, ...), custom_call_target="tpu_custom_call" | custom-call | tf_op jit(solution)/shard_map/pallas_call | solution.py:547
  166.6 4.3 %collective-permute-done.53.refs_4_ = bf16[128,640]{1,0:T(8,128)(2,1)S(1)} collective-permute-done((bf16[128,640]{1,0:T(8,128)(2,1)S(1)}, bf16[128,640]{1,0:T(8,128)(2,1)S(1)}, u32[]{:S(2)}, u32[]{:S(2)}) %collective-permute-start.53) | collective-permute-done | bytes 163872 | tf_op jit(solution)/shard_map/ppermute | solution.py:555
  170.9 3.6 %collective-permute-done.54.refs_5_ = bf16[128,640]{1,0:T(8,128)(2,1)S(1)} collective-permute-done((bf16[128,640]{1,0:T(8,128)(2,1)S(1)}, bf16[128,640]{1,0:T(8,128)(2,1)S(1)}, u32[]{:S(2)}, u32[]{:S(2)}) %collective-permute-start.54) | collective-permute-done | bytes 163872 | tf_op jit(solution)/shard_map/ppermute | solution.py:555
  175.6 3.5 %shard_map.295 = (bf16[448,640]{1,0:T(8,128)(2,1)}, bf16[448,640]{1,0:T(8,128)(2,1)}) custom-call(s32[19]{0:T(128)} %pad_add_fusion.refs_0_, f32[768,640]{1,0:T(8,128)} %get-tuple-element.138.refs_1_, bf16[768,640]{1,0:T(8,128)(2,1)} %copy-done.5, bf16[128,640]{1,0:T(8,128)(2,1)} %get-tuple-element.135.refs_3_, bf16[128,640]{1,0:T(8,128)(2,1)} %copy-done.52, ...), custom_call_target="tpu_custom_call" | custom-call | tf_op jit(solution)/shard_map/pallas_call | solution.py:547
  179.0 3.9 %collective-permute-start.56 = (bf16[448,640]{1,0:T(8,128)(2,1)}, bf16[448,640]{1,0:T(8,128)(2,1)S(1)}, u32[]{:S(2)}, u32[]{:S(2)}) collective-permute-start(bf16[448,640]{1,0:T(8,128)(2,1)} %get-tuple-element.144), channel_id=1, source_target_pairs={{0,8},{4,12},{8,0},{12,4},{16,24},{20,28},{24,16},{28,20},{1,9},{5... | collective-permute-start | bytes 1720328 | tf_op jit(solution)/shard_map/ppermute | solution.py:558
  183.9 2.3 fusion.1
  186.2 8.6 %collective-permute-done.56 = bf16[448,640]{1,0:T(8,128)(2,1)S(1)} collective-permute-done((bf16[448,640]{1,0:T(8,128)(2,1)}, bf16[448,640]{1,0:T(8,128)(2,1)S(1)}, u32[]{:S(2)}, u32[]{:S(2)}) %collective-permute-start.56) | collective-permute-done | bytes 573472 | tf_op jit(solution)/shard_map/ppermute | solution.py:558
  195.0 3.3 %collective-permute-start.57 = (bf16[224,640]{1,0:T(8,128)(2,1)S(1)}, bf16[224,640]{1,0:T(8,128)(2,1)S(1)}, u32[]{:S(2)}, u32[]{:S(2)}) collective-permute-start(bf16[224,640]{1,0:T(8,128)(2,1)S(1)} %dynamic-slice_bitcast_fusion), channel_id=1, source_target_pairs={{0,16},{4,20},{8,24},{12,28},{16,0},{20,4},{24,8},{28,12},{1,17},{... | collective-permute-start | bytes 860168 | tf_op jit(solution)/shard_map/ppermute | solution.py:558
  201.0 2.3 collective-permute-start.35
  204.2 8.5 %collective-permute-done.37.refs_5_ = bf16[256,512]{1,0:T(8,128)(2,1)S(1)} collective-permute-done((bf16[256,512]{1,0:T(8,128)(2,1)}, bf16[256,512]{1,0:T(8,128)(2,1)S(1)}, u32[]{:S(2)}, u32[]{:S(2)}) %collective-permute-start.37) | collective-permute-done | bytes 262176 | tf_op jit(solution)/shard_map/ppermute | solution.py:555
  212.8 14.7 %collective-permute-done.36.refs_4_ = bf16[256,512]{1,0:T(8,128)(2,1)} collective-permute-done((bf16[256,512]{1,0:T(8,128)(2,1)}, bf16[256,512]{1,0:T(8,128)(2,1)}, u32[]{:S(2)}, u32[]{:S(2)}) %collective-permute-start.36) | collective-permute-done | bytes 262176 | tf_op jit(solution)/shard_map/ppermute | solution.py:555
  227.5 5.8 %shard_map.287 = (f32[256,640]{1,0:T(8,128)}, f32[640,768]{1,0:T(8,128)}, bf16[640,768]{1,0:T(8,128)(2,1)}, bf16[16,768]{1,0:T(8,128)(2,1)}) custom-call(s32[19]{0:T(128)} %pad_add_fusion.refs_0_, f32[256,640]{1,0:T(8,128)} %bitcast.37, f32[256,512]{1,0:T(8,128)} %slice_bitcast_fusion.refs_2_, bf16[256,512]{1,0:T(8,128)(2,1)} %collective-permute-done.35.refs_3_, ...), custom_call_target="tpu_custom_call" | custom-call | tf_op jit(solution)/shard_map/pallas_call | solution.py:547
  233.5 4.2 %collective-permute-start.58 = (bf16[224,640]{1,0:T(8,128)(2,1)S(1)}, bf16[224,640]{1,0:T(8,128)(2,1)S(1)}, u32[]{:S(2)}, u32[]{:S(2)}) collective-permute-start(bf16[224,640]{1,0:T(8,128)(2,1)S(1)} %fusion), channel_id=1, source_target_pairs={{0,16},{4,20},{8,24},{12,28},{16,0},{20,4},{24,8},{28,12},{1,17},{... | collective-permute-start | bytes 860168 | tf_op jit(solution)/shard_map/ppermute | solution.py:558
  237.8 13.6 %collective-permute-done.58 = bf16[224,640]{1,0:T(8,128)(2,1)S(1)} collective-permute-done((bf16[224,640]{1,0:T(8,128)(2,1)S(1)}, bf16[224,640]{1,0:T(8,128)(2,1)S(1)}, u32[]{:S(2)}, u32[]{:S(2)}) %collective-permute-start.58) | collective-permute-done | bytes 286752 | tf_op jit(solution)/shard_map/ppermute | solution.py:558
  253.3 2.9 shard_map.288
  256.2 3.4 %collective-permute-start.39 = (bf16[176,768]{1,0:T(8,128)(2,1)}, bf16[176,768]{1,0:T(8,128)(2,1)S(1)}, u32[]{:S(2)}, u32[]{:S(2)}) collective-permute-start(bf16[176,768]{1,0:T(8,128)(2,1)} %get-tuple-element.127), channel_id=1, source_target_pairs={{1,0},{2,1},{3,2},{0,3},{5,4},{6,5},{7,6},{4,7},{9,8},{10,9},{11,1... | collective-permute-start | bytes 811016 | tf_op jit(solution)/shard_map/ppermute | solution.py:555
  261.2 6.1 %collective-permute-done.39.refs_1_ = bf16[176,768]{1,0:T(8,128)(2,1)S(1)} collective-permute-done((bf16[176,768]{1,0:T(8,128)(2,1)}, bf16[176,768]{1,0:T(8,128)(2,1)S(1)}, u32[]{:S(2)}, u32[]{:S(2)}) %collective-permute-start.39) | collective-permute-done | bytes 270368 | tf_op jit(solution)/shard_map/ppermute | solution.py:555
  267.3 6.2 %collective-permute-done.40.refs_2_ = bf16[176,768]{1,0:T(8,128)(2,1)S(1)} collective-permute-done((bf16[176,768]{1,0:T(8,128)(2,1)}, bf16[176,768]{1,0:T(8,128)(2,1)S(1)}, u32[]{:S(2)}, u32[]{:S(2)}) %collective-permute-start.40) | collective-permute-done | bytes 270368 | tf_op jit(solution)/shard_map/ppermute | solution.py:555
  274.2 2.0 shard_map.289.refs_0_
  277.8 5.1 %collective-permute-done.42.refs_1_ = bf16[176,768]{1,0:T(8,128)(2,1)S(1)} collective-permute-done((bf16[176,768]{1,0:T(8,128)(2,1)}, bf16[176,768]{1,0:T(8,128)(2,1)S(1)}, u32[]{:S(2)}, u32[]{:S(2)}) %collective-permute-start.42) | collective-permute-done | bytes 270368 | tf_op jit(solution)/shard_map/ppermute | solution.py:558
  285.4 3.4 %collective-permute-start.43 = (bf16[176,768]{1,0:T(8,128)(2,1)}, bf16[176,768]{1,0:T(8,128)(2,1)S(1)}, u32[]{:S(2)}, u32[]{:S(2)}) collective-permute-start(bf16[176,768]{1,0:T(8,128)(2,1)} %shard_map.290.refs_0_), channel_id=1, source_target_pairs={{0,16},{4,20},{8,24},{12,28},{16,0},{20,4},{24,8},{28,12},{1,17},{... | collective-permute-start | bytes 811016 | tf_op jit(solution)/shard_map/ppermute | solution.py:558
  288.8 9.5 %collective-permute-done.43.refs_1_ = bf16[176,768]{1,0:T(8,128)(2,1)S(1)} collective-permute-done((bf16[176,768]{1,0:T(8,128)(2,1)}, bf16[176,768]{1,0:T(8,128)(2,1)S(1)}, u32[]{:S(2)}, u32[]{:S(2)}) %collective-permute-start.43) | collective-permute-done | bytes 270368 | tf_op jit(solution)/shard_map/ppermute | solution.py:558
  303.3 2.1 shard_map.292
  309.1 4.1 %shard_map.296 = (f32[640,512]{1,0:T(8,128)}, f32[640,512]{1,0:T(8,128)}, f32[512,640]{1,0:T(8,128)}, f32[256,640]{1,0:T(8,128)}) custom-call(s32[19]{0:T(128)} %pad_add_fusion.refs_0_, bf16[896,640]{1,0:T(8,128)(2,1)} %copy-done, bf16[896,640]{1,0:T(8,128)(2,1)} %copy-done.2), custom_call_target="tpu_custom_call" | custom-call | tf_op jit(solution)/shard_map/pallas_call | solution.py:547
  (251 shorter events, 62.0 us)
Async XLA Ops:
  2.4 24.0 %collective-permute-start.5 = (bf16[160,768]{1,0:T(8,128)(2,1)}, bf16[160,768]{1,0:T(8,128)(2,1)S(1)}, u32[]{:S(2)}, u32[]{:S(2)}) collective-permute-start(bf16[160,768]{1,0:T(8,128)(2,1)} %shard_map.281), channel_id=1, source_target_pairs={{3,0},{0,1},{1,2},{2,3},{7,4},{4,5},{5,6},{6,7},{11,8},{8,9},{9,10... | collective-permute-start | bytes 737288 | tf_op jit(solution)/shard_map/ppermute | solution.py:555
  5.4 21.1 %collective-permute-start.4 = (bf16[160,768]{1,0:T(8,128)(2,1)}, bf16[160,768]{1,0:T(8,128)(2,1)S(1)}, u32[]{:S(2)}, u32[]{:S(2)}) collective-permute-start(bf16[160,768]{1,0:T(8,128)(2,1)} %shard_map.281), channel_id=1, source_target_pairs={{2,0},{3,1},{0,2},{1,3},{6,4},{7,5},{4,6},{5,7},{10,8},{11,9},{8,1... | collective-permute-start | bytes 737288 | tf_op jit(solution)/shard_map/ppermute | solution.py:555
  6.9 19.6 %collective-permute-start.3 = (bf16[160,768]{1,0:T(8,128)(2,1)}, bf16[160,768]{1,0:T(8,128)(2,1)S(1)}, u32[]{:S(2)}, u32[]{:S(2)}) collective-permute-start(bf16[160,768]{1,0:T(8,128)(2,1)} %shard_map.281), channel_id=1, source_target_pairs={{1,0},{2,1},{3,2},{0,3},{5,4},{6,5},{7,6},{4,7},{9,8},{10,9},{11,1... | collective-permute-start | bytes 737288 | tf_op jit(solution)/shard_map/ppermute | solution.py:555
  20.1 9.2 %collective-permute-start.18 = (bf16[128,640]{1,0:T(8,128)(2,1)}, bf16[128,640]{1,0:T(8,128)(2,1)S(1)}, u32[]{:S(2)}, u32[]{:S(2)}) collective-permute-start(bf16[128,640]{1,0:T(8,128)(2,1)} %get-tuple-element.93), channel_id=1, source_target_pairs={{3,0},{0,1},{1,2},{2,3},{7,4},{4,5},{5,6},{6,7},{11,8},{8,9},{9,10... | collective-permute-start | bytes 491528 | tf_op jit(solution)/shard_map/ppermute | solution.py:555
  29.3 9.1 %collective-permute-start.8 = (bf16[160,768]{1,0:T(8,128)(2,1)S(1)}, bf16[160,768]{1,0:T(8,128)(2,1)S(1)}, u32[]{:S(2)}, u32[]{:S(2)}) collective-permute-start(bf16[160,768]{1,0:T(8,128)(2,1)S(1)} %collective-permute-done.5.refs_11_), channel_id=1, source_target_pairs={{0,4},{4,0},{8,12},{12,8},{16,20},{20,16},{24,28},{28,24},{1,5},{5... | collective-permute-start | bytes 737288 | tf_op jit(solution)/shard_map/ppermute | solution.py:558
  33.4 10.9 %collective-permute-start.21 = (bf16[128,640]{1,0:T(8,128)(2,1)S(1)}, bf16[128,640]{1,0:T(8,128)(2,1)S(1)}, u32[]{:S(2)}, u32[]{:S(2)}) collective-permute-start(bf16[128,640]{1,0:T(8,128)(2,1)S(1)} %collective-permute-done.18.refs_17_), channel_id=1, source_target_pairs={{0,4},{4,0},{8,12},{12,8},{16,20},{20,16},{24,28},{28,24},{1,5},{5... | collective-permute-start | bytes 491528 | tf_op jit(solution)/shard_map/ppermute | solution.py:558
  34.0 10.5 %collective-permute-start.20 = (bf16[128,640]{1,0:T(8,128)(2,1)S(1)}, bf16[128,640]{1,0:T(8,128)(2,1)S(1)}, u32[]{:S(2)}, u32[]{:S(2)}) collective-permute-start(bf16[128,640]{1,0:T(8,128)(2,1)S(1)} %collective-permute-done.17.refs_16_), channel_id=1, source_target_pairs={{0,4},{4,0},{8,12},{12,8},{16,20},{20,16},{24,28},{28,24},{1,5},{5... | collective-permute-start | bytes 491528 | tf_op jit(solution)/shard_map/ppermute | solution.py:558
  34.0 12.1 %collective-permute-start.19 = (bf16[128,640]{1,0:T(8,128)(2,1)S(1)}, bf16[128,640]{1,0:T(8,128)(2,1)S(1)}, u32[]{:S(2)}, u32[]{:S(2)}) collective-permute-start(bf16[128,640]{1,0:T(8,128)(2,1)S(1)} %collective-permute-done.16.refs_15_), channel_id=1, source_target_pairs={{0,4},{4,0},{8,12},{12,8},{16,20},{20,16},{24,28},{28,24},{1,5},{5... | collective-permute-start | bytes 491528 | tf_op jit(solution)/shard_map/ppermute | solution.py:558
  34.5 36.6 %collective-permute-start.24 = (bf16[640,512]{1,0:T(8,128)(2,1)}, bf16[640,512]{1,0:T(8,128)(2,1)S(1)}, u32[]{:S(2)}, u32[]{:S(2)}) collective-permute-start(bf16[640,512]{1,0:T(8,128)(2,1)} %get-tuple-element.100), channel_id=1, source_target_pairs={{3,0},{0,1},{1,2},{2,3},{7,4},{4,5},{5,6},{6,7},{11,8},{8,9},{9,10... | collective-permute-start | bytes 1966088 | tf_op jit(solution)/shard_map/ppermute | solution.py:555
  38.4 33.6 %collective-permute-start.23 = (bf16[640,512]{1,0:T(8,128)(2,1)}, bf16[640,512]{1,0:T(8,128)(2,1)S(1)}, u32[]{:S(2)}, u32[]{:S(2)}) collective-permute-start(bf16[640,512]{1,0:T(8,128)(2,1)} %get-tuple-element.100), channel_id=1, source_target_pairs={{2,0},{3,1},{0,2},{1,3},{6,4},{7,5},{4,6},{5,7},{10,8},{11,9},{8,1... | collective-permute-start | bytes 1966088 | tf_op jit(solution)/shard_map/ppermute | solution.py:555
  44.5 11.3 %collective-permute-start.11 = (bf16[256,512]{1,0:T(8,128)(2,1)}, bf16[256,512]{1,0:T(8,128)(2,1)S(1)}, u32[]{:S(2)}, u32[]{:S(2)}) collective-permute-start(bf16[256,512]{1,0:T(8,128)(2,1)} %get-tuple-element.89.refs_3_), channel_id=1, source_target_pairs={{24,0},{28,4},{0,8},{4,12},{8,16},{12,20},{16,24},{20,28},{25,1},{... | collective-permute-start | bytes 786440 | tf_op jit(solution)/shard_map/ppermute | solution.py:555
  46.1 25.9 %collective-permute-start.22 = (bf16[640,512]{1,0:T(8,128)(2,1)S(1)}, bf16[640,512]{1,0:T(8,128)(2,1)S(1)}, u32[]{:S(2)}, u32[]{:S(2)}) collective-permute-start(bf16[640,512]{1,0:T(8,128)(2,1)S(1)} %copy-done.56), channel_id=1, source_target_pairs={{1,0},{2,1},{3,2},{0,3},{5,4},{6,5},{7,6},{4,7},{9,8},{10,9},{11,1... | collective-permute-start | bytes 1966088 | tf_op jit(solution)/shard_map/ppermute | solution.py:555
  46.7 19.9 %collective-permute-start.10 = (bf16[256,512]{1,0:T(8,128)(2,1)}, bf16[256,512]{1,0:T(8,128)(2,1)S(1)}, u32[]{:S(2)}, u32[]{:S(2)}) collective-permute-start(bf16[256,512]{1,0:T(8,128)(2,1)} %get-tuple-element.89.refs_3_), channel_id=1, source_target_pairs={{16,0},{20,4},{24,8},{28,12},{0,16},{4,20},{8,24},{12,28},{17,1},{... | collective-permute-start | bytes 786440 | tf_op jit(solution)/shard_map/ppermute | solution.py:555
  55.8 14.5 %collective-permute-start.9 = (bf16[256,512]{1,0:T(8,128)(2,1)}, bf16[256,512]{1,0:T(8,128)(2,1)S(1)}, u32[]{:S(2)}, u32[]{:S(2)}) collective-permute-start(bf16[256,512]{1,0:T(8,128)(2,1)} %get-tuple-element.89.refs_3_), channel_id=1, source_target_pairs={{8,0},{12,4},{16,8},{20,12},{24,16},{28,20},{0,24},{4,28},{9,1},{1... | collective-permute-start | bytes 786440 | tf_op jit(solution)/shard_map/ppermute | solution.py:555
  66.6 11.5 %collective-permute-start.30 = (bf16[256,640]{1,0:T(8,128)(2,1)S(1)}, bf16[256,640]{1,0:T(8,128)(2,1)S(1)}, u32[]{:S(2)}, u32[]{:S(2)}) collective-permute-start(bf16[256,640]{1,0:T(8,128)(2,1)S(1)} %copy-done.57), channel_id=1, source_target_pairs={{3,0},{0,1},{1,2},{2,3},{7,4},{4,5},{5,6},{6,7},{11,8},{8,9},{9,10... | collective-permute-start | bytes 983048 | tf_op jit(solution)/shard_map/ppermute | solution.py:555
  70.4 12.9 %collective-permute-start.29 = (bf16[256,640]{1,0:T(8,128)(2,1)S(1)}, bf16[256,640]{1,0:T(8,128)(2,1)S(1)}, u32[]{:S(2)}, u32[]{:S(2)}) collective-permute-start(bf16[256,640]{1,0:T(8,128)(2,1)S(1)} %copy-done.57), channel_id=1, source_target_pairs={{2,0},{3,1},{0,2},{1,3},{6,4},{7,5},{4,6},{5,7},{10,8},{11,9},{8,1... | collective-permute-start | bytes 983048 | tf_op jit(solution)/shard_map/ppermute | solution.py:555
  71.1 12.2 %collective-permute-start.28 = (bf16[256,640]{1,0:T(8,128)(2,1)S(1)}, bf16[256,640]{1,0:T(8,128)(2,1)S(1)}, u32[]{:S(2)}, u32[]{:S(2)}) collective-permute-start(bf16[256,640]{1,0:T(8,128)(2,1)S(1)} %copy-done.57), channel_id=1, source_target_pairs={{1,0},{2,1},{3,2},{0,3},{5,4},{6,5},{7,6},{4,7},{9,8},{10,9},{11,1... | collective-permute-start | bytes 983048 | tf_op jit(solution)/shard_map/ppermute | solution.py:555
  72.0 11.8 %collective-permute-start.15 = (bf16[256,512]{1,0:T(8,128)(2,1)S(1)}, bf16[256,512]{1,0:T(8,128)(2,1)S(1)}, u32[]{:S(2)}, u32[]{:S(2)}) collective-permute-start(bf16[256,512]{1,0:T(8,128)(2,1)S(1)} %collective-permute-done.11.refs_6_), channel_id=1, source_target_pairs={{0,4},{4,0},{8,12},{12,8},{16,20},{20,16},{24,28},{28,24},{1,5},{5... | collective-permute-start | bytes 786440 | tf_op jit(solution)/shard_map/ppermute | solution.py:558
  72.0 11.8 %collective-permute-start.14 = (bf16[256,512]{1,0:T(8,128)(2,1)S(1)}, bf16[256,512]{1,0:T(8,128)(2,1)S(1)}, u32[]{:S(2)}, u32[]{:S(2)}) collective-permute-start(bf16[256,512]{1,0:T(8,128)(2,1)S(1)} %collective-permute-done.10.refs_5_), channel_id=1, source_target_pairs={{0,4},{4,0},{8,12},{12,8},{16,20},{20,16},{24,28},{28,24},{1,5},{5... | collective-permute-start | bytes 786440 | tf_op jit(solution)/shard_map/ppermute | solution.py:558
  78.1 9.7 %collective-permute-start.33 = (bf16[256,640]{1,0:T(8,128)(2,1)S(1)}, bf16[256,640]{1,0:T(8,128)(2,1)S(1)}, u32[]{:S(2)}, u32[]{:S(2)}) collective-permute-start(bf16[256,640]{1,0:T(8,128)(2,1)S(1)} %collective-permute-done.30.refs_19_), channel_id=1, source_target_pairs={{0,4},{4,0},{8,12},{12,8},{16,20},{20,16},{24,28},{28,24},{1,5},{5... | collective-permute-start | bytes 983048 | tf_op jit(solution)/shard_map/ppermute | solution.py:558
  83.3 12.5 %collective-permute-start.25 = (bf16[640,512]{1,0:T(8,128)(2,1)S(1)}, bf16[640,512]{1,0:T(8,128)(2,1)S(1)}, u32[]{:S(2)}, u32[]{:S(2)}) collective-permute-start(bf16[640,512]{1,0:T(8,128)(2,1)S(1)} %collective-permute-done.22.refs_11_), channel_id=1, source_target_pairs={{0,4},{4,0},{8,12},{12,8},{16,20},{20,16},{24,28},{28,24},{1,5},{5... | collective-permute-start | bytes 1966088 | tf_op jit(solution)/shard_map/ppermute | solution.py:558
  83.3 12.5 %collective-permute-start.26 = (bf16[640,512]{1,0:T(8,128)(2,1)S(1)}, bf16[640,512]{1,0:T(8,128)(2,1)S(1)}, u32[]{:S(2)}, u32[]{:S(2)}) collective-permute-start(bf16[640,512]{1,0:T(8,128)(2,1)S(1)} %collective-permute-done.23.refs_12_), channel_id=1, source_target_pairs={{0,4},{4,0},{8,12},{12,8},{16,20},{20,16},{24,28},{28,24},{1,5},{5... | collective-permute-start | bytes 1966088 | tf_op jit(solution)/shard_map/ppermute | solution.py:558
  83.8 12.0 %collective-permute-start.27 = (bf16[640,512]{1,0:T(8,128)(2,1)S(1)}, bf16[640,512]{1,0:T(8,128)(2,1)S(1)}, u32[]{:S(2)}, u32[]{:S(2)}) collective-permute-start(bf16[640,512]{1,0:T(8,128)(2,1)S(1)} %collective-permute-done.24.refs_13_), channel_id=1, source_target_pairs={{0,4},{4,0},{8,12},{12,8},{16,20},{20,16},{24,28},{28,24},{1,5},{5... | collective-permute-start | bytes 1966088 | tf_op jit(solution)/shard_map/ppermute | solution.py:558
  87.6 8.1 %collective-permute-start.32 = (bf16[256,640]{1,0:T(8,128)(2,1)S(1)}, bf16[256,640]{1,0:T(8,128)(2,1)S(1)}, u32[]{:S(2)}, u32[]{:S(2)}) collective-permute-start(bf16[256,640]{1,0:T(8,128)(2,1)S(1)} %collective-permute-done.29.refs_18_), channel_id=1, source_target_pairs={{0,4},{4,0},{8,12},{12,8},{16,20},{20,16},{24,28},{28,24},{1,5},{5... | collective-permute-start | bytes 983048 | tf_op jit(solution)/shard_map/ppermute | solution.py:558
  111.8 12.4 %collective-permute-start.45 = (bf16[512,640]{1,0:T(8,128)(2,1)}, bf16[512,640]{1,0:T(8,128)(2,1)S(1)}, u32[]{:S(2)}, u32[]{:S(2)}) collective-permute-start(bf16[512,640]{1,0:T(8,128)(2,1)} %get-tuple-element.134), channel_id=1, source_target_pairs={{0,4},{4,0},{8,12},{12,8},{16,20},{20,16},{24,28},{28,24},{1,5},{5... | collective-permute-start | bytes 1966088 | tf_op jit(solution)/shard_map/ppermute | solution.py:558
  112.0 11.5 %collective-permute-start.48 = (bf16[256,640]{1,0:T(8,128)(2,1)S(1)}, bf16[256,640]{1,0:T(8,128)(2,1)S(1)}, u32[]{:S(2)}, u32[]{:S(2)}) collective-permute-start(bf16[256,640]{1,0:T(8,128)(2,1)S(1)} %copy-done.1), channel_id=1, source_target_pairs={{3,0},{0,1},{1,2},{2,3},{7,4},{4,5},{5,6},{6,7},{11,8},{8,9},{9,10... | collective-permute-start | bytes 983048 | tf_op jit(solution)/shard_map/ppermute | solution.py:555
  114.0 16.6 %collective-permute-start.47 = (bf16[256,640]{1,0:T(8,128)(2,1)S(1)}, bf16[256,640]{1,0:T(8,128)(2,1)S(1)}, u32[]{:S(2)}, u32[]{:S(2)}) collective-permute-start(bf16[256,640]{1,0:T(8,128)(2,1)S(1)} %copy-done.1), channel_id=1, source_target_pairs={{2,0},{3,1},{0,2},{1,3},{6,4},{7,5},{4,6},{5,7},{10,8},{11,9},{8,1... | collective-permute-start | bytes 983048 | tf_op jit(solution)/shard_map/ppermute | solution.py:555
  115.1 15.5 %collective-permute-start.46 = (bf16[256,640]{1,0:T(8,128)(2,1)S(1)}, bf16[256,640]{1,0:T(8,128)(2,1)S(1)}, u32[]{:S(2)}, u32[]{:S(2)}) collective-permute-start(bf16[256,640]{1,0:T(8,128)(2,1)S(1)} %copy-done.1), channel_id=1, source_target_pairs={{1,0},{2,1},{3,2},{0,3},{5,4},{6,5},{7,6},{4,7},{9,8},{10,9},{11,1... | collective-permute-start | bytes 983048 | tf_op jit(solution)/shard_map/ppermute | solution.py:555
  115.6 22.0 %collective-permute-start.51 = (bf16[256,640]{1,0:T(8,128)(2,1)}, bf16[256,640]{1,0:T(8,128)(2,1)S(1)}, u32[]{:S(2)}, u32[]{:S(2)}) collective-permute-start(bf16[256,640]{1,0:T(8,128)(2,1)} %get-tuple-element.137.refs_5_), channel_id=1, source_target_pairs={{3,0},{0,1},{1,2},{2,3},{7,4},{4,5},{5,6},{6,7},{11,8},{8,9},{9,10... | collective-permute-start | bytes 983048 | tf_op jit(solution)/shard_map/ppermute | solution.py:555
  123.5 20.4 %collective-permute-start.50 = (bf16[256,640]{1,0:T(8,128)(2,1)}, bf16[256,640]{1,0:T(8,128)(2,1)S(1)}, u32[]{:S(2)}, u32[]{:S(2)}) collective-permute-start(bf16[256,640]{1,0:T(8,128)(2,1)} %get-tuple-element.137.refs_5_), channel_id=1, source_target_pairs={{2,0},{3,1},{0,2},{1,3},{6,4},{7,5},{4,6},{5,7},{10,8},{11,9},{8,1... | collective-permute-start | bytes 983048 | tf_op jit(solution)/shard_map/ppermute | solution.py:555
  124.2 19.8 %collective-permute-start.49 = (bf16[256,640]{1,0:T(8,128)(2,1)}, bf16[256,640]{1,0:T(8,128)(2,1)S(1)}, u32[]{:S(2)}, u32[]{:S(2)}) collective-permute-start(bf16[256,640]{1,0:T(8,128)(2,1)} %get-tuple-element.137.refs_5_), channel_id=1, source_target_pairs={{1,0},{2,1},{3,2},{0,3},{5,4},{6,5},{7,6},{4,7},{9,8},{10,9},{11,1... | collective-permute-start | bytes 983048 | tf_op jit(solution)/shard_map/ppermute | solution.py:555
  155.3 19.2 %collective-permute-start.52 = (bf16[768,640]{1,0:T(8,128)(2,1)}, bf16[768,640]{1,0:T(8,128)(2,1)S(1)}, u32[]{:S(2)}, u32[]{:S(2)}) collective-permute-start(bf16[768,640]{1,0:T(8,128)(2,1)} %get-tuple-element.139), channel_id=1, source_target_pairs={{0,4},{4,0},{8,12},{12,8},{16,20},{20,16},{24,28},{28,24},{1,5},{5... | collective-permute-start | bytes 2949128 | tf_op jit(solution)/shard_map/ppermute | solution.py:558
  163.3 19.6 %collective-permute-start.34 = (bf16[4,256,512]{2,1,0:T(8,128)(2,1)}, bf16[4,256,512]{2,1,0:T(8,128)(2,1)S(1)}, u32[]{:S(2)}, u32[]{:S(2)}) collective-permute-start(bf16[4,256,512]{2,1,0:T(8,128)(2,1)} %get-tuple-element.112), channel_id=1, source_target_pairs={{0,4},{4,0},{8,12},{12,8},{16,20},{20,16},{24,28},{28,24},{1,5},{5... | collective-permute-start | bytes 3145736 | tf_op jit(solution)/shard_map/ppermute | solution.py:558
  165.1 9.4 %collective-permute-start.54 = (bf16[128,640]{1,0:T(8,128)(2,1)S(1)}, bf16[128,640]{1,0:T(8,128)(2,1)S(1)}, u32[]{:S(2)}, u32[]{:S(2)}) collective-permute-start(bf16[128,640]{1,0:T(8,128)(2,1)S(1)} %copy-done.59), channel_id=1, source_target_pairs={{2,0},{3,1},{0,2},{1,3},{6,4},{7,5},{4,6},{5,7},{10,8},{11,9},{8,1... | collective-permute-start | bytes 491528 | tf_op jit(solution)/shard_map/ppermute | solution.py:555
  166.3 8.2 %collective-permute-start.55 = (bf16[128,640]{1,0:T(8,128)(2,1)S(1)}, bf16[128,640]{1,0:T(8,128)(2,1)S(1)}, u32[]{:S(2)}, u32[]{:S(2)}) collective-permute-start(bf16[128,640]{1,0:T(8,128)(2,1)S(1)} %copy-done.58), channel_id=1, source_target_pairs={{3,0},{0,1},{1,2},{2,3},{7,4},{4,5},{5,6},{6,7},{11,8},{8,9},{9,10... | collective-permute-start | bytes 491528 | tf_op jit(solution)/shard_map/ppermute | solution.py:555
  179.0 15.8 %collective-permute-start.56 = (bf16[448,640]{1,0:T(8,128)(2,1)}, bf16[448,640]{1,0:T(8,128)(2,1)S(1)}, u32[]{:S(2)}, u32[]{:S(2)}) collective-permute-start(bf16[448,640]{1,0:T(8,128)(2,1)} %get-tuple-element.144), channel_id=1, source_target_pairs={{0,8},{4,12},{8,0},{12,4},{16,24},{20,28},{24,16},{28,20},{1,9},{5... | collective-permute-start | bytes 1720328 | tf_op jit(solution)/shard_map/ppermute | solution.py:558
  195.0 38.4 %collective-permute-start.57 = (bf16[224,640]{1,0:T(8,128)(2,1)S(1)}, bf16[224,640]{1,0:T(8,128)(2,1)S(1)}, u32[]{:S(2)}, u32[]{:S(2)}) collective-permute-start(bf16[224,640]{1,0:T(8,128)(2,1)S(1)} %dynamic-slice_bitcast_fusion), channel_id=1, source_target_pairs={{0,16},{4,20},{8,24},{12,28},{16,0},{20,4},{24,8},{28,12},{1,17},{... | collective-permute-start | bytes 860168 | tf_op jit(solution)/shard_map/ppermute | solution.py:558
  199.3 13.5 %collective-permute-start.37 = (bf16[256,512]{1,0:T(8,128)(2,1)}, bf16[256,512]{1,0:T(8,128)(2,1)S(1)}, u32[]{:S(2)}, u32[]{:S(2)}) collective-permute-start(bf16[256,512]{1,0:T(8,128)(2,1)} %get-tuple-element.155), channel_id=1, source_target_pairs={{24,0},{28,4},{0,8},{4,12},{8,16},{12,20},{16,24},{20,28},{25,1},{... | collective-permute-start | bytes 786440 | tf_op jit(solution)/shard_map/ppermute | solution.py:555
  201.0 26.5 %collective-permute-start.36 = (bf16[256,512]{1,0:T(8,128)(2,1)}, bf16[256,512]{1,0:T(8,128)(2,1)}, u32[]{:S(2)}, u32[]{:S(2)}) collective-permute-start(bf16[256,512]{1,0:T(8,128)(2,1)} %get-tuple-element.156), channel_id=1, source_target_pairs={{16,0},{20,4},{24,8},{28,12},{0,16},{4,20},{8,24},{12,28},{17,1},{... | collective-permute-start | bytes 786440 | tf_op jit(solution)/shard_map/ppermute | solution.py:555
  201.0 26.5 %collective-permute-start.35 = (bf16[256,512]{1,0:T(8,128)(2,1)}, bf16[256,512]{1,0:T(8,128)(2,1)}, u32[]{:S(2)}, u32[]{:S(2)}) collective-permute-start(bf16[256,512]{1,0:T(8,128)(2,1)} %get-tuple-element.157), channel_id=1, source_target_pairs={{8,0},{12,4},{16,8},{20,12},{24,16},{28,20},{0,24},{4,28},{9,1},{1... | collective-permute-start | bytes 786440 | tf_op jit(solution)/shard_map/ppermute | solution.py:555
  233.4 19.0 %collective-permute-start.38 = (bf16[640,768]{1,0:T(8,128)(2,1)}, bf16[640,768]{1,0:T(8,128)(2,1)S(1)}, u32[]{:S(2)}, u32[]{:S(2)}) collective-permute-start(bf16[640,768]{1,0:T(8,128)(2,1)} %get-tuple-element.124), channel_id=1, source_target_pairs={{0,4},{4,0},{8,12},{12,8},{16,20},{20,16},{24,28},{28,24},{1,5},{5... | collective-permute-start | bytes 2949128 | tf_op jit(solution)/shard_map/ppermute | solution.py:558
  233.5 17.9 %collective-permute-start.58 = (bf16[224,640]{1,0:T(8,128)(2,1)S(1)}, bf16[224,640]{1,0:T(8,128)(2,1)S(1)}, u32[]{:S(2)}, u32[]{:S(2)}) collective-permute-start(bf16[224,640]{1,0:T(8,128)(2,1)S(1)} %fusion), channel_id=1, source_target_pairs={{0,16},{4,20},{8,24},{12,28},{16,0},{20,4},{24,8},{28,12},{1,17},{... | collective-permute-start | bytes 860168 | tf_op jit(solution)/shard_map/ppermute | solution.py:558
  251.5 25.9 %collective-permute-start.59 = (bf16[448,640]{1,0:T(8,128)(2,1)S(1)}, bf16[448,640]{1,0:T(8,128)(2,1)S(1)}, u32[]{:S(2)}, u32[]{:S(2)}) collective-permute-start(bf16[448,640]{1,0:T(8,128)(2,1)S(1)} %pad_maximum_fusion.1), channel_id=1, source_target_pairs={{0,8},{4,12},{8,0},{12,4},{16,24},{20,28},{24,16},{28,20},{1,9},{5... | collective-permute-start | bytes 1720328 | tf_op jit(solution)/shard_map/ppermute | solution.py:558
  256.2 11.1 %collective-permute-start.39 = (bf16[176,768]{1,0:T(8,128)(2,1)}, bf16[176,768]{1,0:T(8,128)(2,1)S(1)}, u32[]{:S(2)}, u32[]{:S(2)}) collective-permute-start(bf16[176,768]{1,0:T(8,128)(2,1)} %get-tuple-element.127), channel_id=1, source_target_pairs={{1,0},{2,1},{3,2},{0,3},{5,4},{6,5},{7,6},{4,7},{9,8},{10,9},{11,1... | collective-permute-start | bytes 811016 | tf_op jit(solution)/shard_map/ppermute | solution.py:555
  259.5 13.9 %collective-permute-start.40 = (bf16[176,768]{1,0:T(8,128)(2,1)}, bf16[176,768]{1,0:T(8,128)(2,1)S(1)}, u32[]{:S(2)}, u32[]{:S(2)}) collective-permute-start(bf16[176,768]{1,0:T(8,128)(2,1)} %get-tuple-element.128), channel_id=1, source_target_pairs={{2,0},{3,1},{0,2},{1,3},{6,4},{7,5},{4,6},{5,7},{10,8},{11,9},{8,1... | collective-permute-start | bytes 811016 | tf_op jit(solution)/shard_map/ppermute | solution.py:555
  261.2 12.3 %collective-permute-start.41 = (bf16[176,768]{1,0:T(8,128)(2,1)}, bf16[176,768]{1,0:T(8,128)(2,1)S(1)}, u32[]{:S(2)}, u32[]{:S(2)}) collective-permute-start(bf16[176,768]{1,0:T(8,128)(2,1)} %get-tuple-element.129), channel_id=1, source_target_pairs={{3,0},{0,1},{1,2},{2,3},{7,4},{4,5},{5,6},{6,7},{11,8},{8,9},{9,10... | collective-permute-start | bytes 811016 | tf_op jit(solution)/shard_map/ppermute | solution.py:555
  277.7 30.3 %collective-permute-start.60 = (bf16[896,640]{1,0:T(8,128)(2,1)S(1)}, bf16[896,640]{1,0:T(8,128)(2,1)S(1)}, u32[]{:S(2)}, u32[]{:S(2)}) collective-permute-start(bf16[896,640]{1,0:T(8,128)(2,1)S(1)} %pad_maximum_fusion.refs_1_), channel_id=1, source_target_pairs={{0,4},{4,0},{8,12},{12,8},{16,20},{20,16},{24,28},{28,24},{1,5},{5... | collective-permute-start | bytes 3440648 | tf_op jit(solution)/shard_map/ppermute | solution.py:558
  285.4 12.9 %collective-permute-start.43 = (bf16[176,768]{1,0:T(8,128)(2,1)}, bf16[176,768]{1,0:T(8,128)(2,1)S(1)}, u32[]{:S(2)}, u32[]{:S(2)}) collective-permute-start(bf16[176,768]{1,0:T(8,128)(2,1)} %shard_map.290.refs_0_), channel_id=1, source_target_pairs={{0,16},{4,20},{8,24},{12,28},{16,0},{20,4},{24,8},{28,12},{1,17},{... | collective-permute-start | bytes 811016 | tf_op jit(solution)/shard_map/ppermute | solution.py:558
  (74 other events, 883.3 us)

commit v2 on v1

--- a/solution.py
+++ b/solution.py
@@ -369,8 +369,14 @@
 
 
 def weight_kernel(ins, outs, scratch):
-    place_ref, feed_refs, grad_refs, gate_ref, up_ref, down_ref = ins
-    mine_ref, theirs_ref = outs
+    place_ref, feed_refs, grad_refs, gate_ref, up_ref, down_ref, omine_ref, oother_ref = ins
+    mine_ref, theirs_ref, chunks = outs
+    fsdp_place, size = place_ref[1], len(chunks)
+    shard = chunks[0].shape[0]
+    for k in range(size):
+        at = pl.multiple_of(lax.rem(fsdp_place + size - k, size) * shard, 16)
+        chunk = omine_ref[pl.ds(at, shard), :] + oother_ref[pl.ds(at, shard), :].astype(f32)
+        chunks[k][...] = chunk.astype(bf16)
     (grad_ref,) = scratch
     parity = place_ref[2]
     units = down_ref.shape[0]
@@ -479,20 +485,8 @@
         ref[...] = pltpu.roll(sums, lax.rem(half - fsdp_place * cols, half), 1)[:, :cols]
 
 
-def out_pack_kernel(ins, outs, scratch):
-    place_ref, mine_ref, other_ref = ins
-    fsdp_place = place_ref[1]
-    size = len(outs)
-    shard = outs[0].shape[0]
-    for k in range(size):
-        at = pl.multiple_of(lax.rem(fsdp_place + size - k, size) * shard, 16)
-        chunk = mine_ref[pl.ds(at, shard), :] + other_ref[pl.ds(at, shard), :].astype(f32)
-        outs[k][...] = chunk.astype(bf16)
-
-
 def early_pack_kernel(ins, outs, scratch):
     place_ref, mine_ref, other_ref, parts = ins
-    keep_ref, send_ref = outs
     (all_ref,) = scratch
     base = mine_ref.shape[0]
     all_ref[:base, :] = (mine_ref[...] + other_ref[...].astype(f32)).astype(bf16)
@@ -500,16 +494,25 @@
     for ref in parts[1:]:
         total = total + ref[...].astype(f32)
     all_ref[base:, :] = total.astype(bf16)
-    rows = keep_ref.shape[0]
-    side = lax.rem(lax.div(place_ref[0], 2), 2)
-    keep_ref[...] = all_ref[pl.ds(pl.multiple_of(side * rows, 16), rows), :]
-    send_ref[...] = all_ref[pl.ds(pl.multiple_of((1 - side) * rows, 16), rows), :]
+    rows = outs[0].shape[0]
+    chip_place = lax.div(place_ref[0], 2)
+    base = chip_place if len(outs) == 4 else lax.rem(chip_place, 2)
+    for k, ref in enumerate(outs):
+        at = pl.multiple_of(lax.bitwise_xor(base, k) * rows, 16)
+        ref[...] = all_ref[pl.ds(at, rows), :]
 
 
 def early_last_kernel(ins, outs, scratch):
-    place_ref, mine_ref, other_ref = ins
+    place_ref, mine, other = ins
     gate_ref, up_ref, down_ref, out_ref = outs
+    mine_ref, other_ref = scratch
     parity = place_ref[2]
+    chip_place = lax.div(place_ref[0], 2)
+    rows = mine[0].shape[0]
+    for k in range(len(mine)):
+        at = 0 if len(mine) == 1 else pl.multiple_of(lax.bitwise_xor(chip_place, k) * rows, 16)
+        mine_ref[pl.ds(at, rows), :] = mine[k][...]
+        other_ref[pl.ds(at, rows), :] = other[k][...]
     half = down_ref.shape[0] // 2
     out_half = out_ref.shape[0] // 2
     for ref, side in ((mine_ref, parity), (other_ref, 1 - parity)):
@@ -569,7 +572,18 @@
     def pick(x, at, axis=0):
         return lax.dynamic_index_in_dim(x, at, axis, keepdims=False)
 
-    def sum_chips(keep, send, ctx_place):
+    def sum_chips(parts, ctx_place):
+        if len(parts) == 4:
+            far = with_partner(parts[3], 2)
+            near = with_partner(parts[1], 2)
+            passed = (parts[2].astype(f32) + far.astype(f32)).astype(bf16)
+            across = with_partner(passed, 4)
+            total = parts[0].astype(f32) + near.astype(f32) + across.astype(f32)
+            total = total.astype(bf16)
+            second = with_partner(total, 4)
+            first = with_partner(total, 2)
+            return [total, first, second, with_partner(second, 2)]
+        keep, send = parts
         width = keep.shape[1]
         steps = []
         bit = 2
@@ -578,9 +592,9 @@
             sent = with_partner(send, bit)
             total = (keep.astype(f32) + sent.astype(f32)).astype(bf16)
             if 2 * bit < ctx_size:
-                parts = total.reshape(2, -1, width)
+                halves = total.reshape(2, -1, width)
                 ahead = (ctx_place // (2 * bit)) % 2
-                keep, send = pick(parts, ahead), pick(parts, 1 - ahead)
+                keep, send = pick(halves, ahead), pick(halves, 1 - ahead)
             steps.append((bit, side))
             bit *= 2
         for bit, side in reversed(steps):
@@ -588,7 +602,7 @@
             first = jnp.where(side == 0, total, other)
             second = jnp.where(side == 0, other, total)
             total = jnp.concatenate([first, second], axis=0)
-        return total
+        return [total]
 
     def body(
         tokens,
@@ -756,43 +770,39 @@
         chip_own = chip_part[0]
         back_parts = [from_peer(chip_send[k - 1], "ctx", 2 * k) for k in range(1, chips)]
 
-        out_chunks = run_kernel(
-            out_pack_kernel,
-            (place, out_own, out_other),
-            [((out_rows // 2, width), bf16)] * fsdp_size,
+        feed_rows = 3 * half_rows
+        early_mine, early_theirs, out_chunks = run_kernel(
+            weight_kernel,
+            (place, feed_all, grad_all, gate_weight, up_weight, down_weight, out_own, out_other),
+            (
+                ((feed_rows, width), f32),
+                ((feed_rows, width), bf16),
+                [((out_rows // 2, width), bf16)] * fsdp_size,
+            ),
+            (((2 * feed_rows, width), f32),),
         )
         out_parts = [out_chunks[0]] + [
             from_peer(out_chunks[k], "fsdp", k) for k in range(1, fsdp_size)
         ]
-
-        feed_rows = 3 * half_rows
-        early_mine, early_theirs = run_kernel(
-            weight_kernel,
-            (place, [after(feed_in, out_chunks[0])] + feed_all[1:], grad_all,
-             gate_weight, up_weight, down_weight),
-            (
-                ((feed_rows, width), f32),
-                ((feed_rows, width), bf16),
-            ),
-            (((2 * feed_rows, width), f32),),
-        )
         early_rows = feed_rows + out_rows // 2
-        keep, send = run_kernel(
+        pieces = 4 if chips == 4 else 2
+        early_parts = run_kernel(
             early_pack_kernel,
             (place, early_mine, with_partner(early_theirs), out_parts),
-            (((early_rows // 2, width), bf16),) * 2,
+            [((early_rows // pieces, width), bf16)] * pieces,
             (((early_rows, width), bf16),),
         )
-        early = sum_chips(keep, send, ctx_place)
+        early = sum_chips(early_parts, ctx_place)
         gate_grad, up_grad, down_grad, out_grad = run_kernel(
             early_last_kernel,
-            (place, early, with_partner(early)),
+            (place, early, with_partners(early)),
             (
                 ((width, hidden_rows), f32),
                 ((width, hidden_rows), f32),
                 ((hidden_rows, width), f32),
                 ((out_rows, width), f32),
             ),
+            (((early_rows, width), bf16),) * 2,
         )
 
         tokens_grad, late_mine, late_theirs, late_terms = run_kernel(

time: 314 us -> 286 us (0.911)
  waiting for transfers between devices: 142 us -> 125 us
  starting transfers between devices: 66.6 us -> 60.3 us
    ppermute x33, waiting for transfers between devices: 100 us -> 80.9 us  [from_peer(): lax.ppermute(x, axis, [((i + offset) % size, i) for i in range(size)])]
    ppermute x28 -> x33, starting transfers between devices: 20.8 us -> 13.4 us  [with_partner(): return lax.ppermute(x, 'ctx', [(i, i ^ bit) for i in range(ctx_size)])]
    ppermute x28 -> x33, waiting for transfers between devices: 42 us -> 43.8 us  [with_partner(): return lax.ppermute(x, 'ctx', [(i, i ^ bit) for i in range(ctx_size)])]
    pallas_call x17 -> x16, Pallas kernels: 77.2 us -> 75.9 us  [run_kernel(): return jax.tree.unflatten(out_tree, call(*flat))]
    unnamed x122 -> x140, local copies, waits for them, and re-layouts: 9.96 us -> 9.98 us
  transfers between devices with their start and end apart: 61 -> 66, of which waited for: 23 -> 22; matrix products, arithmetic and copies ran while one was open for 5% -> 4% of each run, Pallas kernels for 15% -> 17%
where the time goes in v2:
time: 286 us
  waiting for transfers between devices  125 us (44%)
  Pallas kernels  75.9 us (27%)
  starting transfers between devices  60.3 us (21%)
  local copies, waits for them, and re-layouts  20 us (7%)
  other arithmetic  3.32 us (1%)
    ppermute x33, waiting for transfers between devices, from_peer(): lax.ppermute(x, axis, [((i + offset) % size, i) for i in range(size)])  80.9 us
    pallas_call x16, Pallas kernels, run_kernel(): return jax.tree.unflatten(out_tree, call(*flat))  75.9 us
    ppermute x33, starting transfers between devices, from_peer(): lax.ppermute(x, axis, [((i + offset) % size, i) for i in range(size)])  46.9 us
    ppermute x33, waiting for transfers between devices, with_partner(): return lax.ppermute(x, 'ctx', [(i, i ^ bit) for i in range(ctx_size)])  43.8 us
    ppermute x33, starting transfers between devices, with_partner(): return lax.ppermute(x, 'ctx', [(i, i ^ bit) for i in range(ctx_size)])  13.4 us
    unnamed x140, local copies, waits for them, and re-layouts  9.98 us
  transfers between devices with their start and end apart: 66, of which 22 were waited for; matrix products, arithmetic and copies ran while one was open for 4% of the time, Pallas kernels for 17%

profile of v2, /device:TPU:0, one launch (start us, length us, event | category | flops | bytes accessed | tf_op | source)
XLA Modules:
  0.0 285.8 jit_solution(6032034904232267390)
XLA Ops:
  0.7 1.7 shard_map.281
  2.4 3.0 %collective-permute-start.5 = (bf16[160,768]{1,0:T(8,128)(2,1)}, bf16[160,768]{1,0:T(8,128)(2,1)S(1)}, u32[]{:S(2)}, u32[]{:S(2)}) collective-permute-start(bf16[160,768]{1,0:T(8,128)(2,1)} %shard_map.281), channel_id=1, source_target_pairs={{3,0},{0,1},{1,2},{2,3},{7,4},{4,5},{5,6},{6,7},{11,8},{8,9},{9,10... | collective-permute-start | bytes 737288 | tf_op jit(solution)/shard_map/ppermute | solution.py:558
  12.4 2.0 collective-permute-start
  15.7 2.7 shard_map.283
  18.4 1.7 collective-permute-start.2
  22.5 2.2 shard_map.280
  29.3 4.1 %collective-permute-done.17.refs_16_ = bf16[128,640]{1,0:T(8,128)(2,1)S(1)} collective-permute-done((bf16[128,640]{1,0:T(8,128)(2,1)}, bf16[128,640]{1,0:T(8,128)(2,1)S(1)}, u32[]{:S(2)}, u32[]{:S(2)}) %collective-permute-start.17) | collective-permute-done | bytes 163872 | tf_op jit(solution)/shard_map/ppermute | solution.py:558
  34.5 3.8 %collective-permute-start.24 = (bf16[640,512]{1,0:T(8,128)(2,1)}, bf16[640,512]{1,0:T(8,128)(2,1)S(1)}, u32[]{:S(2)}, u32[]{:S(2)}) collective-permute-start(bf16[640,512]{1,0:T(8,128)(2,1)} %get-tuple-element.101), channel_id=1, source_target_pairs={{3,0},{0,1},{1,2},{2,3},{7,4},{4,5},{5,6},{6,7},{11,8},{8,9},{9,10... | collective-permute-start | bytes 1966088 | tf_op jit(solution)/shard_map/ppermute | solution.py:558
  38.4 1.7 collective-permute-start.23
  40.1 4.2 %shard_map.282 = (bf16[256,640]{1,0:T(8,128)(2,1)}, bf16[256,1024]{1,0:T(8,128)(2,1)}, bf16[256,512]{1,0:T(8,128)(2,1)}, f32[256,1024]{1,0:T(8,128)}, f32[256,256]{1,0:T(8,128)}, /*index=5*/bf16[640,1536]{1,0:T(8,128)(2,1)}) custom-call(s32[19]{0:T(128)} %pad_add_fusion.refs_0_, f32[256,640]{1,0:T(8,128)} %bitcast.29, ...), custom_call_target="tpu_custom_call" | custom-call | tf_op jit(solution)/shard_map/pallas_call | solution.py:550
  46.6 2.6 collective-permute-start.10
  49.2 6.6 %collective-permute-done.11.refs_6_ = bf16[256,512]{1,0:T(8,128)(2,1)S(1)} collective-permute-done((bf16[256,512]{1,0:T(8,128)(2,1)}, bf16[256,512]{1,0:T(8,128)(2,1)S(1)}, u32[]{:S(2)}, u32[]{:S(2)}) %collective-permute-start.11) | collective-permute-done | bytes 262176 | tf_op jit(solution)/shard_map/ppermute | solution.py:558
  57.1 9.4 %collective-permute-done.10.refs_5_ = bf16[256,512]{1,0:T(8,128)(2,1)S(1)} collective-permute-done((bf16[256,512]{1,0:T(8,128)(2,1)}, bf16[256,512]{1,0:T(8,128)(2,1)S(1)}, u32[]{:S(2)}, u32[]{:S(2)}) %collective-permute-start.10) | collective-permute-done | bytes 262176 | tf_op jit(solution)/shard_map/ppermute | solution.py:558
  66.6 3.7 %collective-permute-done.9.refs_4_ = bf16[256,512]{1,0:T(8,128)(2,1)S(1)} collective-permute-done((bf16[256,512]{1,0:T(8,128)(2,1)}, bf16[256,512]{1,0:T(8,128)(2,1)S(1)}, u32[]{:S(2)}, u32[]{:S(2)}) %collective-permute-start.9) | collective-permute-done | bytes 262176 | tf_op jit(solution)/shard_map/ppermute | solution.py:558
  72.4 5.6 %collective-permute-done.30.refs_19_ = bf16[256,640]{1,0:T(8,128)(2,1)S(1)} collective-permute-done((bf16[256,640]{1,0:T(8,128)(2,1)S(1)}, bf16[256,640]{1,0:T(8,128)(2,1)S(1)}, u32[]{:S(2)}, u32[]{:S(2)}) %collective-permute-start.30) | collective-permute-done | bytes 327712 | tf_op jit(solution)/shard_map/ppermute | solution.py:558
  78.0 5.2 %collective-permute-done.29.refs_18_ = bf16[256,640]{1,0:T(8,128)(2,1)S(1)} collective-permute-done((bf16[256,640]{1,0:T(8,128)(2,1)S(1)}, bf16[256,640]{1,0:T(8,128)(2,1)S(1)}, u32[]{:S(2)}, u32[]{:S(2)}) %collective-permute-start.29) | collective-permute-done | bytes 327712 | tf_op jit(solution)/shard_map/ppermute | solution.py:558
  84.3 3.2 %collective-permute-done.13.refs_8_ = bf16[256,512]{1,0:T(8,128)(2,1)S(1)} collective-permute-done((bf16[256,512]{1,0:T(8,128)(2,1)S(1)}, bf16[256,512]{1,0:T(8,128)(2,1)S(1)}, u32[]{:S(2)}, u32[]{:S(2)}) %collective-permute-start.13) | collective-permute-done | bytes 262176 | tf_op jit(solution)/shard_map/ppermute | solution.py:561
  88.2 7.3 %shard_map.284 = (bf16[256,1024]{1,0:T(8,128)(2,1)}, f32[2,512,1]{2,1,0:T(8,128)}, bf16[2,1024,512]{2,1,0:T(8,128)(2,1)}, bf16[1024,640]{1,0:T(8,128)(2,1)}, f32...) custom-call(s32[19]{0:T(128)} %pad_add_fusion.refs_0_, f32[256,640]{1,0:T(8,128)} %bitcast.30, ...), custom_call_target="tpu_custom_call" | custom-call | tf_op jit(solution)/shard_map/pallas_call | solution.py:550
  97.1 14.6 %shard_map.285 = (f32[256,640]{1,0:T(8,128)}, bf16[256,640]{1,0:T(8,128)(2,1)}, f32[256,640]{1,0:T(8,128)}, bf16[256,1024]{1,0:T(8,128)(2,1)}, f32[1,640]{1,0:T(...) custom-call(s32[19]{0:T(128)} %pad_add_fusion.refs_0_, ...), custom_call_target="tpu_custom_call" | custom-call | tf_op jit(solution)/shard_map/pallas_call | solution.py:550
  111.7 8.2 %shard_map.286 = (bf16[256,1024]{1,0:T(8,128)(2,1)}, f32[4,256,512]{2,1,0:T(8,128)}, bf16[4,256,512]{2,1,0:T(8,128)(2,1)}, f32[1,256]{1,0:T(1,128)}) custom-call(bf16[256,1024]{1,0:T(8,128)(2,1)} %get-tuple-element.89.refs_2_.refs_0_, bf16[2,1024,512]{2,1,0:T(8,128)(2,1)} %get-tuple-element.108.refs_1_, bf16[256,1024]{1,0:T(8,128)(2,1)} %get-tuple-element.109.refs_2_, ...), custom_call_target="tpu_custom_call" | custom-call | tf_op jit(solution)/shard_map/pallas_call | solution.py:550
  120.0 2.0 collective-permute-start.47
  123.6 7.9 %collective-permute-done.47.refs_4_ = bf16[256,640]{1,0:T(8,128)(2,1)S(1)} collective-permute-done((bf16[256,640]{1,0:T(8,128)(2,1)S(1)}, bf16[256,640]{1,0:T(8,128)(2,1)S(1)}, u32[]{:S(2)}, u32[]{:S(2)}) %collective-permute-start.47) | collective-permute-done | bytes 327712 | tf_op jit(solution)/shard_map/ppermute | solution.py:558
  132.6 5.9 %collective-permute-done.46.refs_3_ = bf16[256,640]{1,0:T(8,128)(2,1)S(1)} collective-permute-done((bf16[256,640]{1,0:T(8,128)(2,1)S(1)}, bf16[256,640]{1,0:T(8,128)(2,1)S(1)}, u32[]{:S(2)}, u32[]{:S(2)}) %collective-permute-start.46) | collective-permute-done | bytes 327712 | tf_op jit(solution)/shard_map/ppermute | solution.py:558
  140.6 5.1 %collective-permute-done.50.refs_8_ = bf16[256,640]{1,0:T(8,128)(2,1)S(1)} collective-permute-done((bf16[256,640]{1,0:T(8,128)(2,1)S(1)}, bf16[256,640]{1,0:T(8,128)(2,1)S(1)}, u32[]{:S(2)}, u32[]{:S(2)}) %collective-permute-start.50) | collective-permute-done | bytes 327712 | tf_op jit(solution)/shard_map/ppermute | solution.py:558
  145.7 6.4 %collective-permute-done.49.refs_7_ = bf16[256,640]{1,0:T(8,128)(2,1)S(1)} collective-permute-done((bf16[256,640]{1,0:T(8,128)(2,1)S(1)}, bf16[256,640]{1,0:T(8,128)(2,1)S(1)}, u32[]{:S(2)}, u32[]{:S(2)}) %collective-permute-start.49) | collective-permute-done | bytes 327712 | tf_op jit(solution)/shard_map/ppermute | solution.py:558
  153.1 10.8 %shard_map.293 = (f32[768,640]{1,0:T(8,128)}, bf16[768,640]{1,0:T(8,128)(2,1)}, bf16[128,640]{1,0:T(8,128)(2,1)}, bf16[128,640]{1,0:T(8,128)(2,1)}, bf16[128,640]{1,0:T(8,128)(2,1)}, /*index=5*/bf16[128,640]{1,0:T(8,128)(2,1)}) custom-call(s32[19]{0:T(128)} %pad_add_fusion.refs_0_, bf16[256,640]{1,0:T(8,128)(2,1)} %get-tuple-element.95.refs_2_.refs_1_, ...), custom_call_target="tpu_custom_call" | custom-call | tf_op jit(solution)/shard_map/pallas_call | solution.py:550
  164.4 4.1 %collective-permute-start.37 = (bf16[256,512]{1,0:T(8,128)(2,1)S(1)}, bf16[256,512]{1,0:T(8,128)(2,1)S(1)}, u32[]{:S(2)}, u32[]{:S(2)}) collective-permute-start(bf16[256,512]{1,0:T(8,128)(2,1)S(1)} %get-tuple-element.155), channel_id=1, source_target_pairs={{24,0},{28,4},{0,8},{4,12},{8,16},{12,20},{16,24},{20,28},{25,1},{... | collective-permute-start | bytes 786440 | tf_op jit(solution)/shard_map/ppermute | solution.py:558
  168.5 3.3 %collective-permute-start.36 = (bf16[256,512]{1,0:T(8,128)(2,1)S(1)}, bf16[256,512]{1,0:T(8,128)(2,1)S(1)}, u32[]{:S(2)}, u32[]{:S(2)}) collective-permute-start(bf16[256,512]{1,0:T(8,128)(2,1)S(1)} %get-tuple-element.156), channel_id=1, source_target_pairs={{16,0},{20,4},{24,8},{28,12},{0,16},{4,20},{8,24},{12,28},{17,1},{... | collective-permute-start | bytes 786440 | tf_op jit(solution)/shard_map/ppermute | solution.py:558
  174.3 4.3 %collective-permute-done.37.refs_5_ = bf16[256,512]{1,0:T(8,128)(2,1)S(1)} collective-permute-done((bf16[256,512]{1,0:T(8,128)(2,1)S(1)}, bf16[256,512]{1,0:T(8,128)(2,1)S(1)}, u32[]{:S(2)}, u32[]{:S(2)}) %collective-permute-start.37) | collective-permute-done | bytes 262176 | tf_op jit(solution)/shard_map/ppermute | solution.py:558
  179.2 10.4 %collective-permute-done.36.refs_4_ = bf16[256,512]{1,0:T(8,128)(2,1)S(1)} collective-permute-done((bf16[256,512]{1,0:T(8,128)(2,1)S(1)}, bf16[256,512]{1,0:T(8,128)(2,1)S(1)}, u32[]{:S(2)}, u32[]{:S(2)}) %collective-permute-start.36) | collective-permute-done | bytes 262176 | tf_op jit(solution)/shard_map/ppermute | solution.py:558
  190.3 5.8 %shard_map.287 = (f32[256,640]{1,0:T(8,128)}, f32[640,768]{1,0:T(8,128)}, bf16[640,768]{1,0:T(8,128)(2,1)}, bf16[16,768]{1,0:T(8,128)(2,1)}) custom-call(s32[19]{0:T(128)} %pad_add_fusion.refs_0_, f32[256,640]{1,0:T(8,128)} %bitcast.31, f32[256,512]{1,0:T(8,128)} %slice_bitcast_fusion.refs_2_, bf16[256,512]{1,0:T(8,128)(2,1)} %copy-done.47, ...), custom_call_target="tpu_custom_call" | custom-call | tf_op jit(solution)/shard_map/pallas_call | solution.py:550
  197.9 5.9 %collective-permute-done.55.refs_6_ = bf16[128,640]{1,0:T(8,128)(2,1)S(1)} collective-permute-done((bf16[128,640]{1,0:T(8,128)(2,1)S(1)}, bf16[128,640]{1,0:T(8,128)(2,1)S(1)}, u32[]{:S(2)}, u32[]{:S(2)}) %collective-permute-start.55) | collective-permute-done | bytes 163872 | tf_op jit(solution)/shard_map/ppermute | solution.py:558
  204.7 3.4 %shard_map.294 = (bf16[224,640]{1,0:T(8,128)(2,1)}, bf16[224,640]{1,0:T(8,128)(2,1)}, bf16[224,640]{1,0:T(8,128)(2,1)}, bf16[224,640]{1,0:T(8,128)(2,1)}) custom-call(s32[19]{0:T(128)} %pad_add_fusion.refs_0_, f32[768,640]{1,0:T(8,128)} %get-tuple-element.137.refs_1_, bf16[768,640]{1,0:T(8,128)(2,1)} %copy-done.4, ...), custom_call_target="tpu_custom_call" | custom-call | tf_op jit(solution)/shard_map/pallas_call | solution.py:550
  208.2 6.1 %collective-permute-start.57 = (bf16[224,640]{1,0:T(8,128)(2,1)}, bf16[224,640]{1,0:T(8,128)(2,1)S(1)}, u32[]{:S(2)}, u32[]{:S(2)}) collective-permute-start(bf16[224,640]{1,0:T(8,128)(2,1)} %get-tuple-element.146), channel_id=1, source_target_pairs={{0,8},{4,12},{8,0},{12,4},{16,24},{20,28},{24,16},{28,20},{1,9},{5... | collective-permute-start | bytes 860168 | tf_op jit(solution)/shard_map/ppermute | solution.py:561
  214.3 7.8 %collective-permute-done.57 = bf16[224,640]{1,0:T(8,128)(2,1)S(1)} collective-permute-done((bf16[224,640]{1,0:T(8,128)(2,1)}, bf16[224,640]{1,0:T(8,128)(2,1)S(1)}, u32[]{:S(2)}, u32[]{:S(2)}) %collective-permute-start.57) | collective-permute-done | bytes 286752 | tf_op jit(solution)/shard_map/ppermute | solution.py:561
  225.2 2.9 %shard_map.288 = (bf16[176,768]{1,0:T(8,128)(2,1)}, bf16[176,768]{1,0:T(8,128)(2,1)}, bf16[176,768]{1,0:T(8,128)(2,1)}, bf16[176,768]{1,0:T(8,128)(2,1)}) custom-call(s32[19]{0:T(128)} %pad_add_fusion.refs_0_, f32[640,768]{1,0:T(8,128)} %get-tuple-element.124.refs_1_, bf16[640,768]{1,0:T(8,128)(2,1)} %copy-done.3, bf16[16,768]{1,0:T(8,128)(2,1)} %get-tuple-element.126.refs_3_), custom_call_target="tpu_custom_call" | custom-call | tf_op jit(solution)/shard_map/pallas_call | solution.py:550
  230.7 10.5 %collective-permute-done.58 = bf16[224,640]{1,0:T(8,128)(2,1)S(1)} collective-permute-done((bf16[224,640]{1,0:T(8,128)(2,1)S(1)}, bf16[224,640]{1,0:T(8,128)(2,1)S(1)}, u32[]{:S(2)}, u32[]{:S(2)}) %collective-permute-start.58) | collective-permute-done | bytes 286752 | tf_op jit(solution)/shard_map/ppermute | solution.py:561
  242.5 2.0 shard_map.289.refs_0_
  244.5 2.0 collective-permute-start.42
  246.6 4.9 %collective-permute-done.60.refs_3_ = bf16[224,640]{1,0:T(8,128)(2,1)S(1)} collective-permute-done((bf16[224,640]{1,0:T(8,128)(2,1)S(1)}, bf16[224,640]{1,0:T(8,128)(2,1)S(1)}, u32[]{:S(2)}, u32[]{:S(2)}) %collective-permute-start.60) | collective-permute-done | bytes 286752 | tf_op jit(solution)/shard_map/ppermute | solution.py:561
  251.6 7.4 %collective-permute-done.42.refs_1_ = bf16[176,768]{1,0:T(8,128)(2,1)S(1)} collective-permute-done((bf16[176,768]{1,0:T(8,128)(2,1)}, bf16[176,768]{1,0:T(8,128)(2,1)S(1)}, u32[]{:S(2)}, u32[]{:S(2)}) %collective-permute-start.42) | collective-permute-done | bytes 270368 | tf_op jit(solution)/shard_map/ppermute | solution.py:561
  259.6 1.8 shard_map.290.refs_0_
  262.0 2.0 collective-permute-done.59.refs_2_
  264.0 4.5 %collective-permute-done.61.refs_4_ = bf16[224,640]{1,0:T(8,128)(2,1)S(1)} collective-permute-done((bf16[224,640]{1,0:T(8,128)(2,1)S(1)}, bf16[224,640]{1,0:T(8,128)(2,1)S(1)}, u32[]{:S(2)}, u32[]{:S(2)}) %collective-permute-start.61) | collective-permute-done | bytes 286752 | tf_op jit(solution)/shard_map/ppermute | solution.py:561
  268.6 3.4 %collective-permute-done.43.refs_1_ = bf16[176,768]{1,0:T(8,128)(2,1)S(1)} collective-permute-done((bf16[176,768]{1,0:T(8,128)(2,1)}, bf16[176,768]{1,0:T(8,128)(2,1)S(1)}, u32[]{:S(2)}, u32[]{:S(2)}) %collective-permute-start.43) | collective-permute-done | bytes 270368 | tf_op jit(solution)/shard_map/ppermute | solution.py:561
  272.7 1.8 shard_map.291.refs_1_
  276.1 4.2 %shard_map.295 = (f32[640,512]{1,0:T(8,128)}, f32[640,512]{1,0:T(8,128)}, f32[512,640]{1,0:T(8,128)}, f32[256,640]{1,0:T(8,128)}) custom-call(s32[19]{0:T(128)} %pad_add_fusion.refs_0_, bf16[224,640]{1,0:T(8,128)(2,1)} %copy-done.2, bf16[224,640]{1,0:T(8,128)(2,1)} %copy-done.26, bf16[224,640]{1,0:T(8,128)(2,1)} %copy-done.25, bf16[224,640]{1,0:T(8,128)(2,1)} %copy-done.27, ...), custom_call_target="tpu_custom_call" | custom-call | tf_op jit(solution)/shard_map/pallas_call | solution.py:550
  281.0 2.1 shard_map.292
  (273 shorter events, 52.0 us)
Async XLA Ops:
  2.4 24.0 %collective-permute-start.5 = (bf16[160,768]{1,0:T(8,128)(2,1)}, bf16[160,768]{1,0:T(8,128)(2,1)S(1)}, u32[]{:S(2)}, u32[]{:S(2)}) collective-permute-start(bf16[160,768]{1,0:T(8,128)(2,1)} %shard_map.281), channel_id=1, source_target_pairs={{3,0},{0,1},{1,2},{2,3},{7,4},{4,5},{5,6},{6,7},{11,8},{8,9},{9,10... | collective-permute-start | bytes 737288 | tf_op jit(solution)/shard_map/ppermute | solution.py:558
  5.4 21.1 %collective-permute-start.4 = (bf16[160,768]{1,0:T(8,128)(2,1)}, bf16[160,768]{1,0:T(8,128)(2,1)S(1)}, u32[]{:S(2)}, u32[]{:S(2)}) collective-permute-start(bf16[160,768]{1,0:T(8,128)(2,1)} %shard_map.281), channel_id=1, source_target_pairs={{2,0},{3,1},{0,2},{1,3},{6,4},{7,5},{4,6},{5,7},{10,8},{11,9},{8,1... | collective-permute-start | bytes 737288 | tf_op jit(solution)/shard_map/ppermute | solution.py:558
  6.9 19.6 %collective-permute-start.3 = (bf16[160,768]{1,0:T(8,128)(2,1)}, bf16[160,768]{1,0:T(8,128)(2,1)S(1)}, u32[]{:S(2)}, u32[]{:S(2)}) collective-permute-start(bf16[160,768]{1,0:T(8,128)(2,1)} %shard_map.281), channel_id=1, source_target_pairs={{1,0},{2,1},{3,2},{0,3},{5,4},{6,5},{7,6},{4,7},{9,8},{10,9},{11,1... | collective-permute-start | bytes 737288 | tf_op jit(solution)/shard_map/ppermute | solution.py:558
  33.4 10.8 %collective-permute-start.21 = (bf16[128,640]{1,0:T(8,128)(2,1)S(1)}, bf16[128,640]{1,0:T(8,128)(2,1)S(1)}, u32[]{:S(2)}, u32[]{:S(2)}) collective-permute-start(bf16[128,640]{1,0:T(8,128)(2,1)S(1)} %collective-permute-done.18.refs_17_), channel_id=1, source_target_pairs={{0,4},{4,0},{8,12},{12,8},{16,20},{20,16},{24,28},{28,24},{1,5},{5... | collective-permute-start | bytes 491528 | tf_op jit(solution)/shard_map/ppermute | solution.py:561
  34.0 10.4 %collective-permute-start.20 = (bf16[128,640]{1,0:T(8,128)(2,1)S(1)}, bf16[128,640]{1,0:T(8,128)(2,1)S(1)}, u32[]{:S(2)}, u32[]{:S(2)}) collective-permute-start(bf16[128,640]{1,0:T(8,128)(2,1)S(1)} %collective-permute-done.17.refs_16_), channel_id=1, source_target_pairs={{0,4},{4,0},{8,12},{12,8},{16,20},{20,16},{24,28},{28,24},{1,5},{5... | collective-permute-start | bytes 491528 | tf_op jit(solution)/shard_map/ppermute | solution.py:561
  34.0 12.0 %collective-permute-start.19 = (bf16[128,640]{1,0:T(8,128)(2,1)S(1)}, bf16[128,640]{1,0:T(8,128)(2,1)}, u32[]{:S(2)}, u32[]{:S(2)}) collective-permute-start(bf16[128,640]{1,0:T(8,128)(2,1)S(1)} %collective-permute-done.16.refs_15_), channel_id=1, source_target_pairs={{0,4},{4,0},{8,12},{12,8},{16,20},{20,16},{24,28},{28,24},{1,5},{5... | collective-permute-start | bytes 491528 | tf_op jit(solution)/shard_map/ppermute | solution.py:561
  34.5 36.5 %collective-permute-start.24 = (bf16[640,512]{1,0:T(8,128)(2,1)}, bf16[640,512]{1,0:T(8,128)(2,1)S(1)}, u32[]{:S(2)}, u32[]{:S(2)}) collective-permute-start(bf16[640,512]{1,0:T(8,128)(2,1)} %get-tuple-element.101), channel_id=1, source_target_pairs={{3,0},{0,1},{1,2},{2,3},{7,4},{4,5},{5,6},{6,7},{11,8},{8,9},{9,10... | collective-permute-start | bytes 1966088 | tf_op jit(solution)/shard_map/ppermute | solution.py:558
  38.4 33.5 %collective-permute-start.23 = (bf16[640,512]{1,0:T(8,128)(2,1)}, bf16[640,512]{1,0:T(8,128)(2,1)S(1)}, u32[]{:S(2)}, u32[]{:S(2)}) collective-permute-start(bf16[640,512]{1,0:T(8,128)(2,1)} %get-tuple-element.101), channel_id=1, source_target_pairs={{2,0},{3,1},{0,2},{1,3},{6,4},{7,5},{4,6},{5,7},{10,8},{11,9},{8,1... | collective-permute-start | bytes 1966088 | tf_op jit(solution)/shard_map/ppermute | solution.py:558
  44.4 11.3 %collective-permute-start.11 = (bf16[256,512]{1,0:T(8,128)(2,1)}, bf16[256,512]{1,0:T(8,128)(2,1)S(1)}, u32[]{:S(2)}, u32[]{:S(2)}) collective-permute-start(bf16[256,512]{1,0:T(8,128)(2,1)} %get-tuple-element.90.refs_3_), channel_id=1, source_target_pairs={{24,0},{28,4},{0,8},{4,12},{8,16},{12,20},{16,24},{20,28},{25,1},{... | collective-permute-start | bytes 786440 | tf_op jit(solution)/shard_map/ppermute | solution.py:558
  46.0 25.9 %collective-permute-start.22 = (bf16[640,512]{1,0:T(8,128)(2,1)S(1)}, bf16[640,512]{1,0:T(8,128)(2,1)S(1)}, u32[]{:S(2)}, u32[]{:S(2)}) collective-permute-start(bf16[640,512]{1,0:T(8,128)(2,1)S(1)} %copy-done.64), channel_id=1, source_target_pairs={{1,0},{2,1},{3,2},{0,3},{5,4},{6,5},{7,6},{4,7},{9,8},{10,9},{11,1... | collective-permute-start | bytes 1966088 | tf_op jit(solution)/shard_map/ppermute | solution.py:558
  46.6 19.9 %collective-permute-start.10 = (bf16[256,512]{1,0:T(8,128)(2,1)}, bf16[256,512]{1,0:T(8,128)(2,1)S(1)}, u32[]{:S(2)}, u32[]{:S(2)}) collective-permute-start(bf16[256,512]{1,0:T(8,128)(2,1)} %get-tuple-element.90.refs_3_), channel_id=1, source_target_pairs={{16,0},{20,4},{24,8},{28,12},{0,16},{4,20},{8,24},{12,28},{17,1},{... | collective-permute-start | bytes 786440 | tf_op jit(solution)/shard_map/ppermute | solution.py:558
  55.7 14.5 %collective-permute-start.9 = (bf16[256,512]{1,0:T(8,128)(2,1)}, bf16[256,512]{1,0:T(8,128)(2,1)S(1)}, u32[]{:S(2)}, u32[]{:S(2)}) collective-permute-start(bf16[256,512]{1,0:T(8,128)(2,1)} %get-tuple-element.90.refs_3_), channel_id=1, source_target_pairs={{8,0},{12,4},{16,8},{20,12},{24,16},{28,20},{0,24},{4,28},{9,1},{1... | collective-permute-start | bytes 786440 | tf_op jit(solution)/shard_map/ppermute | solution.py:558
  66.5 11.5 %collective-permute-start.30 = (bf16[256,640]{1,0:T(8,128)(2,1)S(1)}, bf16[256,640]{1,0:T(8,128)(2,1)S(1)}, u32[]{:S(2)}, u32[]{:S(2)}) collective-permute-start(bf16[256,640]{1,0:T(8,128)(2,1)S(1)} %copy-done.66), channel_id=1, source_target_pairs={{3,0},{0,1},{1,2},{2,3},{7,4},{4,5},{5,6},{6,7},{11,8},{8,9},{9,10... | collective-permute-start | bytes 983048 | tf_op jit(solution)/shard_map/ppermute | solution.py:558
  70.3 12.9 %collective-permute-start.29 = (bf16[256,640]{1,0:T(8,128)(2,1)S(1)}, bf16[256,640]{1,0:T(8,128)(2,1)S(1)}, u32[]{:S(2)}, u32[]{:S(2)}) collective-permute-start(bf16[256,640]{1,0:T(8,128)(2,1)S(1)} %copy-done.66), channel_id=1, source_target_pairs={{2,0},{3,1},{0,2},{1,3},{6,4},{7,5},{4,6},{5,7},{10,8},{11,9},{8,1... | collective-permute-start | bytes 983048 | tf_op jit(solution)/shard_map/ppermute | solution.py:558
  71.0 12.2 %collective-permute-start.28 = (bf16[256,640]{1,0:T(8,128)(2,1)S(1)}, bf16[256,640]{1,0:T(8,128)(2,1)S(1)}, u32[]{:S(2)}, u32[]{:S(2)}) collective-permute-start(bf16[256,640]{1,0:T(8,128)(2,1)S(1)} %copy-done.66), channel_id=1, source_target_pairs={{1,0},{2,1},{3,2},{0,3},{5,4},{6,5},{7,6},{4,7},{9,8},{10,9},{11,1... | collective-permute-start | bytes 983048 | tf_op jit(solution)/shard_map/ppermute | solution.py:558
  71.9 11.8 %collective-permute-start.15 = (bf16[256,512]{1,0:T(8,128)(2,1)S(1)}, bf16[256,512]{1,0:T(8,128)(2,1)S(1)}, u32[]{:S(2)}, u32[]{:S(2)}) collective-permute-start(bf16[256,512]{1,0:T(8,128)(2,1)S(1)} %collective-permute-done.11.refs_6_), channel_id=1, source_target_pairs={{0,4},{4,0},{8,12},{12,8},{16,20},{20,16},{24,28},{28,24},{1,5},{5... | collective-permute-start | bytes 786440 | tf_op jit(solution)/shard_map/ppermute | solution.py:561
  71.9 11.9 %collective-permute-start.14 = (bf16[256,512]{1,0:T(8,128)(2,1)S(1)}, bf16[256,512]{1,0:T(8,128)(2,1)S(1)}, u32[]{:S(2)}, u32[]{:S(2)}) collective-permute-start(bf16[256,512]{1,0:T(8,128)(2,1)S(1)} %collective-permute-done.10.refs_5_), channel_id=1, source_target_pairs={{0,4},{4,0},{8,12},{12,8},{16,20},{20,16},{24,28},{28,24},{1,5},{5... | collective-permute-start | bytes 786440 | tf_op jit(solution)/shard_map/ppermute | solution.py:561
  83.2 12.5 %collective-permute-start.25 = (bf16[640,512]{1,0:T(8,128)(2,1)S(1)}, bf16[640,512]{1,0:T(8,128)(2,1)S(1)}, u32[]{:S(2)}, u32[]{:S(2)}) collective-permute-start(bf16[640,512]{1,0:T(8,128)(2,1)S(1)} %collective-permute-done.22.refs_11_), channel_id=1, source_target_pairs={{0,4},{4,0},{8,12},{12,8},{16,20},{20,16},{24,28},{28,24},{1,5},{5... | collective-permute-start | bytes 1966088 | tf_op jit(solution)/shard_map/ppermute | solution.py:561
  83.2 12.5 %collective-permute-start.26 = (bf16[640,512]{1,0:T(8,128)(2,1)S(1)}, bf16[640,512]{1,0:T(8,128)(2,1)S(1)}, u32[]{:S(2)}, u32[]{:S(2)}) collective-permute-start(bf16[640,512]{1,0:T(8,128)(2,1)S(1)} %collective-permute-done.23.refs_12_), channel_id=1, source_target_pairs={{0,4},{4,0},{8,12},{12,8},{16,20},{20,16},{24,28},{28,24},{1,5},{5... | collective-permute-start | bytes 1966088 | tf_op jit(solution)/shard_map/ppermute | solution.py:561
  83.7 12.0 %collective-permute-start.27 = (bf16[640,512]{1,0:T(8,128)(2,1)S(1)}, bf16[640,512]{1,0:T(8,128)(2,1)S(1)}, u32[]{:S(2)}, u32[]{:S(2)}) collective-permute-start(bf16[640,512]{1,0:T(8,128)(2,1)S(1)} %collective-permute-done.24.refs_13_), channel_id=1, source_target_pairs={{0,4},{4,0},{8,12},{12,8},{16,20},{20,16},{24,28},{28,24},{1,5},{5... | collective-permute-start | bytes 1966088 | tf_op jit(solution)/shard_map/ppermute | solution.py:561
  119.9 44.0 %collective-permute-start.34 = (bf16[4,256,512]{2,1,0:T(8,128)(2,1)}, bf16[4,256,512]{2,1,0:T(8,128)(2,1)S(1)}, u32[]{:S(2)}, u32[]{:S(2)}) collective-permute-start(bf16[4,256,512]{2,1,0:T(8,128)(2,1)} %get-tuple-element.113), channel_id=1, source_target_pairs={{0,4},{4,0},{8,12},{12,8},{16,20},{20,16},{24,28},{28,24},{1,5},{5... | collective-permute-start | bytes 3145736 | tf_op jit(solution)/shard_map/ppermute | solution.py:561
  120.0 11.5 %collective-permute-start.47 = (bf16[256,640]{1,0:T(8,128)(2,1)S(1)}, bf16[256,640]{1,0:T(8,128)(2,1)S(1)}, u32[]{:S(2)}, u32[]{:S(2)}) collective-permute-start(bf16[256,640]{1,0:T(8,128)(2,1)S(1)} %copy-done.1), channel_id=1, source_target_pairs={{3,0},{0,1},{1,2},{2,3},{7,4},{4,5},{5,6},{6,7},{11,8},{8,9},{9,10... | collective-permute-start | bytes 983048 | tf_op jit(solution)/shard_map/ppermute | solution.py:558
  122.0 16.5 %collective-permute-start.46 = (bf16[256,640]{1,0:T(8,128)(2,1)S(1)}, bf16[256,640]{1,0:T(8,128)(2,1)S(1)}, u32[]{:S(2)}, u32[]{:S(2)}) collective-permute-start(bf16[256,640]{1,0:T(8,128)(2,1)S(1)} %copy-done.1), channel_id=1, source_target_pairs={{2,0},{3,1},{0,2},{1,3},{6,4},{7,5},{4,6},{5,7},{10,8},{11,9},{8,1... | collective-permute-start | bytes 983048 | tf_op jit(solution)/shard_map/ppermute | solution.py:558
  123.2 16.0 %collective-permute-start.45 = (bf16[256,640]{1,0:T(8,128)(2,1)S(1)}, bf16[256,640]{1,0:T(8,128)(2,1)S(1)}, u32[]{:S(2)}, u32[]{:S(2)}) collective-permute-start(bf16[256,640]{1,0:T(8,128)(2,1)S(1)} %copy-done.1), channel_id=1, source_target_pairs={{1,0},{2,1},{3,2},{0,3},{5,4},{6,5},{7,6},{4,7},{9,8},{10,9},{11,1... | collective-permute-start | bytes 983048 | tf_op jit(solution)/shard_map/ppermute | solution.py:558
  123.6 28.4 %collective-permute-start.51 = (bf16[512,640]{1,0:T(8,128)(2,1)S(1)}, bf16[512,640]{1,0:T(8,128)(2,1)S(1)}, u32[]{:S(2)}, u32[]{:S(2)}) collective-permute-start(bf16[512,640]{1,0:T(8,128)(2,1)S(1)} %copy-done.65), channel_id=1, source_target_pairs={{0,4},{4,0},{8,12},{12,8},{16,20},{20,16},{24,28},{28,24},{1,5},{5... | collective-permute-start | bytes 1966088 | tf_op jit(solution)/shard_map/ppermute | solution.py:561
  131.6 14.1 %collective-permute-start.50 = (bf16[256,640]{1,0:T(8,128)(2,1)S(1)}, bf16[256,640]{1,0:T(8,128)(2,1)S(1)}, u32[]{:S(2)}, u32[]{:S(2)}) collective-permute-start(bf16[256,640]{1,0:T(8,128)(2,1)S(1)} %copy-done.18), channel_id=1, source_target_pairs={{3,0},{0,1},{1,2},{2,3},{7,4},{4,5},{5,6},{6,7},{11,8},{8,9},{9,10... | collective-permute-start | bytes 983048 | tf_op jit(solution)/shard_map/ppermute | solution.py:558
  138.5 13.5 %collective-permute-start.49 = (bf16[256,640]{1,0:T(8,128)(2,1)S(1)}, bf16[256,640]{1,0:T(8,128)(2,1)S(1)}, u32[]{:S(2)}, u32[]{:S(2)}) collective-permute-start(bf16[256,640]{1,0:T(8,128)(2,1)S(1)} %copy-done.18), channel_id=1, source_target_pairs={{2,0},{3,1},{0,2},{1,3},{6,4},{7,5},{4,6},{5,7},{10,8},{11,9},{8,1... | collective-permute-start | bytes 983048 | tf_op jit(solution)/shard_map/ppermute | solution.py:558
  139.2 12.9 %collective-permute-start.48 = (bf16[256,640]{1,0:T(8,128)(2,1)S(1)}, bf16[256,640]{1,0:T(8,128)(2,1)S(1)}, u32[]{:S(2)}, u32[]{:S(2)}) collective-permute-start(bf16[256,640]{1,0:T(8,128)(2,1)S(1)} %copy-done.18), channel_id=1, source_target_pairs={{1,0},{2,1},{3,2},{0,3},{5,4},{6,5},{7,6},{4,7},{9,8},{10,9},{11,1... | collective-permute-start | bytes 983048 | tf_op jit(solution)/shard_map/ppermute | solution.py:558
  163.9 39.9 %collective-permute-start.52 = (bf16[768,640]{1,0:T(8,128)(2,1)}, bf16[768,640]{1,0:T(8,128)(2,1)S(1)}, u32[]{:S(2)}, u32[]{:S(2)}) collective-permute-start(bf16[768,640]{1,0:T(8,128)(2,1)} %get-tuple-element.138), channel_id=1, source_target_pairs={{0,4},{4,0},{8,12},{12,8},{16,20},{20,16},{24,28},{28,24},{1,5},{5... | collective-permute-start | bytes 2949128 | tf_op jit(solution)/shard_map/ppermute | solution.py:561
  164.4 14.2 %collective-permute-start.37 = (bf16[256,512]{1,0:T(8,128)(2,1)S(1)}, bf16[256,512]{1,0:T(8,128)(2,1)S(1)}, u32[]{:S(2)}, u32[]{:S(2)}) collective-permute-start(bf16[256,512]{1,0:T(8,128)(2,1)S(1)} %get-tuple-element.155), channel_id=1, source_target_pairs={{24,0},{28,4},{0,8},{4,12},{8,16},{12,20},{16,24},{20,28},{25,1},{... | collective-permute-start | bytes 786440 | tf_op jit(solution)/shard_map/ppermute | solution.py:558
  168.5 21.0 %collective-permute-start.36 = (bf16[256,512]{1,0:T(8,128)(2,1)S(1)}, bf16[256,512]{1,0:T(8,128)(2,1)S(1)}, u32[]{:S(2)}, u32[]{:S(2)}) collective-permute-start(bf16[256,512]{1,0:T(8,128)(2,1)S(1)} %get-tuple-element.156), channel_id=1, source_target_pairs={{16,0},{20,4},{24,8},{28,12},{0,16},{4,20},{8,24},{12,28},{17,1},{... | collective-permute-start | bytes 786440 | tf_op jit(solution)/shard_map/ppermute | solution.py:558
  171.8 17.7 %collective-permute-start.35 = (bf16[256,512]{1,0:T(8,128)(2,1)S(1)}, bf16[256,512]{1,0:T(8,128)(2,1)S(1)}, u32[]{:S(2)}, u32[]{:S(2)}) collective-permute-start(bf16[256,512]{1,0:T(8,128)(2,1)S(1)} %get-tuple-element.157), channel_id=1, source_target_pairs={{8,0},{12,4},{16,8},{20,12},{24,16},{28,20},{0,24},{4,28},{9,1},{1... | collective-permute-start | bytes 786440 | tf_op jit(solution)/shard_map/ppermute | solution.py:558
  171.8 26.0 %collective-permute-start.53 = (bf16[128,640]{1,0:T(8,128)(2,1)S(1)}, bf16[128,640]{1,0:T(8,128)(2,1)S(1)}, u32[]{:S(2)}, u32[]{:S(2)}) collective-permute-start(bf16[128,640]{1,0:T(8,128)(2,1)S(1)} %copy-done.69), channel_id=1, source_target_pairs={{1,0},{2,1},{3,2},{0,3},{5,4},{6,5},{7,6},{4,7},{9,8},{10,9},{11,1... | collective-permute-start | bytes 491528 | tf_op jit(solution)/shard_map/ppermute | solution.py:558
  178.6 19.3 %collective-permute-start.54 = (bf16[128,640]{1,0:T(8,128)(2,1)S(1)}, bf16[128,640]{1,0:T(8,128)(2,1)S(1)}, u32[]{:S(2)}, u32[]{:S(2)}) collective-permute-start(bf16[128,640]{1,0:T(8,128)(2,1)S(1)} %copy-done.68), channel_id=1, source_target_pairs={{2,0},{3,1},{0,2},{1,3},{6,4},{7,5},{4,6},{5,7},{10,8},{11,9},{8,1... | collective-permute-start | bytes 491528 | tf_op jit(solution)/shard_map/ppermute | solution.py:558
  196.2 28.1 %collective-permute-start.38 = (bf16[640,768]{1,0:T(8,128)(2,1)}, bf16[640,768]{1,0:T(8,128)(2,1)S(1)}, u32[]{:S(2)}, u32[]{:S(2)}) collective-permute-start(bf16[640,768]{1,0:T(8,128)(2,1)} %get-tuple-element.125), channel_id=1, source_target_pairs={{0,4},{4,0},{8,12},{12,8},{16,20},{20,16},{24,28},{28,24},{1,5},{5... | collective-permute-start | bytes 2949128 | tf_op jit(solution)/shard_map/ppermute | solution.py:561
  208.2 13.9 %collective-permute-start.57 = (bf16[224,640]{1,0:T(8,128)(2,1)}, bf16[224,640]{1,0:T(8,128)(2,1)S(1)}, u32[]{:S(2)}, u32[]{:S(2)}) collective-permute-start(bf16[224,640]{1,0:T(8,128)(2,1)} %get-tuple-element.146), channel_id=1, source_target_pairs={{0,8},{4,12},{8,0},{12,4},{16,24},{20,28},{24,16},{28,20},{1,9},{5... | collective-permute-start | bytes 860168 | tf_op jit(solution)/shard_map/ppermute | solution.py:561
  214.2 16.5 %collective-permute-start.56 = (bf16[224,640]{1,0:T(8,128)(2,1)}, bf16[224,640]{1,0:T(8,128)(2,1)S(1)}, u32[]{:S(2)}, u32[]{:S(2)}) collective-permute-start(bf16[224,640]{1,0:T(8,128)(2,1)} %get-tuple-element.144), channel_id=1, source_target_pairs={{0,8},{4,12},{8,0},{12,4},{16,24},{20,28},{24,16},{28,20},{1,9},{5... | collective-permute-start | bytes 860168 | tf_op jit(solution)/shard_map/ppermute | solution.py:561
  223.2 18.1 %collective-permute-start.58 = (bf16[224,640]{1,0:T(8,128)(2,1)S(1)}, bf16[224,640]{1,0:T(8,128)(2,1)S(1)}, u32[]{:S(2)}, u32[]{:S(2)}) collective-permute-start(bf16[224,640]{1,0:T(8,128)(2,1)S(1)} %add_convert_fusion.1), channel_id=1, source_target_pairs={{0,16},{4,20},{8,24},{12,28},{16,0},{20,4},{24,8},{28,12},{1,17},{... | collective-permute-start | bytes 860168 | tf_op jit(solution)/shard_map/ppermute | solution.py:561
  228.1 13.4 %collective-permute-start.39 = (bf16[176,768]{1,0:T(8,128)(2,1)}, bf16[176,768]{1,0:T(8,128)(2,1)S(1)}, u32[]{:S(2)}, u32[]{:S(2)}) collective-permute-start(bf16[176,768]{1,0:T(8,128)(2,1)} %get-tuple-element.128), channel_id=1, source_target_pairs={{1,0},{2,1},{3,2},{0,3},{5,4},{6,5},{7,6},{4,7},{9,8},{10,9},{11,1... | collective-permute-start | bytes 811016 | tf_op jit(solution)/shard_map/ppermute | solution.py:558
  228.8 12.7 %collective-permute-start.40 = (bf16[176,768]{1,0:T(8,128)(2,1)}, bf16[176,768]{1,0:T(8,128)(2,1)S(1)}, u32[]{:S(2)}, u32[]{:S(2)}) collective-permute-start(bf16[176,768]{1,0:T(8,128)(2,1)} %get-tuple-element.129), channel_id=1, source_target_pairs={{2,0},{3,1},{0,2},{1,3},{6,4},{7,5},{4,6},{5,7},{10,8},{11,9},{8,1... | collective-permute-start | bytes 811016 | tf_op jit(solution)/shard_map/ppermute | solution.py:558
  230.2 11.3 %collective-permute-start.41 = (bf16[176,768]{1,0:T(8,128)(2,1)}, bf16[176,768]{1,0:T(8,128)(2,1)S(1)}, u32[]{:S(2)}, u32[]{:S(2)}) collective-permute-start(bf16[176,768]{1,0:T(8,128)(2,1)} %get-tuple-element.130), channel_id=1, source_target_pairs={{3,0},{0,1},{1,2},{2,3},{7,4},{4,5},{5,6},{6,7},{11,8},{8,9},{9,10... | collective-permute-start | bytes 811016 | tf_op jit(solution)/shard_map/ppermute | solution.py:558
  244.5 14.4 %collective-permute-start.42 = (bf16[176,768]{1,0:T(8,128)(2,1)}, bf16[176,768]{1,0:T(8,128)(2,1)S(1)}, u32[]{:S(2)}, u32[]{:S(2)}) collective-permute-start(bf16[176,768]{1,0:T(8,128)(2,1)} %shard_map.289.refs_0_), channel_id=1, source_target_pairs={{0,8},{4,12},{8,0},{12,4},{16,24},{20,28},{24,16},{28,20},{1,9},{5... | collective-permute-start | bytes 811016 | tf_op jit(solution)/shard_map/ppermute | solution.py:561
  246.6 17.5 %collective-permute-start.59 = (bf16[224,640]{1,0:T(8,128)(2,1)S(1)}, bf16[224,640]{1,0:T(8,128)(2,1)S(1)}, u32[]{:S(2)}, u32[]{:S(2)}) collective-permute-start(bf16[224,640]{1,0:T(8,128)(2,1)S(1)} %add_convert_fusion.refs_1_), channel_id=1, source_target_pairs={{0,8},{4,12},{8,0},{12,4},{16,24},{20,28},{24,16},{28,20},{1,9},{5... | collective-permute-start | bytes 860168 | tf_op jit(solution)/shard_map/ppermute | solution.py:561
  251.5 17.0 %collective-permute-start.61 = (bf16[224,640]{1,0:T(8,128)(2,1)S(1)}, bf16[224,640]{1,0:T(8,128)(2,1)S(1)}, u32[]{:S(2)}, u32[]{:S(2)}) collective-permute-start(bf16[224,640]{1,0:T(8,128)(2,1)S(1)} %collective-permute-done.60.refs_3_), channel_id=1, source_target_pairs={{0,8},{4,12},{8,0},{12,4},{16,24},{20,28},{24,16},{28,20},{1,9},{5... | collective-permute-start | bytes 860168 | tf_op jit(solution)/shard_map/ppermute | solution.py:561
  261.4 10.5 %collective-permute-start.43 = (bf16[176,768]{1,0:T(8,128)(2,1)}, bf16[176,768]{1,0:T(8,128)(2,1)S(1)}, u32[]{:S(2)}, u32[]{:S(2)}) collective-permute-start(bf16[176,768]{1,0:T(8,128)(2,1)} %shard_map.290.refs_0_), channel_id=1, source_target_pairs={{0,16},{4,20},{8,24},{12,28},{16,0},{20,4},{24,8},{28,12},{1,17},{... | collective-permute-start | bytes 811016 | tf_op jit(solution)/shard_map/ppermute | solution.py:561
  261.5 12.9 %collective-permute-start.62 = (bf16[224,640]{1,0:T(8,128)(2,1)S(1)}, bf16[224,640]{1,0:T(8,128)(2,1)S(1)}, u32[]{:S(2)}, u32[]{:S(2)}) collective-permute-start(bf16[224,640]{1,0:T(8,128)(2,1)S(1)} %add_convert_fusion.refs_1_), channel_id=1, source_target_pairs={{0,4},{4,0},{8,12},{12,8},{16,20},{20,16},{24,28},{28,24},{1,5},{5... | collective-permute-start | bytes 860168 | tf_op jit(solution)/shard_map/ppermute | solution.py:561
  261.5 12.9 %collective-permute-start.64 = (bf16[224,640]{1,0:T(8,128)(2,1)S(1)}, bf16[224,640]{1,0:T(8,128)(2,1)S(1)}, u32[]{:S(2)}, u32[]{:S(2)}) collective-permute-start(bf16[224,640]{1,0:T(8,128)(2,1)S(1)} %collective-permute-done.60.refs_3_), channel_id=1, source_target_pairs={{0,4},{4,0},{8,12},{12,8},{16,20},{20,16},{24,28},{28,24},{1,5},{5... | collective-permute-start | bytes 860168 | tf_op jit(solution)/shard_map/ppermute | solution.py:561
  264.0 10.4 %collective-permute-start.63 = (bf16[224,640]{1,0:T(8,128)(2,1)S(1)}, bf16[224,640]{1,0:T(8,128)(2,1)S(1)}, u32[]{:S(2)}, u32[]{:S(2)}) collective-permute-start(bf16[224,640]{1,0:T(8,128)(2,1)S(1)} %collective-permute-done.59.refs_2_), channel_id=1, source_target_pairs={{0,4},{4,0},{8,12},{12,8},{16,20},{20,16},{24,28},{28,24},{1,5},{5... | collective-permute-start | bytes 860168 | tf_op jit(solution)/shard_map/ppermute | solution.py:561
  (88 other events, 1049.9 us)

commit v3 on v2

--- a/solution.py
+++ b/solution.py
@@ -112,6 +112,13 @@
         send_ref[:, :rest] = qw_ref[:, half:]
         send_ref[:, rest : rest + head_dim] = kw_ref[...]
         send_ref[:, rest + head_dim :] = vw_ref[...]
+
+
+def gains_kernel(ins, outs, scratch):
+    (gains_ref,) = outs
+    gains_ref[...] = jnp.zeros(gains_ref.shape, f32)
+    for row, ref in enumerate(ins):
+        gains_ref[row, : ref.shape[0]] = ref[...].astype(f32)
 
 
 def halves_kernel(ins, outs, scratch):
@@ -465,7 +472,7 @@
 
 def late_last_kernel(ins, outs, scratch):
     place_ref, mine_ref, other_ref = ins
-    q_ref, k_ref, v_ref, wide_ref, narrow_ref = outs
+    q_ref, k_ref, v_ref, wide_refs, narrow_refs = outs
     (full_ref,) = scratch
     parity = place_ref[2]
     fsdp_place = place_ref[1]
@@ -480,9 +487,11 @@
     v_ref[...] = full_ref[:, width + head_dim :]
     both = mine_ref[rows:, :].astype(f32) + other_ref[rows:, :].astype(f32)
     sums = both[:8] + both[8:]
-    for ref in (wide_ref, narrow_ref):
-        cols = ref.shape[1]
-        ref[...] = pltpu.roll(sums, lax.rem(half - fsdp_place * cols, half), 1)[:, :cols]
+    for refs, row in ((wide_refs, 0), (narrow_refs, len(wide_refs))):
+        cols = refs[0].shape[0]
+        shard = pltpu.roll(sums, lax.rem(half - fsdp_place * cols, half), 1)
+        for k, ref in enumerate(refs):
+            ref[...] = shard[row + k, :cols]
 
 
 def early_pack_kernel(ins, outs, scratch):
@@ -517,8 +526,8 @@
     out_half = out_ref.shape[0] // 2
     for ref, side in ((mine_ref, parity), (other_ref, 1 - parity)):
         cols = pl.multiple_of(side * half, 128)
-        gate_ref[:, pl.ds(cols, half)] = ref[:half, :].astype(f32).T
-        up_ref[:, pl.ds(cols, half)] = ref[half : 2 * half, :].astype(f32).T
+        gate_ref[:, pl.ds(cols, half)] = ref[:half, :].T.astype(f32)
+        up_ref[:, pl.ds(cols, half)] = ref[half : 2 * half, :].T.astype(f32)
         at = pl.multiple_of(side * half, 16)
         down_ref[pl.ds(at, half), :] = ref[2 * half : 3 * half, :].astype(f32)
         at = pl.multiple_of(side * out_half, 16)
@@ -541,7 +550,7 @@
 
     call = pl.pallas_call(
         wrapped,
-        in_specs=[smem if a.ndim == 1 else vmem for a in flat],
+        in_specs=[smem if a.dtype == jnp.int32 and a.ndim == 1 else vmem for a in flat],
         out_specs=[vmem for _ in flat_out],
         out_shape=flat_out,
         scratch_shapes=[pltpu.VMEM(s, d) for s, d in scratch],
@@ -651,9 +660,10 @@
         )
         proj_mine = others_fsdp(proj_send)
         gain_cols, head_cols = input_gain.shape[0], query_gain.shape[0]
-        gains_own = jnp.stack(
-            [g.astype(f32) for g in (input_gain, mixer_gain, prefeed_gain, postfeed_gain)]
-            + [jnp.pad(g.astype(f32), (0, gain_cols - head_cols)) for g in (query_gain, key_gain)]
+        (gains_own,) = run_kernel(
+            gains_kernel,
+            (input_gain, mixer_gain, prefeed_gain, postfeed_gain, query_gain, key_gain),
+            (((8, gain_cols), f32),),
         )
         gain_parts = [gains_own] + others_fsdp(gains_own)
         gain_full = jnp.zeros((fsdp_size,) + gains_own.shape, f32)
@@ -663,7 +673,7 @@
             )
         gain_full = gain_full.transpose(1, 0, 2)
         gains = gain_full[:4].reshape(4, width)
-        qk_gains = gain_full[4:, :, :head_cols].reshape(2, head_dim)
+        qk_gains = gain_full[4:6, :, :head_cols].reshape(2, head_dim)
 
         frequency = rope_base ** (-2.0 * jnp.arange(head_dim // 2, dtype=f32) / head_dim)
         cosines, sine_terms, query_last, query_first, key_ids = run_kernel(
@@ -691,7 +701,6 @@
                 ((half_rows, width), bf16),
             ),
         )
-        pair_half = after(pair_half, *proj_mine)
         out_mine = others_fsdp(out_half)
         pair_mine = others_fsdp(pair_half)
 
@@ -844,8 +853,8 @@
                 ((shard_rows, query_width), f32),
                 ((shard_rows, head_dim), f32),
                 ((shard_rows, head_dim), f32),
-                ((8, gain_cols), f32),
-                ((8, head_cols), f32),
+                [((gain_cols,), f32)] * 4,
+                [((head_cols,), f32)] * 2,
             ),
             (((shard_rows, proj_width), f32),),
         )
@@ -860,8 +869,8 @@
             up_grad,
             down_grad,
             wide_sums[0],
-            narrow_sums[4],
-            narrow_sums[5],
+            narrow_sums[0],
+            narrow_sums[1],
             wide_sums[1],
             wide_sums[2],
             wide_sums[3],

time: 286 us -> 285 us (level)
  local copies, waits for them, and re-layouts: 20 us -> 13.8 us
  starting transfers between devices: 60.3 us -> 64.8 us
    ppermute x33, starting transfers between devices: 13.4 us -> 18.7 us  [with_partner(): return lax.ppermute(x, 'ctx', [(i, i ^ bit) for i in range(ctx_size)])]
    ppermute x33, waiting for transfers between devices: 43.8 us -> 38.7 us  [with_partner(): return lax.ppermute(x, 'ctx', [(i, i ^ bit) for i in range(ctx_size)])]
    ppermute x33, waiting for transfers between devices: 80.9 us -> 85.6 us  [from_peer(): lax.ppermute(x, axis, [((i + offset) % size, i) for i in range(size)])]
    pallas_call x16 -> x17, Pallas kernels: 75.9 us -> 77.2 us  [run_kernel(): return jax.tree.unflatten(out_tree, call(*flat))]
    unnamed x140 -> x142, local copies, waits for them, and re-layouts: 9.98 us -> 10.4 us
  transfers between devices with their start and end apart: 66 -> 66, of which waited for: 22 -> 21; matrix products, arithmetic and copies ran while one was open for 4% -> 2% of each run, Pallas kernels for 17% -> 18%
where the time goes in v3:
time: 285 us
  waiting for transfers between devices  124 us (44%)
  Pallas kernels  77.2 us (27%)
  starting transfers between devices  64.8 us (23%)
  local copies, waits for them, and re-layouts  13.8 us (5%)
  other arithmetic  3.32 us (1%)
    ppermute x33, waiting for transfers between devices, from_peer(): lax.ppermute(x, axis, [((i + offset) % size, i) for i in range(size)])  85.6 us
    pallas_call x17, Pallas kernels, run_kernel(): return jax.tree.unflatten(out_tree, call(*flat))  77.2 us
    ppermute x33, starting transfers between devices, from_peer(): lax.ppermute(x, axis, [((i + offset) % size, i) for i in range(size)])  46.1 us
    ppermute x33, waiting for transfers between devices, with_partner(): return lax.ppermute(x, 'ctx', [(i, i ^ bit) for i in range(ctx_size)])  38.7 us
    ppermute x33, starting transfers between devices, with_partner(): return lax.ppermute(x, 'ctx', [(i, i ^ bit) for i in range(ctx_size)])  18.7 us
    unnamed x142, local copies, waits for them, and re-layouts  10.4 us
  transfers between devices with their start and end apart: 66, of which 21 were waited for; matrix products, arithmetic and copies ran while one was open for 2% of the time, Pallas kernels for 18%

profile of v3, /device:TPU:0, one launch (start us, length us, event | category | flops | bytes accessed | tf_op | source)
XLA Modules:
  0.0 284.8 jit_solution(5048236408516627010)
XLA Ops:
  0.7 1.7 shard_map.282
  2.4 3.0 %collective-permute-start.5 = (bf16[160,768]{1,0:T(8,128)(2,1)}, bf16[160,768]{1,0:T(8,128)(2,1)S(1)}, u32[]{:S(2)}, u32[]{:S(2)}) collective-permute-start(bf16[160,768]{1,0:T(8,128)(2,1)} %shard_map.282), channel_id=1, source_target_pairs={{3,0},{0,1},{1,2},{2,3},{7,4},{4,5},{5,6},{6,7},{11,8},{8,9},{9,10... | collective-permute-start | bytes 737288 | tf_op jit(solution)/shard_map/ppermute | solution.py:567
  10.8 7.3 %collective-permute-done.2 = f32[8,160]{1,0:T(8,128)S(1)} collective-permute-done((f32[8,160]{1,0:T(8,128)}, f32[8,160]{1,0:T(8,128)S(1)}, u32[]{:S(2)}, u32[]{:S(2)}) %collective-permute-start.2) | collective-permute-done | bytes 5152 | tf_op jit(solution)/shard_map/ppermute | solution.py:567
  21.0 2.7 shard_map.284
  24.1 1.7 collective-permute-start.17
  27.1 2.2 shard_map.281
  34.6 17.3 %collective-permute-done.16.refs_15_ = bf16[128,640]{1,0:T(8,128)(2,1)S(1)} collective-permute-done((bf16[128,640]{1,0:T(8,128)(2,1)}, bf16[128,640]{1,0:T(8,128)(2,1)S(1)}, u32[]{:S(2)}, u32[]{:S(2)}) %collective-permute-start.16) | collective-permute-done | bytes 163872 | tf_op jit(solution)/shard_map/ppermute | solution.py:567
  52.6 2.6 collective-permute-start.22
  56.1 4.2 %shard_map.283 = (bf16[256,640]{1,0:T(8,128)(2,1)}, bf16[256,1024]{1,0:T(8,128)(2,1)}, bf16[256,512]{1,0:T(8,128)(2,1)}, f32[256,1024]{1,0:T(8,128)}, f32[256,256]{1,0:T(8,128)}, /*index=5*/bf16[640,1536]{1,0:T(8,128)(2,1)}) custom-call(s32[19]{0:T(128)} %pad_add_fusion.refs_0_, f32[256,640]{1,0:T(8,128)} %bitcast.21, ...), custom_call_target="tpu_custom_call" | custom-call | tf_op jit(solution)/shard_map/pallas_call | solution.py:559
  62.2 2.7 collective-permute-start.10
  64.9 2.2 collective-permute-start.9
  67.1 3.0 %collective-permute-done.22.refs_11_ = bf16[640,512]{1,0:T(8,128)(2,1)S(1)} collective-permute-done((bf16[640,512]{1,0:T(8,128)(2,1)}, bf16[640,512]{1,0:T(8,128)(2,1)S(1)}, u32[]{:S(2)}, u32[]{:S(2)}) %collective-permute-start.22) | collective-permute-done | bytes 655392 | tf_op jit(solution)/shard_map/ppermute | solution.py:567
  70.1 2.3 collective-permute-start.30
  74.5 8.0 %collective-permute-done.10.refs_5_ = bf16[256,512]{1,0:T(8,128)(2,1)S(1)} collective-permute-done((bf16[256,512]{1,0:T(8,128)(2,1)}, bf16[256,512]{1,0:T(8,128)(2,1)S(1)}, u32[]{:S(2)}, u32[]{:S(2)}) %collective-permute-start.10) | collective-permute-done | bytes 262176 | tf_op jit(solution)/shard_map/ppermute | solution.py:567
  83.1 4.8 %collective-permute-done.29.refs_18_ = bf16[256,640]{1,0:T(8,128)(2,1)S(1)} collective-permute-done((bf16[256,640]{1,0:T(8,128)(2,1)S(1)}, bf16[256,640]{1,0:T(8,128)(2,1)S(1)}, u32[]{:S(2)}, u32[]{:S(2)}) %collective-permute-start.29) | collective-permute-done | bytes 327712 | tf_op jit(solution)/shard_map/ppermute | solution.py:567
  88.9 2.8 collective-permute-done.13.refs_8_
  92.5 7.3 %shard_map.285 = (bf16[256,1024]{1,0:T(8,128)(2,1)}, f32[2,512,1]{2,1,0:T(8,128)}, bf16[2,1024,512]{2,1,0:T(8,128)(2,1)}, bf16[1024,640]{1,0:T(8,128)(2,1)}, f32...) custom-call(s32[19]{0:T(128)} %pad_add_fusion.refs_0_, f32[256,640]{1,0:T(8,128)} %bitcast.22, ...), custom_call_target="tpu_custom_call" | custom-call | tf_op jit(solution)/shard_map/pallas_call | solution.py:559
  101.4 14.6 %shard_map.286 = (f32[256,640]{1,0:T(8,128)}, bf16[256,640]{1,0:T(8,128)(2,1)}, f32[256,640]{1,0:T(8,128)}, bf16[256,1024]{1,0:T(8,128)(2,1)}, f32[1,640]{1,0:T(...) custom-call(s32[19]{0:T(128)} %pad_add_fusion.refs_0_, ...), custom_call_target="tpu_custom_call" | custom-call | tf_op jit(solution)/shard_map/pallas_call | solution.py:559
  115.9 8.2 %shard_map.287 = (bf16[256,1024]{1,0:T(8,128)(2,1)}, f32[4,256,512]{2,1,0:T(8,128)}, bf16[4,256,512]{2,1,0:T(8,128)(2,1)}, f32[1,256]{1,0:T(1,128)}) custom-call(bf16[256,1024]{1,0:T(8,128)(2,1)} %get-tuple-element.92.refs_2_.refs_0_, bf16[2,1024,512]{2,1,0:T(8,128)(2,1)} %get-tuple-element.110.refs_1_, bf16[256,1024]{1,0:T(8,128)(2,1)} %get-tuple-element.111.refs_2_, ...), custom_call_target="tpu_custom_call" | custom-call | tf_op jit(solution)/shard_map/pallas_call | solution.py:559
  128.1 7.7 %collective-permute-done.47.refs_4_ = bf16[256,640]{1,0:T(8,128)(2,1)S(1)} collective-permute-done((bf16[256,640]{1,0:T(8,128)(2,1)S(1)}, bf16[256,640]{1,0:T(8,128)(2,1)S(1)}, u32[]{:S(2)}, u32[]{:S(2)}) %collective-permute-start.47) | collective-permute-done | bytes 327712 | tf_op jit(solution)/shard_map/ppermute | solution.py:567
  136.2 6.6 %collective-permute-done.46.refs_3_ = bf16[256,640]{1,0:T(8,128)(2,1)S(1)} collective-permute-done((bf16[256,640]{1,0:T(8,128)(2,1)S(1)}, bf16[256,640]{1,0:T(8,128)(2,1)S(1)}, u32[]{:S(2)}, u32[]{:S(2)}) %collective-permute-start.46) | collective-permute-done | bytes 327712 | tf_op jit(solution)/shard_map/ppermute | solution.py:567
  144.6 5.3 %collective-permute-done.50.refs_8_ = bf16[256,640]{1,0:T(8,128)(2,1)S(1)} collective-permute-done((bf16[256,640]{1,0:T(8,128)(2,1)S(1)}, bf16[256,640]{1,0:T(8,128)(2,1)S(1)}, u32[]{:S(2)}, u32[]{:S(2)}) %collective-permute-start.50) | collective-permute-done | bytes 327712 | tf_op jit(solution)/shard_map/ppermute | solution.py:567
  149.9 6.4 %collective-permute-done.49.refs_7_ = bf16[256,640]{1,0:T(8,128)(2,1)S(1)} collective-permute-done((bf16[256,640]{1,0:T(8,128)(2,1)S(1)}, bf16[256,640]{1,0:T(8,128)(2,1)S(1)}, u32[]{:S(2)}, u32[]{:S(2)}) %collective-permute-start.49) | collective-permute-done | bytes 327712 | tf_op jit(solution)/shard_map/ppermute | solution.py:567
  157.4 10.8 %shard_map.294 = (f32[768,640]{1,0:T(8,128)}, bf16[768,640]{1,0:T(8,128)(2,1)}, bf16[128,640]{1,0:T(8,128)(2,1)}, bf16[128,640]{1,0:T(8,128)(2,1)}, bf16[128,640]{1,0:T(8,128)(2,1)}, /*index=5*/bf16[128,640]{1,0:T(8,128)(2,1)}) custom-call(s32[19]{0:T(128)} %pad_add_fusion.refs_0_, bf16[256,640]{1,0:T(8,128)(2,1)} %get-tuple-element.98.refs_2_.refs_1_, ...), custom_call_target="tpu_custom_call" | custom-call | tf_op jit(solution)/shard_map/pallas_call | solution.py:559
  168.7 2.1 collective-permute-start.37
  170.7 2.1 collective-permute-start.36
  174.3 2.1 collective-permute-start.53
  177.2 2.6 collective-permute-done.37.refs_5_
  180.7 9.9 %collective-permute-done.36.refs_4_ = bf16[256,512]{1,0:T(8,128)(2,1)S(1)} collective-permute-done((bf16[256,512]{1,0:T(8,128)(2,1)S(1)}, bf16[256,512]{1,0:T(8,128)(2,1)S(1)}, u32[]{:S(2)}, u32[]{:S(2)}) %collective-permute-start.36) | collective-permute-done | bytes 262176 | tf_op jit(solution)/shard_map/ppermute | solution.py:567
  191.4 5.8 %shard_map.288 = (f32[256,640]{1,0:T(8,128)}, f32[640,768]{1,0:T(8,128)}, bf16[640,768]{1,0:T(8,128)(2,1)}, bf16[16,768]{1,0:T(8,128)(2,1)}) custom-call(s32[19]{0:T(128)} %pad_add_fusion.refs_0_, f32[256,640]{1,0:T(8,128)} %bitcast.23, f32[256,512]{1,0:T(8,128)} %slice_bitcast_fusion.refs_2_, bf16[256,512]{1,0:T(8,128)(2,1)} %copy-done.47, ...), custom_call_target="tpu_custom_call" | custom-call | tf_op jit(solution)/shard_map/pallas_call | solution.py:559
  198.5 6.3 %collective-permute-done.55.refs_6_ = bf16[128,640]{1,0:T(8,128)(2,1)S(1)} collective-permute-done((bf16[128,640]{1,0:T(8,128)(2,1)S(1)}, bf16[128,640]{1,0:T(8,128)(2,1)S(1)}, u32[]{:S(2)}, u32[]{:S(2)}) %collective-permute-start.55) | collective-permute-done | bytes 163872 | tf_op jit(solution)/shard_map/ppermute | solution.py:567
  205.8 3.4 %shard_map.295 = (bf16[224,640]{1,0:T(8,128)(2,1)}, bf16[224,640]{1,0:T(8,128)(2,1)}, bf16[224,640]{1,0:T(8,128)(2,1)}, bf16[224,640]{1,0:T(8,128)(2,1)}) custom-call(s32[19]{0:T(128)} %pad_add_fusion.refs_0_, f32[768,640]{1,0:T(8,128)} %get-tuple-element.139.refs_1_, bf16[768,640]{1,0:T(8,128)(2,1)} %copy-done.4, ...), custom_call_target="tpu_custom_call" | custom-call | tf_op jit(solution)/shard_map/pallas_call | solution.py:559
  209.3 6.0 %collective-permute-start.57 = (bf16[224,640]{1,0:T(8,128)(2,1)}, bf16[224,640]{1,0:T(8,128)(2,1)S(1)}, u32[]{:S(2)}, u32[]{:S(2)}) collective-permute-start(bf16[224,640]{1,0:T(8,128)(2,1)} %get-tuple-element.148), channel_id=1, source_target_pairs={{0,8},{4,12},{8,0},{12,4},{16,24},{20,28},{24,16},{28,20},{1,9},{5... | collective-permute-start | bytes 860168 | tf_op jit(solution)/shard_map/ppermute | solution.py:570
  215.4 7.8 %collective-permute-done.57 = bf16[224,640]{1,0:T(8,128)(2,1)S(1)} collective-permute-done((bf16[224,640]{1,0:T(8,128)(2,1)}, bf16[224,640]{1,0:T(8,128)(2,1)S(1)}, u32[]{:S(2)}, u32[]{:S(2)}) %collective-permute-start.57) | collective-permute-done | bytes 286752 | tf_op jit(solution)/shard_map/ppermute | solution.py:570
  224.2 1.7 collective-permute-start.58
  226.9 2.9 %shard_map.289 = (bf16[176,768]{1,0:T(8,128)(2,1)}, bf16[176,768]{1,0:T(8,128)(2,1)}, bf16[176,768]{1,0:T(8,128)(2,1)}, bf16[176,768]{1,0:T(8,128)(2,1)}) custom-call(s32[19]{0:T(128)} %pad_add_fusion.refs_0_, f32[640,768]{1,0:T(8,128)} %get-tuple-element.126.refs_1_, bf16[640,768]{1,0:T(8,128)(2,1)} %copy-done.3, bf16[16,768]{1,0:T(8,128)(2,1)} %get-tuple-element.128.refs_3_), custom_call_target="tpu_custom_call" | custom-call | tf_op jit(solution)/shard_map/pallas_call | solution.py:559
  232.7 9.6 %collective-permute-done.58 = bf16[224,640]{1,0:T(8,128)(2,1)S(1)} collective-permute-done((bf16[224,640]{1,0:T(8,128)(2,1)S(1)}, bf16[224,640]{1,0:T(8,128)(2,1)S(1)}, u32[]{:S(2)}, u32[]{:S(2)}) %collective-permute-start.58) | collective-permute-done | bytes 286752 | tf_op jit(solution)/shard_map/ppermute | solution.py:570
  243.6 2.0 shard_map.290.refs_0_
  245.6 3.8 %collective-permute-start.42 = (bf16[176,768]{1,0:T(8,128)(2,1)}, bf16[176,768]{1,0:T(8,128)(2,1)S(1)}, u32[]{:S(2)}, u32[]{:S(2)}) collective-permute-start(bf16[176,768]{1,0:T(8,128)(2,1)} %shard_map.290.refs_0_), channel_id=1, source_target_pairs={{0,8},{4,12},{8,0},{12,4},{16,24},{20,28},{24,16},{28,20},{1,9},{5... | collective-permute-start | bytes 811016 | tf_op jit(solution)/shard_map/ppermute | solution.py:570
  249.5 3.0 %collective-permute-done.60.refs_3_ = bf16[224,640]{1,0:T(8,128)(2,1)S(1)} collective-permute-done((bf16[224,640]{1,0:T(8,128)(2,1)S(1)}, bf16[224,640]{1,0:T(8,128)(2,1)S(1)}, u32[]{:S(2)}, u32[]{:S(2)}) %collective-permute-start.60) | collective-permute-done | bytes 286752 | tf_op jit(solution)/shard_map/ppermute | solution.py:570
  252.5 1.7 collective-permute-start.61
  254.2 6.3 %collective-permute-done.42.refs_1_ = bf16[176,768]{1,0:T(8,128)(2,1)S(1)} collective-permute-done((bf16[176,768]{1,0:T(8,128)(2,1)}, bf16[176,768]{1,0:T(8,128)(2,1)S(1)}, u32[]{:S(2)}, u32[]{:S(2)}) %collective-permute-start.42) | collective-permute-done | bytes 270368 | tf_op jit(solution)/shard_map/ppermute | solution.py:570
  261.3 1.8 shard_map.291.refs_0_
  265.4 4.3 %collective-permute-done.61.refs_4_ = bf16[224,640]{1,0:T(8,128)(2,1)S(1)} collective-permute-done((bf16[224,640]{1,0:T(8,128)(2,1)S(1)}, bf16[224,640]{1,0:T(8,128)(2,1)S(1)}, u32[]{:S(2)}, u32[]{:S(2)}) %collective-permute-start.61) | collective-permute-done | bytes 286752 | tf_op jit(solution)/shard_map/ppermute | solution.py:570
  269.7 3.8 %collective-permute-done.43.refs_1_ = bf16[176,768]{1,0:T(8,128)(2,1)S(1)} collective-permute-done((bf16[176,768]{1,0:T(8,128)(2,1)}, bf16[176,768]{1,0:T(8,128)(2,1)S(1)}, u32[]{:S(2)}, u32[]{:S(2)}) %collective-permute-start.43) | collective-permute-done | bytes 270368 | tf_op jit(solution)/shard_map/ppermute | solution.py:570
  274.3 1.8 shard_map.292.refs_1_
  277.7 4.2 %shard_map.296 = (f32[640,512]{1,0:T(8,128)}, f32[640,512]{1,0:T(8,128)}, f32[512,640]{1,0:T(8,128)}, f32[256,640]{1,0:T(8,128)}) custom-call(s32[19]{0:T(128)} %pad_add_fusion.refs_0_, bf16[224,640]{1,0:T(8,128)(2,1)} %copy-done.2, bf16[224,640]{1,0:T(8,128)(2,1)} %copy-done.26, bf16[224,640]{1,0:T(8,128)(2,1)} %copy-done.25, bf16[224,640]{1,0:T(8,128)(2,1)} %copy-done.27, ...), custom_call_target="tpu_custom_call" | custom-call | tf_op jit(solution)/shard_map/pallas_call | solution.py:559
  282.7 2.1 shard_map.293
  (264 shorter events, 50.5 us)
Async XLA Ops:
  2.4 28.7 %collective-permute-start.5 = (bf16[160,768]{1,0:T(8,128)(2,1)}, bf16[160,768]{1,0:T(8,128)(2,1)S(1)}, u32[]{:S(2)}, u32[]{:S(2)}) collective-permute-start(bf16[160,768]{1,0:T(8,128)(2,1)} %shard_map.282), channel_id=1, source_target_pairs={{3,0},{0,1},{1,2},{2,3},{7,4},{4,5},{5,6},{6,7},{11,8},{8,9},{9,10... | collective-permute-start | bytes 737288 | tf_op jit(solution)/shard_map/ppermute | solution.py:567
  5.4 25.7 %collective-permute-start.4 = (bf16[160,768]{1,0:T(8,128)(2,1)}, bf16[160,768]{1,0:T(8,128)(2,1)S(1)}, u32[]{:S(2)}, u32[]{:S(2)}) collective-permute-start(bf16[160,768]{1,0:T(8,128)(2,1)} %shard_map.282), channel_id=1, source_target_pairs={{2,0},{3,1},{0,2},{1,3},{6,4},{7,5},{4,6},{5,7},{10,8},{11,9},{8,1... | collective-permute-start | bytes 737288 | tf_op jit(solution)/shard_map/ppermute | solution.py:567
  6.9 24.2 %collective-permute-start.3 = (bf16[160,768]{1,0:T(8,128)(2,1)}, bf16[160,768]{1,0:T(8,128)(2,1)S(1)}, u32[]{:S(2)}, u32[]{:S(2)}) collective-permute-start(bf16[160,768]{1,0:T(8,128)(2,1)} %shard_map.282), channel_id=1, source_target_pairs={{1,0},{2,1},{3,2},{0,3},{5,4},{6,5},{7,6},{4,7},{9,8},{10,9},{11,1... | collective-permute-start | bytes 737288 | tf_op jit(solution)/shard_map/ppermute | solution.py:567
  10.3 13.4 %collective-permute-start.1 = (f32[8,160]{1,0:T(8,128)}, f32[8,160]{1,0:T(8,128)S(1)}, u32[]{:S(2)}, u32[]{:S(2)}) collective-permute-start(f32[8,160]{1,0:T(8,128)} %shard_map.280), channel_id=1, source_target_pairs={{2,0},{3,1},{0,2},{1,3},{6,4},{7,5},{4,6},{5,7},{10,8},{11,9},{8,1... | collective-permute-start | bytes 15368 | tf_op jit(solution)/shard_map/ppermute | solution.py:567
  23.7 10.5 %collective-permute-start.18 = (bf16[128,640]{1,0:T(8,128)(2,1)}, bf16[128,640]{1,0:T(8,128)(2,1)S(1)}, u32[]{:S(2)}, u32[]{:S(2)}) collective-permute-start(bf16[128,640]{1,0:T(8,128)(2,1)} %get-tuple-element.97), channel_id=1, source_target_pairs={{3,0},{0,1},{1,2},{2,3},{7,4},{4,5},{5,6},{6,7},{11,8},{8,9},{9,10... | collective-permute-start | bytes 491528 | tf_op jit(solution)/shard_map/ppermute | solution.py:567
  31.1 21.5 %collective-permute-start.6 = (bf16[160,768]{1,0:T(8,128)(2,1)S(1)}, bf16[160,768]{1,0:T(8,128)(2,1)S(1)}, u32[]{:S(2)}, u32[]{:S(2)}) collective-permute-start(bf16[160,768]{1,0:T(8,128)(2,1)S(1)} %collective-permute-done.3.refs_9_), channel_id=1, source_target_pairs={{0,4},{4,0},{8,12},{12,8},{16,20},{20,16},{24,28},{28,24},{1,5},{5... | collective-permute-start | bytes 737288 | tf_op jit(solution)/shard_map/ppermute | solution.py:570
  31.2 31.1 %collective-permute-start.24 = (bf16[640,512]{1,0:T(8,128)(2,1)}, bf16[640,512]{1,0:T(8,128)(2,1)S(1)}, u32[]{:S(2)}, u32[]{:S(2)}) collective-permute-start(bf16[640,512]{1,0:T(8,128)(2,1)} %get-tuple-element.103), channel_id=1, source_target_pairs={{3,0},{0,1},{1,2},{2,3},{7,4},{4,5},{5,6},{6,7},{11,8},{8,9},{9,10... | collective-permute-start | bytes 1966088 | tf_op jit(solution)/shard_map/ppermute | solution.py:567
  32.6 19.2 %collective-permute-start.16 = (bf16[128,640]{1,0:T(8,128)(2,1)}, bf16[128,640]{1,0:T(8,128)(2,1)S(1)}, u32[]{:S(2)}, u32[]{:S(2)}) collective-permute-start(bf16[128,640]{1,0:T(8,128)(2,1)} %get-tuple-element.97), channel_id=1, source_target_pairs={{1,0},{2,1},{3,2},{0,3},{5,4},{6,5},{7,6},{4,7},{9,8},{10,9},{11,1... | collective-permute-start | bytes 491528 | tf_op jit(solution)/shard_map/ppermute | solution.py:567
  34.2 17.7 %collective-permute-start.21 = (bf16[128,640]{1,0:T(8,128)(2,1)S(1)}, bf16[128,640]{1,0:T(8,128)(2,1)S(1)}, u32[]{:S(2)}, u32[]{:S(2)}) collective-permute-start(bf16[128,640]{1,0:T(8,128)(2,1)S(1)} %collective-permute-done.18.refs_17_), channel_id=1, source_target_pairs={{0,4},{4,0},{8,12},{12,8},{16,20},{20,16},{24,28},{28,24},{1,5},{5... | collective-permute-start | bytes 491528 | tf_op jit(solution)/shard_map/ppermute | solution.py:570
  34.2 30.7 %collective-permute-start.23 = (bf16[640,512]{1,0:T(8,128)(2,1)}, bf16[640,512]{1,0:T(8,128)(2,1)S(1)}, u32[]{:S(2)}, u32[]{:S(2)}) collective-permute-start(bf16[640,512]{1,0:T(8,128)(2,1)} %get-tuple-element.103), channel_id=1, source_target_pairs={{2,0},{3,1},{0,2},{1,3},{6,4},{7,5},{4,6},{5,7},{10,8},{11,9},{8,1... | collective-permute-start | bytes 1966088 | tf_op jit(solution)/shard_map/ppermute | solution.py:567
  52.6 17.5 %collective-permute-start.22 = (bf16[640,512]{1,0:T(8,128)(2,1)}, bf16[640,512]{1,0:T(8,128)(2,1)S(1)}, u32[]{:S(2)}, u32[]{:S(2)}) collective-permute-start(bf16[640,512]{1,0:T(8,128)(2,1)} %get-tuple-element.103), channel_id=1, source_target_pairs={{1,0},{2,1},{3,2},{0,3},{5,4},{6,5},{7,6},{4,7},{9,8},{10,9},{11,1... | collective-permute-start | bytes 1966088 | tf_op jit(solution)/shard_map/ppermute | solution.py:567
  60.3 12.2 %collective-permute-start.12 = (bf16[256,512]{1,0:T(8,128)(2,1)}, bf16[256,512]{1,0:T(8,128)(2,1)S(1)}, u32[]{:S(2)}, u32[]{:S(2)}) collective-permute-start(bf16[256,512]{1,0:T(8,128)(2,1)} %get-tuple-element.93.refs_3_), channel_id=1, source_target_pairs={{0,4},{4,0},{8,12},{12,8},{16,20},{20,16},{24,28},{28,24},{1,5},{5... | collective-permute-start | bytes 786440 | tf_op jit(solution)/shard_map/ppermute | solution.py:570
  60.7 13.3 %collective-permute-start.11 = (bf16[256,512]{1,0:T(8,128)(2,1)}, bf16[256,512]{1,0:T(8,128)(2,1)S(1)}, u32[]{:S(2)}, u32[]{:S(2)}) collective-permute-start(bf16[256,512]{1,0:T(8,128)(2,1)} %get-tuple-element.93.refs_3_), channel_id=1, source_target_pairs={{24,0},{28,4},{0,8},{4,12},{8,16},{12,20},{16,24},{20,28},{25,1},{... | collective-permute-start | bytes 786440 | tf_op jit(solution)/shard_map/ppermute | solution.py:567
  62.2 20.2 %collective-permute-start.10 = (bf16[256,512]{1,0:T(8,128)(2,1)}, bf16[256,512]{1,0:T(8,128)(2,1)S(1)}, u32[]{:S(2)}, u32[]{:S(2)}) collective-permute-start(bf16[256,512]{1,0:T(8,128)(2,1)} %get-tuple-element.93.refs_3_), channel_id=1, source_target_pairs={{16,0},{20,4},{24,8},{28,12},{0,16},{4,20},{8,24},{12,28},{17,1},{... | collective-permute-start | bytes 786440 | tf_op jit(solution)/shard_map/ppermute | solution.py:567
  64.9 17.6 %collective-permute-start.9 = (bf16[256,512]{1,0:T(8,128)(2,1)}, bf16[256,512]{1,0:T(8,128)(2,1)S(1)}, u32[]{:S(2)}, u32[]{:S(2)}) collective-permute-start(bf16[256,512]{1,0:T(8,128)(2,1)} %get-tuple-element.93.refs_3_), channel_id=1, source_target_pairs={{8,0},{12,4},{16,8},{20,12},{24,16},{28,20},{0,24},{4,28},{9,1},{1... | collective-permute-start | bytes 786440 | tf_op jit(solution)/shard_map/ppermute | solution.py:567
  70.1 12.9 %collective-permute-start.30 = (bf16[256,640]{1,0:T(8,128)(2,1)S(1)}, bf16[256,640]{1,0:T(8,128)(2,1)S(1)}, u32[]{:S(2)}, u32[]{:S(2)}) collective-permute-start(bf16[256,640]{1,0:T(8,128)(2,1)S(1)} %copy-done.67), channel_id=1, source_target_pairs={{3,0},{0,1},{1,2},{2,3},{7,4},{4,5},{5,6},{6,7},{11,8},{8,9},{9,10... | collective-permute-start | bytes 983048 | tf_op jit(solution)/shard_map/ppermute | solution.py:567
  72.4 15.4 %collective-permute-start.29 = (bf16[256,640]{1,0:T(8,128)(2,1)S(1)}, bf16[256,640]{1,0:T(8,128)(2,1)S(1)}, u32[]{:S(2)}, u32[]{:S(2)}) collective-permute-start(bf16[256,640]{1,0:T(8,128)(2,1)S(1)} %copy-done.67), channel_id=1, source_target_pairs={{2,0},{3,1},{0,2},{1,3},{6,4},{7,5},{4,6},{5,7},{10,8},{11,9},{8,1... | collective-permute-start | bytes 983048 | tf_op jit(solution)/shard_map/ppermute | solution.py:567
  74.0 13.9 %collective-permute-start.28 = (bf16[256,640]{1,0:T(8,128)(2,1)S(1)}, bf16[256,640]{1,0:T(8,128)(2,1)S(1)}, u32[]{:S(2)}, u32[]{:S(2)}) collective-permute-start(bf16[256,640]{1,0:T(8,128)(2,1)S(1)} %copy-done.67), channel_id=1, source_target_pairs={{1,0},{2,1},{3,2},{0,3},{5,4},{6,5},{7,6},{4,7},{9,8},{10,9},{11,1... | collective-permute-start | bytes 983048 | tf_op jit(solution)/shard_map/ppermute | solution.py:567
  83.0 16.9 %collective-permute-start.25 = (bf16[640,512]{1,0:T(8,128)(2,1)S(1)}, bf16[640,512]{1,0:T(8,128)(2,1)S(1)}, u32[]{:S(2)}, u32[]{:S(2)}) collective-permute-start(bf16[640,512]{1,0:T(8,128)(2,1)S(1)} %collective-permute-done.22.refs_11_), channel_id=1, source_target_pairs={{0,4},{4,0},{8,12},{12,8},{16,20},{20,16},{24,28},{28,24},{1,5},{5... | collective-permute-start | bytes 1966088 | tf_op jit(solution)/shard_map/ppermute | solution.py:570
  87.9 12.0 %collective-permute-start.26 = (bf16[640,512]{1,0:T(8,128)(2,1)S(1)}, bf16[640,512]{1,0:T(8,128)(2,1)S(1)}, u32[]{:S(2)}, u32[]{:S(2)}) collective-permute-start(bf16[640,512]{1,0:T(8,128)(2,1)S(1)} %collective-permute-done.23.refs_12_), channel_id=1, source_target_pairs={{0,4},{4,0},{8,12},{12,8},{16,20},{20,16},{24,28},{28,24},{1,5},{5... | collective-permute-start | bytes 1966088 | tf_op jit(solution)/shard_map/ppermute | solution.py:570
  88.4 11.5 %collective-permute-start.27 = (bf16[640,512]{1,0:T(8,128)(2,1)S(1)}, bf16[640,512]{1,0:T(8,128)(2,1)S(1)}, u32[]{:S(2)}, u32[]{:S(2)}) collective-permute-start(bf16[640,512]{1,0:T(8,128)(2,1)S(1)} %collective-permute-done.24.refs_13_), channel_id=1, source_target_pairs={{0,4},{4,0},{8,12},{12,8},{16,20},{20,16},{24,28},{28,24},{1,5},{5... | collective-permute-start | bytes 1966088 | tf_op jit(solution)/shard_map/ppermute | solution.py:570
  124.2 44.0 %collective-permute-start.34 = (bf16[4,256,512]{2,1,0:T(8,128)(2,1)}, bf16[4,256,512]{2,1,0:T(8,128)(2,1)S(1)}, u32[]{:S(2)}, u32[]{:S(2)}) collective-permute-start(bf16[4,256,512]{2,1,0:T(8,128)(2,1)} %get-tuple-element.115), channel_id=1, source_target_pairs={{0,4},{4,0},{8,12},{12,8},{16,20},{20,16},{24,28},{28,24},{1,5},{5... | collective-permute-start | bytes 3145736 | tf_op jit(solution)/shard_map/ppermute | solution.py:570
  124.3 11.5 %collective-permute-start.47 = (bf16[256,640]{1,0:T(8,128)(2,1)S(1)}, bf16[256,640]{1,0:T(8,128)(2,1)S(1)}, u32[]{:S(2)}, u32[]{:S(2)}) collective-permute-start(bf16[256,640]{1,0:T(8,128)(2,1)S(1)} %copy-done.1), channel_id=1, source_target_pairs={{3,0},{0,1},{1,2},{2,3},{7,4},{4,5},{5,6},{6,7},{11,8},{8,9},{9,10... | collective-permute-start | bytes 983048 | tf_op jit(solution)/shard_map/ppermute | solution.py:567
  125.6 17.2 %collective-permute-start.46 = (bf16[256,640]{1,0:T(8,128)(2,1)S(1)}, bf16[256,640]{1,0:T(8,128)(2,1)S(1)}, u32[]{:S(2)}, u32[]{:S(2)}) collective-permute-start(bf16[256,640]{1,0:T(8,128)(2,1)S(1)} %copy-done.1), channel_id=1, source_target_pairs={{2,0},{3,1},{0,2},{1,3},{6,4},{7,5},{4,6},{5,7},{10,8},{11,9},{8,1... | collective-permute-start | bytes 983048 | tf_op jit(solution)/shard_map/ppermute | solution.py:567
  126.7 16.9 %collective-permute-start.45 = (bf16[256,640]{1,0:T(8,128)(2,1)S(1)}, bf16[256,640]{1,0:T(8,128)(2,1)S(1)}, u32[]{:S(2)}, u32[]{:S(2)}) collective-permute-start(bf16[256,640]{1,0:T(8,128)(2,1)S(1)} %copy-done.1), channel_id=1, source_target_pairs={{1,0},{2,1},{3,2},{0,3},{5,4},{6,5},{7,6},{4,7},{9,8},{10,9},{11,1... | collective-permute-start | bytes 983048 | tf_op jit(solution)/shard_map/ppermute | solution.py:567
  128.1 28.2 %collective-permute-start.51 = (bf16[512,640]{1,0:T(8,128)(2,1)S(1)}, bf16[512,640]{1,0:T(8,128)(2,1)S(1)}, u32[]{:S(2)}, u32[]{:S(2)}) collective-permute-start(bf16[512,640]{1,0:T(8,128)(2,1)S(1)} %copy-done.66), channel_id=1, source_target_pairs={{0,4},{4,0},{8,12},{12,8},{16,20},{20,16},{24,28},{28,24},{1,5},{5... | collective-permute-start | bytes 1966088 | tf_op jit(solution)/shard_map/ppermute | solution.py:570
  135.8 14.1 %collective-permute-start.50 = (bf16[256,640]{1,0:T(8,128)(2,1)S(1)}, bf16[256,640]{1,0:T(8,128)(2,1)S(1)}, u32[]{:S(2)}, u32[]{:S(2)}) collective-permute-start(bf16[256,640]{1,0:T(8,128)(2,1)S(1)} %copy-done.18), channel_id=1, source_target_pairs={{3,0},{0,1},{1,2},{2,3},{7,4},{4,5},{5,6},{6,7},{11,8},{8,9},{9,10... | collective-permute-start | bytes 983048 | tf_op jit(solution)/shard_map/ppermute | solution.py:567
  142.8 13.5 %collective-permute-start.49 = (bf16[256,640]{1,0:T(8,128)(2,1)S(1)}, bf16[256,640]{1,0:T(8,128)(2,1)S(1)}, u32[]{:S(2)}, u32[]{:S(2)}) collective-permute-start(bf16[256,640]{1,0:T(8,128)(2,1)S(1)} %copy-done.18), channel_id=1, source_target_pairs={{2,0},{3,1},{0,2},{1,3},{6,4},{7,5},{4,6},{5,7},{10,8},{11,9},{8,1... | collective-permute-start | bytes 983048 | tf_op jit(solution)/shard_map/ppermute | solution.py:567
  143.6 12.7 %collective-permute-start.48 = (bf16[256,640]{1,0:T(8,128)(2,1)S(1)}, bf16[256,640]{1,0:T(8,128)(2,1)S(1)}, u32[]{:S(2)}, u32[]{:S(2)}) collective-permute-start(bf16[256,640]{1,0:T(8,128)(2,1)S(1)} %copy-done.18), channel_id=1, source_target_pairs={{1,0},{2,1},{3,2},{0,3},{5,4},{6,5},{7,6},{4,7},{9,8},{10,9},{11,1... | collective-permute-start | bytes 983048 | tf_op jit(solution)/shard_map/ppermute | solution.py:567
  168.1 36.7 %collective-permute-start.52 = (bf16[768,640]{1,0:T(8,128)(2,1)}, bf16[768,640]{1,0:T(8,128)(2,1)S(1)}, u32[]{:S(2)}, u32[]{:S(2)}) collective-permute-start(bf16[768,640]{1,0:T(8,128)(2,1)} %get-tuple-element.140), channel_id=1, source_target_pairs={{0,4},{4,0},{8,12},{12,8},{16,20},{20,16},{24,28},{28,24},{1,5},{5... | collective-permute-start | bytes 2949128 | tf_op jit(solution)/shard_map/ppermute | solution.py:570
  168.7 11.2 %collective-permute-start.37 = (bf16[256,512]{1,0:T(8,128)(2,1)S(1)}, bf16[256,512]{1,0:T(8,128)(2,1)S(1)}, u32[]{:S(2)}, u32[]{:S(2)}) collective-permute-start(bf16[256,512]{1,0:T(8,128)(2,1)S(1)} %get-tuple-element.161), channel_id=1, source_target_pairs={{24,0},{28,4},{0,8},{4,12},{8,16},{12,20},{16,24},{20,28},{25,1},{... | collective-permute-start | bytes 786440 | tf_op jit(solution)/shard_map/ppermute | solution.py:567
  170.7 19.9 %collective-permute-start.36 = (bf16[256,512]{1,0:T(8,128)(2,1)S(1)}, bf16[256,512]{1,0:T(8,128)(2,1)S(1)}, u32[]{:S(2)}, u32[]{:S(2)}) collective-permute-start(bf16[256,512]{1,0:T(8,128)(2,1)S(1)} %get-tuple-element.162), channel_id=1, source_target_pairs={{16,0},{20,4},{24,8},{28,12},{0,16},{4,20},{8,24},{12,28},{17,1},{... | collective-permute-start | bytes 786440 | tf_op jit(solution)/shard_map/ppermute | solution.py:567
  172.9 17.7 %collective-permute-start.35 = (bf16[256,512]{1,0:T(8,128)(2,1)S(1)}, bf16[256,512]{1,0:T(8,128)(2,1)S(1)}, u32[]{:S(2)}, u32[]{:S(2)}) collective-permute-start(bf16[256,512]{1,0:T(8,128)(2,1)S(1)} %get-tuple-element.163), channel_id=1, source_target_pairs={{8,0},{12,4},{16,8},{20,12},{24,16},{28,20},{0,24},{4,28},{9,1},{1... | collective-permute-start | bytes 786440 | tf_op jit(solution)/shard_map/ppermute | solution.py:567
  174.3 24.2 %collective-permute-start.53 = (bf16[128,640]{1,0:T(8,128)(2,1)S(1)}, bf16[128,640]{1,0:T(8,128)(2,1)S(1)}, u32[]{:S(2)}, u32[]{:S(2)}) collective-permute-start(bf16[128,640]{1,0:T(8,128)(2,1)S(1)} %copy-done.70), channel_id=1, source_target_pairs={{1,0},{2,1},{3,2},{0,3},{5,4},{6,5},{7,6},{4,7},{9,8},{10,9},{11,1... | collective-permute-start | bytes 491528 | tf_op jit(solution)/shard_map/ppermute | solution.py:567
  179.9 18.7 %collective-permute-start.54 = (bf16[128,640]{1,0:T(8,128)(2,1)S(1)}, bf16[128,640]{1,0:T(8,128)(2,1)S(1)}, u32[]{:S(2)}, u32[]{:S(2)}) collective-permute-start(bf16[128,640]{1,0:T(8,128)(2,1)S(1)} %copy-done.69), channel_id=1, source_target_pairs={{2,0},{3,1},{0,2},{1,3},{6,4},{7,5},{4,6},{5,7},{10,8},{11,9},{8,1... | collective-permute-start | bytes 491528 | tf_op jit(solution)/shard_map/ppermute | solution.py:567
  197.3 28.7 %collective-permute-start.38 = (bf16[640,768]{1,0:T(8,128)(2,1)}, bf16[640,768]{1,0:T(8,128)(2,1)S(1)}, u32[]{:S(2)}, u32[]{:S(2)}) collective-permute-start(bf16[640,768]{1,0:T(8,128)(2,1)} %get-tuple-element.127), channel_id=1, source_target_pairs={{0,4},{4,0},{8,12},{12,8},{16,20},{20,16},{24,28},{28,24},{1,5},{5... | collective-permute-start | bytes 2949128 | tf_op jit(solution)/shard_map/ppermute | solution.py:570
  209.3 13.9 %collective-permute-start.57 = (bf16[224,640]{1,0:T(8,128)(2,1)}, bf16[224,640]{1,0:T(8,128)(2,1)S(1)}, u32[]{:S(2)}, u32[]{:S(2)}) collective-permute-start(bf16[224,640]{1,0:T(8,128)(2,1)} %get-tuple-element.148), channel_id=1, source_target_pairs={{0,8},{4,12},{8,0},{12,4},{16,24},{20,28},{24,16},{28,20},{1,9},{5... | collective-permute-start | bytes 860168 | tf_op jit(solution)/shard_map/ppermute | solution.py:570
  215.3 17.4 %collective-permute-start.56 = (bf16[224,640]{1,0:T(8,128)(2,1)}, bf16[224,640]{1,0:T(8,128)(2,1)S(1)}, u32[]{:S(2)}, u32[]{:S(2)}) collective-permute-start(bf16[224,640]{1,0:T(8,128)(2,1)} %get-tuple-element.146), channel_id=1, source_target_pairs={{0,8},{4,12},{8,0},{12,4},{16,24},{20,28},{24,16},{28,20},{1,9},{5... | collective-permute-start | bytes 860168 | tf_op jit(solution)/shard_map/ppermute | solution.py:570
  224.2 18.0 %collective-permute-start.58 = (bf16[224,640]{1,0:T(8,128)(2,1)S(1)}, bf16[224,640]{1,0:T(8,128)(2,1)S(1)}, u32[]{:S(2)}, u32[]{:S(2)}) collective-permute-start(bf16[224,640]{1,0:T(8,128)(2,1)S(1)} %add_convert_fusion.1), channel_id=1, source_target_pairs={{0,16},{4,20},{8,24},{12,28},{16,0},{20,4},{24,8},{28,12},{1,17},{... | collective-permute-start | bytes 860168 | tf_op jit(solution)/shard_map/ppermute | solution.py:570
  229.8 12.7 %collective-permute-start.39 = (bf16[176,768]{1,0:T(8,128)(2,1)}, bf16[176,768]{1,0:T(8,128)(2,1)S(1)}, u32[]{:S(2)}, u32[]{:S(2)}) collective-permute-start(bf16[176,768]{1,0:T(8,128)(2,1)} %get-tuple-element.130), channel_id=1, source_target_pairs={{1,0},{2,1},{3,2},{0,3},{5,4},{6,5},{7,6},{4,7},{9,8},{10,9},{11,1... | collective-permute-start | bytes 811016 | tf_op jit(solution)/shard_map/ppermute | solution.py:567
  231.1 11.7 %collective-permute-start.40 = (bf16[176,768]{1,0:T(8,128)(2,1)}, bf16[176,768]{1,0:T(8,128)(2,1)S(1)}, u32[]{:S(2)}, u32[]{:S(2)}) collective-permute-start(bf16[176,768]{1,0:T(8,128)(2,1)} %get-tuple-element.131), channel_id=1, source_target_pairs={{2,0},{3,1},{0,2},{1,3},{6,4},{7,5},{4,6},{5,7},{10,8},{11,9},{8,1... | collective-permute-start | bytes 811016 | tf_op jit(solution)/shard_map/ppermute | solution.py:567
  231.7 11.1 %collective-permute-start.41 = (bf16[176,768]{1,0:T(8,128)(2,1)}, bf16[176,768]{1,0:T(8,128)(2,1)S(1)}, u32[]{:S(2)}, u32[]{:S(2)}) collective-permute-start(bf16[176,768]{1,0:T(8,128)(2,1)} %get-tuple-element.132), channel_id=1, source_target_pairs={{3,0},{0,1},{1,2},{2,3},{7,4},{4,5},{5,6},{6,7},{11,8},{8,9},{9,10... | collective-permute-start | bytes 811016 | tf_op jit(solution)/shard_map/ppermute | solution.py:567
  245.6 14.9 %collective-permute-start.42 = (bf16[176,768]{1,0:T(8,128)(2,1)}, bf16[176,768]{1,0:T(8,128)(2,1)S(1)}, u32[]{:S(2)}, u32[]{:S(2)}) collective-permute-start(bf16[176,768]{1,0:T(8,128)(2,1)} %shard_map.290.refs_0_), channel_id=1, source_target_pairs={{0,8},{4,12},{8,0},{12,4},{16,24},{20,28},{24,16},{28,20},{1,9},{5... | collective-permute-start | bytes 811016 | tf_op jit(solution)/shard_map/ppermute | solution.py:570
  249.5 16.0 %collective-permute-start.59 = (bf16[224,640]{1,0:T(8,128)(2,1)S(1)}, bf16[224,640]{1,0:T(8,128)(2,1)S(1)}, u32[]{:S(2)}, u32[]{:S(2)}) collective-permute-start(bf16[224,640]{1,0:T(8,128)(2,1)S(1)} %add_convert_fusion.refs_1_), channel_id=1, source_target_pairs={{0,8},{4,12},{8,0},{12,4},{16,24},{20,28},{24,16},{28,20},{1,9},{5... | collective-permute-start | bytes 860168 | tf_op jit(solution)/shard_map/ppermute | solution.py:570
  252.5 17.2 %collective-permute-start.61 = (bf16[224,640]{1,0:T(8,128)(2,1)S(1)}, bf16[224,640]{1,0:T(8,128)(2,1)S(1)}, u32[]{:S(2)}, u32[]{:S(2)}) collective-permute-start(bf16[224,640]{1,0:T(8,128)(2,1)S(1)} %collective-permute-done.60.refs_3_), channel_id=1, source_target_pairs={{0,8},{4,12},{8,0},{12,4},{16,24},{20,28},{24,16},{28,20},{1,9},{5... | collective-permute-start | bytes 860168 | tf_op jit(solution)/shard_map/ppermute | solution.py:570
  264.0 12.1 %collective-permute-start.62 = (bf16[224,640]{1,0:T(8,128)(2,1)S(1)}, bf16[224,640]{1,0:T(8,128)(2,1)S(1)}, u32[]{:S(2)}, u32[]{:S(2)}) collective-permute-start(bf16[224,640]{1,0:T(8,128)(2,1)S(1)} %add_convert_fusion.refs_1_), channel_id=1, source_target_pairs={{0,4},{4,0},{8,12},{12,8},{16,20},{20,16},{24,28},{28,24},{1,5},{5... | collective-permute-start | bytes 860168 | tf_op jit(solution)/shard_map/ppermute | solution.py:570
  264.0 12.1 %collective-permute-start.64 = (bf16[224,640]{1,0:T(8,128)(2,1)S(1)}, bf16[224,640]{1,0:T(8,128)(2,1)S(1)}, u32[]{:S(2)}, u32[]{:S(2)}) collective-permute-start(bf16[224,640]{1,0:T(8,128)(2,1)S(1)} %collective-permute-done.60.refs_3_), channel_id=1, source_target_pairs={{0,4},{4,0},{8,12},{12,8},{16,20},{20,16},{24,28},{28,24},{1,5},{5... | collective-permute-start | bytes 860168 | tf_op jit(solution)/shard_map/ppermute | solution.py:570
  265.4 10.7 %collective-permute-start.63 = (bf16[224,640]{1,0:T(8,128)(2,1)S(1)}, bf16[224,640]{1,0:T(8,128)(2,1)S(1)}, u32[]{:S(2)}, u32[]{:S(2)}) collective-permute-start(bf16[224,640]{1,0:T(8,128)(2,1)S(1)} %collective-permute-done.59.refs_2_), channel_id=1, source_target_pairs={{0,4},{4,0},{8,12},{12,8},{16,20},{20,16},{24,28},{28,24},{1,5},{5... | collective-permute-start | bytes 860168 | tf_op jit(solution)/shard_map/ppermute | solution.py:570
  (89 other events, 943.5 us)
